TPU v7x, 32 devices: a whole 2x2x4 slice. The times are simulated.
32 devices in a mesh: wide: 16 (over z, y, core), narrow: 2 (over x).
Axes of the slice: x: 2, y: 2, z: 4, core: 2. Of those that a mesh axis runs over, the one named last changes fastest.
Arguments:
- amplitudes: bfloat16 [65536, 1024], P(('wide', 'narrow')), may hold values from -0.046875 to 0.046875
- integral_slab: bfloat16 [65536, 1024], P(('wide', 'narrow')), may hold values from -0.046875 to 0.046875
- coupling: float32 [32, 1024, 1024], P(('wide', 'narrow')), may hold values from -0.046875 to 0.046875
- pair_of_block: int32 [32], replicated, may hold values from 0 to 31, each once
- pair_shift: float32 [32], replicated, may hold values from -4 to 4
- virt_energy: float32 [1024], replicated, may hold values from 0 to 26
- core_energy: float32 [64], replicated, may hold values from -6 to -4
- core_index: int32 [2], replicated, may hold values from 0 to 63, as said below
- frequency: float32 [16], replicated, may hold values from 6 to 30
- dipole: float32 [64, 1024], P(None, 'narrow'), may hold values from -6 to 6
Outputs:
- response: float32 [2, 32, 1024], P(None, None, 'narrow')
- residual_rms: float32 [2, 32], replicated
Inputs may be any that keep to these rules, and one draw needn't show every extreme that they name: `core_index`: the 2 core orbitals are different occupied orbitals, and the last of them is orbital 64 - 1.
All inputs are finite; a program needn't handle non-finite values.
Results may differ from a plain program's by a relative error of at most 0.0003.
Values sent between devices are 32-bit elements; how exact they have to be, the bound alone decides.
No kernel may reach another device: no remote copies, remote signals or barrier semaphores. Data moves between devices by JAX's collectives and lax.ppermute only.
A program may use at most 64 MiB of HBM per device.

v0:
```python
from functools import partial

import jax
import jax.numpy as jnp
from jax import lax
from jax.sharding import PartitionSpec as P

ITERS = 2


damping = 0.5
highest = lax.Precision.HIGHEST
contract_rows = (((0,), (0,)), ((), ()))
contract_last = (((1,), (1,)), ((), ()))
contract_pairs = (((0, 2), (0, 1)), ((), ()))


def divide_precond(real_part, imag_part, level, level_mag):
    return (
        (real_part * level - imag_part * damping) / level_mag,
        (imag_part * level + real_part * damping) / level_mag,
    )


def divide_denom(real_part, imag_part, denom_real, denom_mag):
    return (
        (real_part * denom_real + imag_part * damping) / denom_mag,
        (imag_part * denom_real - real_part * damping) / denom_mag,
    )


def apply_precond(real_part, imag_part, level):
    return (level * real_part + damping * imag_part, level * imag_part - damping * real_part)


def side_slab(slab_wide, total, flattened, start):
    return lax.dot_general(
        slab_wide, flattened, contract_last, precision=highest, preferred_element_type=jnp.float32
    )


def absorb(coupling, side, carry, piece, start):
    doubles_in, side_total = carry
    width = piece.shape[2]
    flattened = piece.reshape(-1, width)
    columns = coupling[0]
    updates = [
        lax.dot_general(
            flattened, columns, contract_last, precision=highest, preferred_element_type=jnp.float32
        )
    ]
    doubles_in = jnp.stack(updates, 0)
    side_total = side(side_total, flattened, start)
    return (doubles_in, side_total)


def per_device(
    amplitudes,
    integral_slab,
    coupling,
    pair_of_block,
    pair_shift,
    virt_energy,
    core_energy,
    core_index,
    frequency,
    dipole,
):
    virt_total = virt_energy.shape[0]
    block_rows = dipole.shape[1]
    row_start = lax.axis_index("narrow") * block_rows
    freq_count = frequency.shape[0]
    mode_count = freq_count * core_index.shape[0]
    local_pairs = coupling.shape[0]
    pair_count = pair_of_block.shape[0]
    local_rows = amplitudes.shape[0]
    chooser = (
        core_index[:, None] == jnp.arange(core_energy.shape[0], dtype=jnp.int32)[None, :]
    ).astype(jnp.float32)
    picked_energy = jnp.sum(chooser * core_energy[None, :], axis=1)
    picked_dipole = jnp.dot(chooser, dipole, precision=highest)
    shift = (frequency[None, :] + picked_energy[:, None]).reshape(-1)
    level = lax.dynamic_slice_in_dim(virt_energy, row_start, block_rows)[None, :] - shift[:, None]
    level_mag = level * level + damping * damping
    rhs = jnp.repeat(picked_dipole, freq_count, axis=0)
    slot_ids = lax.axis_index(("wide", "narrow")) * local_pairs + jnp.arange(
        local_pairs, dtype=jnp.int32
    )
    slot_match = slot_ids[:, None] == jnp.arange(pair_count, dtype=jnp.int32)[None, :]
    pair_ids = jnp.sum(jnp.where(slot_match, pair_of_block[None, :], 0), axis=1)
    pair_match = pair_ids[:, None] == jnp.arange(pair_count, dtype=jnp.int32)[None, :]
    slot_shift = jnp.sum(jnp.where(pair_match, pair_shift[None, :], 0.0), axis=1)
    denom_real = shift[None, :, None] - slot_shift[:, None, None] - virt_energy[None, None, :]
    denom_mag = denom_real * denom_real + damping * damping
    side = partial(side_slab, integral_slab.astype(jnp.float32))
    side_empty = jnp.zeros((local_rows, 2 * mode_count), jnp.float32)
    amplitudes_wide = amplitudes.astype(jnp.float32)
    resp_re, resp_im = divide_precond(rhs, jnp.zeros_like(rhs), level, level_mag)
    empty_doubles = jnp.zeros((local_pairs, 2 * mode_count, virt_total), jnp.float32)
    fold_plain = partial(absorb, coupling, side)
    rms_rows = []
    for sweep in range(ITERS):
        response = jnp.stack([resp_re, resp_im], 0)
        if sweep == 0:
            doubles_in, singles_term = fold_plain(
                (empty_doubles, side_empty),
                lax.all_gather(response, "narrow", axis=2, tiled=True),
                jnp.int32(0),
            )
        else:
            doubles_in, singles_term = fold_plain(
                (empty_doubles, side_empty),
                lax.all_gather(response, "narrow", axis=2, tiled=True),
                jnp.int32(0),
            )
        out_re, out_im = divide_denom(
            doubles_in[:, :mode_count], doubles_in[:, mode_count:], denom_real, denom_mag
        )
        outgoing = jnp.concatenate([out_re, out_im], 1)
        folded = lax.dot_general(
            outgoing,
            coupling,
            contract_pairs,
            precision=highest,
            preferred_element_type=jnp.float32,
        )
        folded = folded + lax.dot_general(
            singles_term,
            amplitudes_wide,
            contract_rows,
            precision=highest,
            preferred_element_type=jnp.float32,
        )
        summed = lax.psum(folded, ("wide", "narrow"))
        summed = lax.dynamic_slice_in_dim(summed, row_start, block_rows, 1)
        app_re, app_im = apply_precond(resp_re, resp_im, level)
        res_re = rhs - (app_re + summed[:mode_count])
        res_im = -(app_im + summed[mode_count:])
        partial_squares = jnp.sum(res_re * res_re + res_im * res_im, axis=1)
        total_squares = lax.psum(partial_squares, "narrow")
        rms_rows.append(jnp.sqrt(total_squares / (2 * virt_total) + 1e-06))
        step_re, step_im = divide_precond(res_re, res_im, level, level_mag)
        resp_re = resp_re + step_re
        resp_im = resp_im + step_im
    return (jnp.stack([resp_re, resp_im], 0), jnp.stack(rms_rows, 0))


def solution(mesh):
    placed = (
        P(("wide", "narrow"), None),
        P(("wide", "narrow"), None),
        P(("wide", "narrow"), None, None),
        P(),
        P(),
        P(),
        P(),
        P(),
        P(),
        P(None, "narrow"),
    )
    return jax.shard_map(
        per_device,
        mesh=mesh,
        in_specs=placed,
        out_specs=(P(None, None, "narrow"), P()),
        check_vma=False,
    )
```

profile of v0, /device:TPU:0, one launch (start us, length us, event | category | flops | bytes accessed | tf_op | source)
XLA Modules:
  0.0 329.7 jit_solution(13404999844428857127)
XLA Ops:
  7.2 0.0 all-reduce.4.cloned.1.call-start
  7.2 0.9 select_reduce_fusion
  8.1 0.7 broadcast_add_fusion
  8.8 0.1 add.152
  8.9 0.9 fusion.63
  9.8 1.4 fusion.64
  11.2 1.9 fusion.65
  13.1 0.6 broadcast_subtract_fusion
  13.8 0.8 dynamic_slice.9
  14.5 0.1 fusion.35
  14.7 7.1 %all_gather.6 = f32[2,32,1024]{2,1,0:T(8,128)S(1)} all-gather(f32[2,32,512]{2,1,0:T(8,128)S(1)} %pad_maximum_fusion), channel_id=1, replica_groups=mesh['wide'=16,'narrow'=2] {'narrow'}, dimensions={2}, use_global_device_ids=true | all-gather | bytes 393216 | tf_op jit(solution)/shard_map/all_gather | solution.py:107
  21.8 6.4 %fusion.8 = f32[1,64,1024]{2,1,0:T(8,128)S(1)} fusion(f32[64,1024]{1,0:T(8,128)S(1)} %bitcast.86, f32[1,1024,1024]{2,1,0:T(8,128)} %param.12), kind=kOutput, calls=%fused_computation.8 | convolution fusion | flops 805306368 | bytes 4718592 | tf_op jit(solution)/shard_map/dot_general | solution.py:48
  28.2 3.9 %fusion.71 = f32[64,2048]{1,0:T(8,128)S(1)} fusion(f32[64,1024]{1,0:T(8,128)S(1)} %bitcast.87, bf16[2048,1024]{1,0:T(8,128)(2,1)S(1)} %copy-done.3), kind=kOutput, calls=%fused_computation.100 | convolution fusion | flops 1610612736 | bytes 4980736 | tf_op jit(solution)/shard_map/dot_general | solution.py:37
  32.1 0.1 fusion.25
  32.3 2.3 fusion.72
  34.6 3.4 %fusion.11 = f32[64,1024]{1,0:T(8,128)} fusion(f32[64,1024]{1,0:T(8,128)S(1)} %fusion.72, f32[1,1024,1024]{2,1,0:T(8,128)S(1)} %copy-done.1, f32[1,32,1024]{2,1,0:T(8,128)S(1)} %get-tuple-element.13, f32[1,32,1024]{2,1,0:T(8,128)S(1)} %get-tuple-element.12), kind=kOutput, calls=%fused_computation.9 | convolution fusion | flops 805437440 | bytes 4980736 | tf_op jit(solution)/shard_map/dot_general | solution.py:120
  38.0 0.0 all-reduce.6.cloned.1.call-start
  38.0 128.3 %all-reduce.4.cloned.1.call-done = f32[64,1024]{1,0:T(8,128)} async-done(((f32[64,1024]{1,0:T(8,128)}), f32[64,1024]{1,0:T(8,128)}) %all-reduce.4.cloned.1.call-update) | async-done | bytes 262160 | tf_op jit(solution)/shard_map/psum | solution.py:134
  166.3 1.2 add_reduce_fusion.1
  167.5 0.1 fusion.45
  167.7 5.8 %all_gather.7 = f32[2,32,1024]{2,1,0:T(8,128)S(1)} all-gather(f32[2,32,512]{2,1,0:T(8,128)S(1)} %pad_maximum_fusion.1), channel_id=1, replica_groups=mesh['wide'=16,'narrow'=2] {'narrow'}, dimensions={2}, use_global_device_ids=true | all-gather | bytes 393216 | tf_op jit(solution)/shard_map/all_gather | solution.py:113
  173.5 6.4 %fusion.14 = f32[1,64,1024]{2,1,0:T(8,128)S(1)} fusion(f32[64,1024]{1,0:T(8,128)S(1)} %bitcast.88, f32[1,1024,1024]{2,1,0:T(8,128)} %param.12), kind=kOutput, calls=%fused_computation.10 | convolution fusion | flops 805306368 | bytes 4718592 | tf_op jit(solution)/shard_map/dot_general | solution.py:48
  179.9 3.9 %fusion.73 = f32[64,2048]{1,0:T(8,128)S(1)} fusion(f32[64,1024]{1,0:T(8,128)S(1)} %bitcast.89, bf16[2048,1024]{1,0:T(8,128)(2,1)S(1)} %copy-done.4), kind=kOutput, calls=%fused_computation.102 | convolution fusion | flops 1610612736 | bytes 4980736 | tf_op jit(solution)/shard_map/dot_general | solution.py:37
  183.8 0.1 fusion.28
  183.9 2.3 fusion.74
  186.3 3.4 %fusion.17 = f32[64,1024]{1,0:T(8,128)} fusion(f32[64,1024]{1,0:T(8,128)S(1)} %fusion.74, f32[1,1024,1024]{2,1,0:T(8,128)S(1)} %copy-done.2, f32[1,32,1024]{2,1,0:T(8,128)S(1)} %get-tuple-element.11, f32[1,32,1024]{2,1,0:T(8,128)S(1)} %get-tuple-element.10), kind=kOutput, calls=%fused_computation.11 | convolution fusion | flops 805437440 | bytes 4980736 | tf_op jit(solution)/shard_map/dot_general | solution.py:120
  189.6 125.8 %all-reduce.6.cloned.1.call-done = f32[64,1024]{1,0:T(8,128)} async-done(((f32[64,1024]{1,0:T(8,128)}), f32[64,1024]{1,0:T(8,128)}) %all-reduce.6.cloned.1.call-update) | async-done | bytes 262160 | tf_op jit(solution)/shard_map/psum | solution.py:134
  315.5 1.1 add_reduce_fusion
  316.5 0.1 fusion.48
  316.7 0.7 pad_maximum_fusion.2
  317.3 4.9 %all-reduce = (f32[32]{0:T(128)S(1)}, f32[32]{0:T(128)S(1)}) all-reduce(f32[32]{0:T(128)S(1)} %get-tuple-element.7, f32[32]{0:T(128)S(1)} %get-tuple-element.4), channel_id=1, replica_groups=mesh['wide'=16,'narrow'=2] {'narrow'}, use_global_device_ids=true, to_apply=%region_8.9 | all-reduce | flops 64 | bytes 512 | tf_op jit(solution)/shard_map/psum | solution.py:140
  322.2 0.6 pad_maximum_fusion.3
  (22 shorter events, 0.1 us)
Async XLA Ops:
  7.2 1.7 copy-start
  7.2 159.1 %all-reduce.4.cloned.1.call-start = ((), (), s32[]{:S(2)}) async-start(), calls=%async_computation | async-start | bytes 524288 | tf_op jit(solution)/shard_map/psum | solution.py:134
  9.8 18.4 %copy-start.3 = (bf16[2048,1024]{1,0:T(8,128)(2,1)S(1)}, bf16[2048,1024]{1,0:T(8,128)(2,1)}, u32[]{:S(2)}) copy-start(bf16[2048,1024]{1,0:T(8,128)(2,1)} %param.11) | copy-start | bytes 12582916
  21.8 10.3 %copy-start.7 = (f32[1024]{0:T(1024)S(1)}, f32[1024]{0:T(1024)}, u32[]{:S(2)}) copy-start(f32[1024]{0:T(1024)} %param.15) | copy-start | bytes 12292
  21.8 10.5 %copy-start.5 = (bf16[2048,1024]{1,0:T(8,128)(2,1)S(1)}, bf16[2048,1024]{1,0:T(8,128)(2,1)}, u32[]{:S(2)}) copy-start(bf16[2048,1024]{1,0:T(8,128)(2,1)} %param.10) | copy-start | bytes 12582916
  28.2 6.4 %copy-start.1 = (f32[1,1024,1024]{2,1,0:T(8,128)S(1)}, f32[1,1024,1024]{2,1,0:T(8,128)}, u32[]{:S(2)}) copy-start(f32[1,1024,1024]{2,1,0:T(8,128)} %param.12) | copy-start | bytes 12582916
  38.0 277.5 %all-reduce.6.cloned.1.call-start = ((), (), s32[]{:S(2)}) async-start(), calls=%async_computation.1 | async-start | bytes 524288 | tf_op jit(solution)/shard_map/psum | solution.py:134
  166.3 13.6 %copy-start.4 = (bf16[2048,1024]{1,0:T(8,128)(2,1)S(1)}, bf16[2048,1024]{1,0:T(8,128)(2,1)}, u32[]{:S(2)}) copy-start(bf16[2048,1024]{1,0:T(8,128)(2,1)} %param.11) | copy-start | bytes 12582916
  173.5 10.5 %copy-start.6 = (bf16[2048,1024]{1,0:T(8,128)(2,1)S(1)}, bf16[2048,1024]{1,0:T(8,128)(2,1)}, u32[]{:S(2)}) copy-start(bf16[2048,1024]{1,0:T(8,128)(2,1)} %param.10) | copy-start | bytes 12582916
  179.9 6.4 %copy-start.2 = (f32[1,1024,1024]{2,1,0:T(8,128)S(1)}, f32[1,1024,1024]{2,1,0:T(8,128)}, u32[]{:S(2)}) copy-start(f32[1,1024,1024]{2,1,0:T(8,128)} %param.12) | copy-start | bytes 12582916
Sparse Core Ops, SparseCore 0:
  38.1 128.1 all-reduce.3
  189.8 125.6 all-reduce.5
where the time goes:
time: 330 us
  waiting for transfers between devices  254 us (77%)
  matrix products  32.8 us (10%)
  blocking collectives  17.8 us (5%)
  between operations  14.2 us (4%)
  other arithmetic  9.76 us (3%)
    psum x2, waiting for transfers between devices, per_device(): summed = lax.psum(folded, ('wide', 'narrow'))  254 us
    all_gather x2, blocking collectives, per_device(): lax.all_gather(response, 'narrow', axis=2, tiled=True)  12.9 us
    dot_general x2, matrix products, absorb(): lax.dot_general(flattened, columns, contract_last, precision=highest, pre...  12.8 us
    dot_general x2, matrix products, side_slab(): lax.dot_general(slab_wide, flattened, contract_last, precision=highest, p...  7.81 us
    dot_general x2, matrix products, per_device(): lax.dot_general(outgoing, coupling, contract_pairs, precision=highest, pr...  6.71 us
  transfers between devices with their start and end apart: 2, of which 2 were waited for; matrix products, arithmetic and copies ran while one was open for 0% of the time, Pallas kernels for 0%

commit v1 on v0

v1 whole, which is shorter than its diff:
```python
import jax
import jax.numpy as jnp
from jax import lax
from jax.sharding import PartitionSpec as P

ITERS = 2
DAMP = 0.5
HIGHEST = lax.Precision.HIGHEST
ROWS = (((0,), (0,)), ((), ()))
LAST = (((1,), (1,)), ((), ()))


def per_device(
    wide,
    narrow,
    amplitudes,
    integral_slab,
    coupling,
    pair_of_block,
    pair_shift,
    virt_energy,
    core_energy,
    core_index,
    frequency,
    dipole,
):
    virt = virt_energy.shape[0]
    freqs = frequency.shape[0]
    modes = freqs * core_index.shape[0]
    slots = coupling.shape[0]
    block = dipole.shape[1]
    everyone = modes % (wide * narrow) == 0
    group = ("wide", "narrow") if everyone else "wide"
    members = wide * narrow if everyone else wide
    owned = modes // members

    here = lax.axis_index(("wide", "narrow"))
    mine = lax.axis_index(group)
    picked = jnp.take(dipole, core_index, axis=0)
    picked = lax.all_gather(picked, "narrow", axis=1, tiled=True)
    shift = (frequency[None, :] + jnp.take(core_energy, core_index)[:, None]).reshape(-1)
    offset = jnp.take(pair_shift, lax.dynamic_slice_in_dim(pair_of_block, here * slots, slots))
    rhs = jnp.repeat(picked, freqs, axis=0)
    level = virt_energy[None, :] - shift[:, None]
    mag = level * level + DAMP * DAMP
    response = jnp.concatenate([rhs * level / mag, rhs * DAMP / mag], 0)
    den = shift[None, :, None] - offset[:, None, None] - virt_energy[None, None, :]
    den_mag = den * den + DAMP * DAMP
    own_rhs = lax.dynamic_slice_in_dim(rhs, mine * owned, owned)
    own_level = lax.dynamic_slice_in_dim(level, mine * owned, owned)
    own_mag = own_level * own_level + DAMP * DAMP
    own_re, own_im = own_rhs * own_level / own_mag, own_rhs * DAMP / own_mag
    slab = integral_slab.astype(jnp.float32)
    ampl = amplitudes.astype(jnp.float32)

    def dot(left, right, dims):
        return lax.dot_general(left, right, dims, precision=HIGHEST, preferred_element_type=jnp.float32)

    rms = []
    for sweep in range(ITERS):
        folded = dot(dot(response, slab, LAST), ampl, (((1,), (0,)), ((), ())))
        for slot in range(slots):
            inner = dot(response, coupling[slot], LAST)
            re, im = inner[:modes], inner[modes:]
            quot = jnp.concatenate(
                [
                    (re * den[slot] + im * DAMP) / den_mag[slot],
                    (im * den[slot] - re * DAMP) / den_mag[slot],
                ],
                0,
            )
            folded = folded + dot(quot, coupling[slot], (((1,), (0,)), ((), ())))
        pieces = folded.reshape(2, members, owned, virt).transpose(1, 0, 2, 3)
        total = jnp.sum(lax.all_to_all(pieces, group, 0, 0, tiled=True), 0)
        if not everyone:
            total = lax.psum(total, "narrow")
        res_re = own_rhs - (own_level * own_re + DAMP * own_im + total[0])
        res_im = -(own_level * own_im - DAMP * own_re + total[1])
        squares = jnp.sum(res_re * res_re + res_im * res_im, axis=1)
        rms.append(jnp.sqrt(squares / (2 * virt) + 1e-6))
        own_re = own_re + (res_re * own_level - res_im * DAMP) / own_mag
        own_im = own_im + (res_im * own_level + res_re * DAMP) / own_mag
        own = jnp.stack([own_re, own_im], 0)
        if sweep + 1 < ITERS:
            sent = jnp.broadcast_to(own[None], (members,) + own.shape)
            got = lax.all_to_all(sent, group, 0, 0, tiled=True)
            response = got.transpose(1, 0, 2, 3).reshape(2 * modes, virt)
    if everyone:
        sent = own.reshape(2, owned, narrow, block).transpose(2, 0, 1, 3)
        sent = jnp.broadcast_to(sent[None], (wide,) + sent.shape).reshape(members, 2, owned, block)
    else:
        sent = lax.dynamic_slice_in_dim(own, lax.axis_index("narrow") * block, block, 2)
        sent = jnp.broadcast_to(sent[None], (members,) + sent.shape)
    extra = jnp.broadcast_to(jnp.stack(rms, 0)[None, :, :, None], (members, 2, owned, 128))
    got = lax.all_to_all(jnp.concatenate([sent, extra], 3), group, 0, 0, tiled=True)
    got = got.transpose(1, 0, 2, 3).reshape(2, modes, block + 128)
    return got[:, :, :block], got[:, :, block]


def solution(mesh):
    wide, narrow = mesh.shape["wide"], mesh.shape["narrow"]
    split = ("wide", "narrow")

    def body(*args):
        return per_device(wide, narrow, *args)

    return jax.shard_map(
        body,
        mesh=mesh,
        in_specs=(
            P(split, None),
            P(split, None),
            P(split, None, None),
            P(),
            P(),
            P(),
            P(),
            P(),
            P(),
            P(None, "narrow"),
        ),
        out_specs=(P(None, None, "narrow"), P()),
        check_vma=False,
    )
```

time: 330 us -> 107 us (0.32)
  waiting for transfers between devices: 254 us -> 9.98 us
  blocking collectives: 17.8 us -> 46.2 us
  between operations: 14.2 us -> 4.87 us
  local copies, waits for them, and re-layouts: 0.9 us -> 7.25 us
  other arithmetic: 9.76 us -> 4.88 us
    psum x2 -> x0, waiting for transfers between devices: 254 us -> none  [per_device(): summed = lax.psum(folded, ('wide', 'narrow'))]
    all_to_all x0 -> x3, blocking collectives: none -> 40.8 us  [the longest x1 16.9 us: per_device(): total = jnp.sum(lax.all_to_all(pieces, group, 0, 0, tiled=True), 0)]
    all_to_all x0 -> x1, waiting for transfers between devices: none -> 9.98 us  [per_device(): total = jnp.sum(lax.all_to_all(pieces, group, 0, 0, tiled=True), 0)]
    all_gather x2 -> x1, blocking collectives: 12.9 us -> 5.4 us  [per_device(): picked = lax.all_gather(picked, 'narrow', axis=1, tiled=True)]
    reduce_sum x5 -> x3, other arithmetic: 6.54 us -> 0.84 us  [the longest x1 0.64 us: per_device(): squares = jnp.sum(res_re * res_re + res_im * res_im, axis=1)]
    psum x1 -> x0, blocking collectives: 4.91 us -> none  [per_device(): total_squares = lax.psum(partial_squares, 'narrow')]
    dot_general x9 -> x8, matrix products: 32.8 us -> 30.5 us  [dot(): lax.dot_general(left, right, dims, precision=HIGHEST, preferred_element_t...]
  transfers between devices with their start and end apart: 2 -> 1, of which waited for: 2 -> 1; matrix products, arithmetic and copies ran while one was open for 0% -> 0% of each run, Pallas kernels for 0% -> 0%
where the time goes in v1:
time: 107 us; the launch traced here: 106 us
  blocking collectives  46.2 us (43%)
  matrix products  30.5 us (29%)
  waiting for transfers between devices  9.98 us (9%)
  local copies, waits for them, and re-layouts  7.25 us (7%)
  other arithmetic  4.88 us (5%)
  between operations  4.87 us (5%)
  starting transfers between devices  2.58 us (2%)
    dot_general x8, matrix products, dot(): lax.dot_general(left, right, dims, precision=HIGHEST, preferred_element_t...  30.5 us
    all_to_all x1, blocking collectives, per_device(): total = jnp.sum(lax.all_to_all(pieces, group, 0, 0, tiled=True), 0)  16.9 us
    all_to_all x1, blocking collectives, per_device(): got = lax.all_to_all(sent, group, 0, 0, tiled=True)  12.8 us
    all_to_all x1, blocking collectives, per_device(): lax.all_to_all(jnp.concatenate([sent, extra], 3), group, 0, 0, tiled=True)  11.1 us
    all_to_all x1, waiting for transfers between devices, per_device(): total = jnp.sum(lax.all_to_all(pieces, group, 0, 0, tiled=True), 0)  9.98 us
    all_gather x1, blocking collectives, per_device(): picked = lax.all_gather(picked, 'narrow', axis=1, tiled=True)  5.4 us
    all_to_all x1, starting transfers between devices, per_device(): total = jnp.sum(lax.all_to_all(pieces, group, 0, 0, tiled=True), 0)  2.58 us
  transfers between devices with their start and end apart: 1, of which 1 were waited for; matrix products, arithmetic and copies ran while one was open for 0% of the time, Pallas kernels for 0%

profile of v1, /device:TPU:0, one launch (start us, length us, event | category | flops | bytes accessed | tf_op | source)
XLA Modules:
  0.0 106.3 jit_solution(7400897052668210896)
XLA Ops:
  0.7 1.3 %dynamic_slice.11 = s32[1]{0:T(128)} dynamic-slice(s32[32]{0:T(128)} %param.13, s32[]{:T(128)S(6)} %select_n.33), dynamic_slice_sizes={1} | dynamic-slice | bytes 12 | tf_op jit(solution)/shard_map/dynamic_slice | solution.py:42
  3.9 0.7 compare_select_fusion
  4.5 1.3 %gather_fusion.1 = f32[2]{0:T(128)S(1)} fusion(f32[64]{0:T(128)} %param.16, s32[1024]{0:T(1024)S(1)} %pad_clamp_fusion), kind=kCustom, calls=%fused_computation.1 | custom fusion | bytes 24 | tf_op jit(solution)/shard_map/jit(_take)/gather | solution.py:41
  5.8 0.6 gather_fusion
  6.4 0.7 broadcast_select_fusion.1
  7.1 0.7 broadcast_add_fusion
  7.9 5.4 %all_gather.3 = f32[2,1024]{1,0:T(2,128)S(1)} all-gather(f32[2,512]{1,0:T(2,128)S(1)} %broadcast_select_fusion), channel_id=1, replica_groups=mesh['wide'=16,'narrow'=2] {'narrow'}, dimensions={1}, use_global_device_ids=true | all-gather | bytes 12288 | tf_op jit(solution)/shard_map/all_gather | solution.py:40
  13.4 1.2 %dynamic-slice.2 = f32[1]{0:T(128)} dynamic-slice(f32[32]{0:T(128)} %param.14, s32[]{:T(128)} %bitcast.2), dynamic_slice_sizes={1} | dynamic-slice | bytes 12 | tf_op jit(solution)/shard_map/jit(_take)/gather | solution.py:42
  15.3 0.8 fusion.30
  16.1 6.4 %fusion.6 = f32[64,1024]{1,0:T(8,128)S(1)} fusion(f32[1,1024,1024]{2,1,0:T(8,128)} %param.12, f32[32,1024]{1,0:T(8,128)S(1)} %get-tuple-element.34, f32[32,1024]{1,0:T(8,128)S(1)} %get-tuple-element.33), kind=kOutput, calls=%fused_computation.8 | convolution fusion | flops 805371904 | bytes 4718592 | tf_op jit(solution)/shard_map/dot_general | solution.py:57
  22.5 3.9 %fusion.20 = f32[64,2048]{1,0:T(8,128)S(1)} fusion(bf16[2048,1024]{1,0:T(8,128)(2,1)S(1)} %copy-done.3, f32[32,1024]{1,0:T(8,128)S(1)} %get-tuple-element.34, f32[32,1024]{1,0:T(8,128)S(1)} %get-tuple-element.33), kind=kOutput, calls=%fused_computation.26 | convolution fusion | flops 1610678272 | bytes 4980736 | tf_op jit(solution)/shard_map/dot_general | solution.py:57
  26.4 0.1 fusion.22
  26.5 2.3 %fusion.39 = f32[64,1024]{1,0:T(8,128)S(1)} fusion(f32[64,2048]{1,0:T(8,128)S(1)} %fusion.20, bf16[2048,1024]{1,0:T(8,128)(2,1)S(1)} %copy-done.5), kind=kOutput, calls=%fused_computation.74 | convolution fusion | flops 1610612736 | bytes 4980736 | tf_op jit(solution)/shard_map/dot_general | solution.py:57
  28.9 2.7 %fusion.8 = f32[64,1024]{1,0:T(8,128)S(1)} fusion(f32[64,1024]{1,0:T(8,128)S(1)} %fusion.39, f32[1,1024,1024]{2,1,0:T(8,128)S(1)} %copy-done.1, f32[32,1024]{1,0:T(8,128)S(1)} %get-tuple-element.28, f32[32,1024]{1,0:T(8,128)S(1)} %get-tuple-element.27), kind=kOutput, calls=%fused_computation.10 | convolution fusion | flops 805437440 | bytes 4980736 | tf_op jit(solution)/shard_map/dot_general | solution.py:57
  31.5 0.2 copy.21
  31.7 16.9 %all_to_all.20 = f32[32,2,1,1024]{3,1,2,0:T(2,128)S(1)} all-to-all(f32[32,2,1,1024]{3,1,2,0:T(2,128)S(1)} %bitcast.62), channel_id=1, replica_groups=mesh['wide'=16,'narrow'=2] {'wide','narrow'}, dimensions={0} | all-to-all | bytes 524288 | tf_op jit(solution)/shard_map/all_to_all | solution.py:74
  48.6 0.1 reduce_sum.36
  48.7 0.6 add_reduce_fusion.1
  49.5 12.8 %all_to_all.21 = f32[32,2,1,1024]{3,1,2,0:T(2,128)S(1)} all-to-all(f32[32,2,1,1024]{3,1,2,0:T(2,128)S(1)} %broadcast_in_dim.58), channel_id=1, replica_groups=mesh['wide'=16,'narrow'=2] {'wide','narrow'}, dimensions={0} | all-to-all | bytes 524288 | tf_op jit(solution)/shard_map/all_to_all | solution.py:86
  62.4 6.4 %fusion.2 = f32[64,1024]{1,0:T(8,128)S(1)} fusion(f32[64,1024]{1,0:T(8,128)S(1)} %bitcast.58, f32[1,1024,1024]{2,1,0:T(8,128)} %param.12), kind=kOutput, calls=%fused_computation.4 | convolution fusion | flops 805306368 | bytes 4718592 | tf_op jit(solution)/shard_map/dot_general | solution.py:57
  68.8 3.9 %fusion.40 = f32[64,2048]{1,0:T(8,128)S(1)} fusion(f32[64,1024]{1,0:T(8,128)S(1)} %bitcast.59, bf16[2048,1024]{1,0:T(8,128)(2,1)S(1)} %copy-done.4), kind=kOutput, calls=%fused_computation.75 | convolution fusion | flops 1610612736 | bytes 4980736 | tf_op jit(solution)/shard_map/dot_general | solution.py:57
  72.7 0.1 fusion.25
  72.8 2.3 %fusion.41 = f32[64,1024]{1,0:T(8,128)S(1)} fusion(f32[64,2048]{1,0:T(8,128)S(1)} %fusion.40, bf16[2048,1024]{1,0:T(8,128)(2,1)S(1)} %copy-done.6), kind=kOutput, calls=%fused_computation.76 | convolution fusion | flops 1610612736 | bytes 4980736 | tf_op jit(solution)/shard_map/dot_general | solution.py:57
  75.2 2.7 %fusion.11 = f32[64,1024]{1,0:T(8,128)S(1)} fusion(f32[64,1024]{1,0:T(8,128)S(1)} %fusion.41, f32[1,1024,1024]{2,1,0:T(8,128)S(1)} %copy-done.2, f32[32,1024]{1,0:T(8,128)S(1)} %get-tuple-element.26, f32[32,1024]{1,0:T(8,128)S(1)} %get-tuple-element.25), kind=kOutput, calls=%fused_computation.11 | convolution fusion | flops 805437440 | bytes 4980736 | tf_op jit(solution)/shard_map/dot_general | solution.py:57
  77.8 0.9 copy.20
  78.7 2.6 %all-to-all-start.2 = ((f32[32,2,1,1024]{3,1,2,0:T(2,128)}), f32[32,2,1,1024]{3,1,2,0:T(2,128)S(1)}, u32[]{:S(2)}, u32[]{:S(2)}) async-start(f32[32,2,1,1024]{3,1,2,0:T(2,128)} %bitcast.56), calls=%async_computation.2 | async-start | bytes 524288 | tf_op jit(solution)/shard_map/all_to_all | solution.py:74
  82.0 10.0 %all-to-all-done.2 = f32[32,2,1,1024]{3,1,2,0:T(2,128)S(1)} async-done(((f32[32,2,1,1024]{3,1,2,0:T(2,128)}), f32[32,2,1,1024]{3,1,2,0:T(2,128)S(1)}, u32[]{:S(2)}, u32[]{:S(2)}) %all-to-all-start.2) | async-done | bytes 262176 | tf_op jit(solution)/shard_map/all_to_all | solution.py:74
  92.0 0.1 reduce_sum.37
  92.1 0.6 add_reduce_fusion.3
  93.8 11.1 %all_to_all.22 = f32[32,2,1,640]{3,1,2,0:T(2,128)S(1)} all-to-all(f32[32,2,1,640]{3,1,2,0:T(2,128)S(1)} %pad_maximum_fusion.3), channel_id=1, replica_groups=mesh['wide'=16,'narrow'=2] {'wide','narrow'}, dimensions={0} | all-to-all | bytes 327680 | tf_op jit(solution)/shard_map/all_to_all | solution.py:95
  105.0 0.6 copy.16
  105.6 0.7 copy.17
  (36 shorter events, 0.8 us)
Async XLA Ops:
  0.6 5.2 %copy-start = (f32[64,512]{1,0:T(8,128)S(1)}, f32[64,512]{1,0:T(8,128)}, u32[]{:S(2)}) copy-start(f32[64,512]{1,0:T(8,128)} %param.19) | copy-start | bytes 393220
  7.9 14.6 %copy-start.3 = (bf16[2048,1024]{1,0:T(8,128)(2,1)S(1)}, bf16[2048,1024]{1,0:T(8,128)(2,1)}, u32[]{:S(2)}) copy-start(bf16[2048,1024]{1,0:T(8,128)(2,1)} %param.11) | copy-start | bytes 12582916
  16.1 10.4 %copy-start.7 = (f32[1024]{0:T(1024)S(1)}, f32[1024]{0:T(1024)}, u32[]{:S(2)}) copy-start(f32[1024]{0:T(1024)} %param.15) | copy-start | bytes 12292
  16.1 10.5 %copy-start.5 = (bf16[2048,1024]{1,0:T(8,128)(2,1)S(1)}, bf16[2048,1024]{1,0:T(8,128)(2,1)}, u32[]{:S(2)}) copy-start(bf16[2048,1024]{1,0:T(8,128)(2,1)} %param.10) | copy-start | bytes 12582916
  22.5 6.4 %copy-start.1 = (f32[1,1024,1024]{2,1,0:T(8,128)S(1)}, f32[1,1024,1024]{2,1,0:T(8,128)}, u32[]{:S(2)}) copy-start(f32[1,1024,1024]{2,1,0:T(8,128)} %param.12) | copy-start | bytes 12582916
  48.7 20.1 %copy-start.4 = (bf16[2048,1024]{1,0:T(8,128)(2,1)S(1)}, bf16[2048,1024]{1,0:T(8,128)(2,1)}, u32[]{:S(2)}) copy-start(bf16[2048,1024]{1,0:T(8,128)(2,1)} %param.11) | copy-start | bytes 12582916
  62.4 10.5 %copy-start.6 = (bf16[2048,1024]{1,0:T(8,128)(2,1)S(1)}, bf16[2048,1024]{1,0:T(8,128)(2,1)}, u32[]{:S(2)}) copy-start(bf16[2048,1024]{1,0:T(8,128)(2,1)} %param.10) | copy-start | bytes 12582916
  68.8 6.4 %copy-start.2 = (f32[1,1024,1024]{2,1,0:T(8,128)S(1)}, f32[1,1024,1024]{2,1,0:T(8,128)}, u32[]{:S(2)}) copy-start(f32[1,1024,1024]{2,1,0:T(8,128)} %param.12) | copy-start | bytes 12582916
  78.7 13.3 %all-to-all-start.2 = ((f32[32,2,1,1024]{3,1,2,0:T(2,128)}), f32[32,2,1,1024]{3,1,2,0:T(2,128)S(1)}, u32[]{:S(2)}, u32[]{:S(2)}) async-start(f32[32,2,1,1024]{3,1,2,0:T(2,128)} %bitcast.56), calls=%async_computation.2 | async-start | bytes 524288 | tf_op jit(solution)/shard_map/all_to_all | solution.py:74

commit v2 on v1

--- a/solution.py
+++ b/solution.py
@@ -1,16 +1,389 @@
+from functools import partial
+
 import jax
 import jax.numpy as jnp
 from jax import lax
-from jax.sharding import PartitionSpec as P
+from jax.experimental import pallas as pl
+from jax.experimental.pallas import tpu as pltpu
+from jax.sharding import Mesh, PartitionSpec as P
 
 ITERS = 2
 DAMP = 0.5
 HIGHEST = lax.Precision.HIGHEST
-ROWS = (((0,), (0,)), ((), ()))
+F32, BF16 = jnp.float32, jnp.bfloat16
 LAST = (((1,), (1,)), ((), ()))
-
-
-def per_device(
+INNER = (((1,), (0,)), ((), ()))
+SUB, LANE = 8, 128
+VMEM = pl.BlockSpec(memory_space=pltpu.VMEM)
+SMEM = pl.BlockSpec(memory_space=pltpu.SMEM)
+HBM = pl.BlockSpec(memory_space=pl.ANY)
+
+
+def mxu(left, right, dims):
+    return lax.dot_general(left, right, dims, preferred_element_type=F32)
+
+
+def halves(value):
+    high = value.astype(BF16)
+    return high, (value - high.astype(F32)).astype(BF16)
+
+
+def stacked(value):
+    return jnp.concatenate(halves(value), 0)
+
+
+def joined(value):
+    rows = value.shape[0] // 2
+    return value[:rows] + value[rows:]
+
+
+def call(body, name, operands, in_specs, outs, scratch=(), flops=0, moved=0):
+    return pl.pallas_call(
+        body,
+        out_shape=[jax.ShapeDtypeStruct(s, d) for s, d in outs],
+        in_specs=in_specs,
+        out_specs=[VMEM] * len(outs),
+        scratch_shapes=scratch,
+        name=name,
+        compiler_params=pltpu.CompilerParams(vmem_limit_bytes=20 << 20),
+        cost_estimate=pl.CostEstimate(flops=flops, bytes_accessed=moved, transcendentals=0),
+    )(*operands)
+
+
+def pick_body(index, dipole, picked, sem):
+    copies = [
+        pltpu.make_async_copy(dipole.at[pl.ds(index[c], 1)], picked.at[pl.ds(c, 1)], sem.at[c])
+        for c in range(index.shape[0])
+    ]
+    for copy in copies:
+        copy.start()
+    for copy in copies:
+        copy.wait()
+
+
+def prepare_body(
+    index, energy, frequency, blocks, pair_shift, virt, coupling, level, denom, high, low
+):
+    freqs = frequency.shape[0]
+    modes, columns = level.shape
+    slots = coupling.shape[0]
+    device = lax.axis_index(("chip", "core", "narrow"))
+    rows = lax.broadcasted_iota(jnp.int32, (SUB, LANE), 0)
+    tiles = []
+    for start in range(0, modes, SUB):
+        tile = jnp.zeros((SUB, LANE), F32)
+        for k in range(start, start + SUB):
+            value = frequency[k % freqs] + energy[index[k // freqs]]
+            tile = jnp.where(rows == k - start, value, tile)
+        tiles.append(tile)
+    shift = jnp.concatenate(tiles, 0)
+    for at in range(0, columns, LANE):
+        here = jnp.broadcast_to(virt[:, at : at + LANE], (modes, LANE))
+        level[:, at : at + LANE] = here - shift
+        for s in range(slots):
+            offset = pair_shift[blocks[device * slots + s]]
+            denom[s, :, at : at + LANE] = (shift - offset) - here
+    for s in range(slots):
+        upper, lower = halves(coupling[s])
+        high[s] = upper
+        low[s] = lower
+
+
+def fold(response, slab, denom, high, low):
+    modes = response.shape[0] // 2
+    upper, lower = halves(response)
+    both = jnp.concatenate([upper, lower], 0)
+    singles = stacked(joined(mxu(both, slab[...], LAST)))
+    doubles = []
+    for s in range(high.shape[0]):
+        inner = joined(mxu(both, high[s], LAST)) + mxu(upper, low[s], LAST)
+        re, im = inner[:modes], inner[modes:]
+        den = denom[s]
+        inverse = 1.0 / (den * den + DAMP * DAMP)
+        doubles.append(
+            stacked(
+                jnp.concatenate(
+                    [(re * den + im * DAMP) * inverse, (im * den - re * DAMP) * inverse], 0
+                )
+            )
+        )
+    return singles, doubles
+
+
+def unfold(singles, doubles, amplitudes, high, low, columns):
+    total = mxu(singles, amplitudes[:, columns], INNER)
+    for s, outgoing in enumerate(doubles):
+        total = total + mxu(outgoing, high[s, :, columns], INNER)
+    total = joined(total)
+    for s, outgoing in enumerate(doubles):
+        total = total + mxu(outgoing[: outgoing.shape[0] // 2], low[s, :, columns], INNER)
+    return total
+
+
+def first_body(
+    own, other, level, denom, high, low, slab, amplitudes, rhs, start, give, keep
+):
+    modes, virt = level.shape
+    cores, block = own.shape
+    freqs = modes // cores
+    side = lax.axis_index("narrow")
+    for part, at in ((own, side), (other, 1 - side)):
+        columns = pl.ds(pl.multiple_of(at * block, LANE), block)
+        for c in range(cores):
+            rhs[c * freqs : (c + 1) * freqs, columns] = jnp.broadcast_to(
+                part[c : c + 1], (freqs, block)
+            )
+    lev = level[...]
+    inverse = 1.0 / (lev * lev + DAMP * DAMP)
+    start[:modes] = rhs[...] * lev * inverse
+    start[modes:] = rhs[...] * DAMP * inverse
+    singles, doubles = fold(start[...], slab, denom, high, low)
+    core = lax.axis_index("core")
+    half = virt // 2
+    for out, at in ((give, 1 - core), (keep, core)):
+        columns = pl.ds(pl.multiple_of(at * half, LANE), half)
+        total = unfold(singles, doubles, amplitudes, high, low, columns)
+        for group in range(modes // SUB):
+            for tile in range(half // LANE):
+                piece = group * (half // LANE) + tile
+                lanes = slice(tile * LANE, (tile + 1) * LANE)
+                out[piece, 0] = total[group * SUB : (group + 1) * SUB, lanes]
+                out[piece, 1] = total[modes + group * SUB : modes + (group + 1) * SUB, lanes]
+
+
+def add_body(left, right, out):
+    out[...] = left[...] + right[...]
+
+
+def first_update_body(got, level, rhs, start, sent):
+    members = got.shape[0]
+    modes, virt = level.shape
+    tiles = virt // 2 // LANE
+    mine = lax.axis_index(("chip", "narrow"))
+    group, tile = lax.div(mine, tiles), lax.rem(mine, tiles)
+    column = lax.axis_index("core") * (virt // 2) + tile * LANE
+    columns = pl.ds(pl.multiple_of(column, LANE), LANE)
+    rows = pl.ds(pl.multiple_of(group * SUB, SUB), SUB)
+    total = got[0]
+    for j in range(1, members):
+        total = total + got[j]
+    lev, right = level[rows, columns], rhs[rows, columns]
+    re = start[rows, columns]
+    im = start[pl.ds(pl.multiple_of(modes + group * SUB, SUB), SUB), columns]
+    inverse = 1.0 / (lev * lev + DAMP * DAMP)
+    res_re = right - (lev * re + DAMP * im + total[0])
+    res_im = -(lev * im - DAMP * re + total[1])
+    re = re + (res_re * lev - res_im * DAMP) * inverse
+    im = im + (res_im * lev + res_re * DAMP) * inverse
+    for j in range(members):
+        sent[j, 0] = re
+        sent[j, 1] = im
+
+
+def second_body(
+    own, other, level, denom, high, low, slab, amplitudes, response, give, keep
+):
+    modes, virt = level.shape
+    members = own.shape[0]
+    half, quarter = virt // 2, virt // 4
+    core = lax.axis_index("core")
+    for part, at in ((own, core), (other, 1 - core)):
+        for group in range(modes // SUB):
+            for tile in range(half // LANE):
+                piece = group * (half // LANE) + tile
+                columns = pl.ds(pl.multiple_of(at * half + tile * LANE, LANE), LANE)
+                response[group * SUB : (group + 1) * SUB, columns] = part[piece, 0]
+                response[modes + group * SUB : modes + (group + 1) * SUB, columns] = part[piece, 1]
+    singles, doubles = fold(response[...], slab, denom, high, low)
+    owned = modes // members
+    for out, at in ((give, 1 - core), (keep, core)):
+        for side in range(2):
+            columns = pl.ds(pl.multiple_of(side * half + at * quarter, LANE), quarter)
+            total = unfold(singles, doubles, amplitudes, high, low, columns)
+            lanes = slice(side * quarter, (side + 1) * quarter)
+            for j in range(members):
+                out[j, :owned, lanes] = total[j * owned : (j + 1) * owned]
+                out[j, owned:, lanes] = total[modes + j * owned : modes + (j + 1) * owned]
+
+
+def second_update_body(got, level, rhs, start, response, sent):
+    members, double, width = got.shape
+    owned = double // 2
+    modes, virt = level.shape
+    half, quarter = virt // 2, virt // 4
+    mine = lax.axis_index(("chip", "narrow"))
+    core = lax.axis_index("core")
+    total = got[0]
+    for j in range(1, members):
+        total = total + got[j]
+    per_tile = SUB // owned
+    within = lax.rem(mine, per_tile)
+
+    def own_rows(ref, first, columns):
+        at = first + lax.div(mine, per_tile) * SUB
+        tile = ref[pl.ds(pl.multiple_of(at, SUB), SUB), columns]
+        rows = tile[:owned]
+        for q in range(1, per_tile):
+            rows = jnp.where(within == q, tile[q * owned : (q + 1) * owned], rows)
+        return rows
+
+    old_squares = jnp.zeros((owned, 1), F32)
+    new_squares = jnp.zeros((owned, 1), F32)
+    fresh = []
+    for side in range(2):
+        columns = pl.ds(pl.multiple_of(side * half + core * quarter, LANE), quarter)
+        lanes = slice(side * quarter, (side + 1) * quarter)
+        lev, right = own_rows(level, 0, columns), own_rows(rhs, 0, columns)
+        re, im = own_rows(response, 0, columns), own_rows(response, modes, columns)
+        step_re = re - own_rows(start, 0, columns)
+        step_im = im - own_rows(start, modes, columns)
+        old_re = lev * step_re + DAMP * step_im
+        old_im = lev * step_im - DAMP * step_re
+        old_squares += jnp.sum(old_re * old_re + old_im * old_im, axis=1, keepdims=True)
+        inverse = 1.0 / (lev * lev + DAMP * DAMP)
+        res_re = right - (lev * re + DAMP * im + total[:owned, lanes])
+        res_im = -(lev * im - DAMP * re + total[owned:, lanes])
+        new_squares += jnp.sum(res_re * res_re + res_im * res_im, axis=1, keepdims=True)
+        re = re + (res_re * lev - res_im * DAMP) * inverse
+        im = im + (res_im * lev + res_re * DAMP) * inverse
+        fresh.append((re, im))
+    squares = jnp.concatenate([old_squares, new_squares], 0)
+    for j in range(members):
+        re, im = fresh[j % 2]
+        sent[j, :owned, :quarter] = re
+        sent[j, owned:, :quarter] = im
+        sent[j, :, quarter:] = jnp.broadcast_to(squares, (double, LANE))
+
+
+def finish_body(own, other, response, rms):
+    members, double, _ = own.shape
+    owned = double // 2
+    quarter = response.shape[2] // 2
+    sweeps, modes = rms.shape
+    core = lax.axis_index("core")
+    for part, at in ((own, core), (other, 1 - core)):
+        columns = pl.ds(pl.multiple_of(at * quarter, LANE), quarter)
+        for j in range(members):
+            for q in range(2):
+                response[q, j * owned : (j + 1) * owned, columns] = part[
+                    j, q * owned : (q + 1) * owned, :quarter
+                ]
+    row = lax.broadcasted_iota(jnp.int32, (sweeps, LANE), 0)
+    lane = lax.broadcasted_iota(jnp.int32, (sweeps, LANE), 1)
+    squares = jnp.zeros((sweeps, LANE), F32)
+    for j in range(members):
+        both = own[j, :, quarter:] + other[j, :, quarter:]
+        for s in range(sweeps):
+            for i in range(owned):
+                at = s * owned + i
+                value = jnp.broadcast_to(both[at : at + 1], (sweeps, LANE))
+                squares = jnp.where((row == s) & (lane == j * owned + i), value, squares)
+    virt = 4 * quarter
+    rms[...] = jnp.sqrt(squares / (2 * virt) + 1e-6)[:, :modes]
+
+
+def fast_path(
+    chips,
+    narrow,
+    amplitudes,
+    integral_slab,
+    coupling,
+    pair_of_block,
+    pair_shift,
+    virt_energy,
+    core_energy,
+    core_index,
+    frequency,
+    dipole,
+):
+    virt = virt_energy.shape[0]
+    cores = core_index.shape[0]
+    modes = frequency.shape[0] * cores
+    slots = coupling.shape[0]
+    block = dipole.shape[1]
+    rows = amplitudes.shape[0]
+    members = chips * narrow
+    half = virt // 2
+    flip_core = [(0, 1), (1, 0)]
+    group = ("chip", "narrow")
+    cost = dict(flops=8 * modes * virt * (virt * slots + rows), moved=4 * virt * (virt * slots + rows))
+
+    (picked,) = call(
+        pick_body,
+        "pick",
+        (core_index, dipole),
+        [SMEM, HBM],
+        [((cores, block), F32)],
+        scratch=[pltpu.SemaphoreType.DMA((cores,))],
+        moved=cores * block * 4,
+    )
+    across = lax.ppermute(picked, "narrow", flip_core)
+    level, denom, high, low = call(
+        prepare_body,
+        "prepare",
+        (core_index, core_energy, frequency, pair_of_block, pair_shift, virt_energy[None], coupling),
+        [SMEM] * 5 + [VMEM] * 2,
+        [
+            ((modes, virt), F32),
+            ((slots, modes, virt), F32),
+            ((slots, virt, virt), BF16),
+            ((slots, virt, virt), BF16),
+        ],
+        flops=4 * slots * virt * virt,
+        moved=8 * slots * virt * virt,
+    )
+    piece = (members, 2, SUB, LANE)
+    rhs, start, give, keep = call(
+        first_body,
+        "first",
+        (picked, across, level, denom, high, low, integral_slab, amplitudes),
+        [VMEM] * 8,
+        [((modes, virt), F32), ((2 * modes, virt), F32), (piece, F32), (piece, F32)],
+        **cost,
+    )
+    got = lax.ppermute(give, "core", flip_core)
+    (total,) = call(add_body, "add_first", (keep, got), [VMEM] * 2, [(piece, F32)])
+    got = lax.all_to_all(total, group, 0, 0, tiled=True)
+    (sent,) = call(
+        first_update_body, "first_update", (got, level, rhs, start), [VMEM] * 4, [(piece, F32)]
+    )
+    got = lax.all_to_all(sent, group, 0, 0, tiled=True)
+    other = lax.ppermute(got, "core", flip_core)
+    owned = modes // members
+    piece = (members, 2 * owned, half)
+    response, give, keep = call(
+        second_body,
+        "second",
+        (got, other, level, denom, high, low, integral_slab, amplitudes),
+        [VMEM] * 8,
+        [((2 * modes, virt), F32), (piece, F32), (piece, F32)],
+        **cost,
+    )
+    got = lax.ppermute(give, "core", flip_core)
+    (total,) = call(add_body, "add_second", (keep, got), [VMEM] * 2, [(piece, F32)])
+    got = lax.all_to_all(total, group, 0, 0, tiled=True)
+    piece = (members, 2 * owned, half // 2 + LANE)
+    (sent,) = call(
+        second_update_body,
+        "second_update",
+        (got, level, rhs, start, response),
+        [VMEM] * 5,
+        [(piece, F32)],
+    )
+    got = lax.all_to_all(sent, group, 0, 0, tiled=True)
+    other = lax.ppermute(got, "core", flip_core)
+    return tuple(
+        call(
+            finish_body,
+            "finish",
+            (got, other),
+            [VMEM] * 2,
+            [((2, modes, block), F32), ((ITERS, modes), F32)],
+        )
+    )
+
+
+def plain_path(
     wide,
     narrow,
     amplitudes,
@@ -30,11 +403,11 @@
     slots = coupling.shape[0]
     block = dipole.shape[1]
     everyone = modes % (wide * narrow) == 0
-    group = ("wide", "narrow") if everyone else "wide"
+    group = ("chip", "core", "narrow") if everyone else ("chip", "core")
     members = wide * narrow if everyone else wide
     owned = modes // members
 
-    here = lax.axis_index(("wide", "narrow"))
+    here = lax.axis_index(("chip", "core", "narrow"))
     mine = lax.axis_index(group)
     picked = jnp.take(dipole, core_index, axis=0)
     picked = lax.all_gather(picked, "narrow", axis=1, tiled=True)
@@ -50,15 +423,15 @@
     own_level = lax.dynamic_slice_in_dim(level, mine * owned, owned)
     own_mag = own_level * own_level + DAMP * DAMP
     own_re, own_im = own_rhs * own_level / own_mag, own_rhs * DAMP / own_mag
-    slab = integral_slab.astype(jnp.float32)
-    ampl = amplitudes.astype(jnp.float32)
+    slab = integral_slab.astype(F32)
+    ampl = amplitudes.astype(F32)
 
     def dot(left, right, dims):
-        return lax.dot_general(left, right, dims, precision=HIGHEST, preferred_element_type=jnp.float32)
+        return lax.dot_general(left, right, dims, precision=HIGHEST, preferred_element_type=F32)
 
     rms = []
     for sweep in range(ITERS):
-        folded = dot(dot(response, slab, LAST), ampl, (((1,), (0,)), ((), ())))
+        folded = dot(dot(response, slab, LAST), ampl, INNER)
         for slot in range(slots):
             inner = dot(response, coupling[slot], LAST)
             re, im = inner[:modes], inner[modes:]
@@ -69,7 +442,7 @@
                 ],
                 0,
             )
-            folded = folded + dot(quot, coupling[slot], (((1,), (0,)), ((), ())))
+            folded = folded + dot(quot, coupling[slot], INNER)
         pieces = folded.reshape(2, members, owned, virt).transpose(1, 0, 2, 3)
         total = jnp.sum(lax.all_to_all(pieces, group, 0, 0, tiled=True), 0)
         if not everyone:
@@ -91,22 +464,35 @@
     else:
         sent = lax.dynamic_slice_in_dim(own, lax.axis_index("narrow") * block, block, 2)
         sent = jnp.broadcast_to(sent[None], (members,) + sent.shape)
-    extra = jnp.broadcast_to(jnp.stack(rms, 0)[None, :, :, None], (members, 2, owned, 128))
+    extra = jnp.broadcast_to(jnp.stack(rms, 0)[None, :, :, None], (members, 2, owned, LANE))
     got = lax.all_to_all(jnp.concatenate([sent, extra], 3), group, 0, 0, tiled=True)
-    got = got.transpose(1, 0, 2, 3).reshape(2, modes, block + 128)
+    got = got.transpose(1, 0, 2, 3).reshape(2, modes, block + LANE)
     return got[:, :, :block], got[:, :, block]
 
 
 def solution(mesh):
     wide, narrow = mesh.shape["wide"], mesh.shape["narrow"]
-    split = ("wide", "narrow")
+    chips = wide // 2
+    finer = Mesh(mesh.devices.reshape(chips, 2, narrow), ("chip", "core", "narrow"))
+    split = ("chip", "core", "narrow")
 
     def body(*args):
-        return per_device(wide, narrow, *args)
+        virt, modes = args[5].shape[0], args[8].shape[0] * args[7].shape[0]
+        pieces = (modes // SUB) * (virt // LANE)
+        fits = (
+            narrow == 2
+            and pieces == 2 * chips * narrow
+            and modes % (chips * narrow) == 0
+            and SUB % (modes // (chips * narrow)) == 0
+            and virt % (4 * LANE) == 0
+        )
+        if fits:
+            return fast_path(chips, narrow, *args)
+        return plain_path(wide, narrow, *args)
 
     return jax.shard_map(
         body,
-        mesh=mesh,
+        mesh=finer,
         in_specs=(
             P(split, None),
             P(split, None),

time: 107 us -> 75.9 us (0.71)
  matrix products: 30.5 us -> 0 us
  Pallas kernels: 0 us -> 11.2 us
  other arithmetic: 4.88 us -> 0 us
  waiting for transfers between devices: 9.98 us -> 5.22 us
  between operations: 4.87 us -> 0.73 us
  local copies, waits for them, and re-layouts: 7.25 us -> 9.64 us
    dot_general x8 -> x0, matrix products: 30.5 us -> none  [dot(): lax.dot_general(left, right, dims, precision=HIGHEST, preferred_element_t...]
    pallas_call x0 -> x9, Pallas kernels: none -> 11.2 us  [call(): pl.pallas_call(body, out_shape=[jax.ShapeDtypeStruct(s, d) for s, d in ou...]
    all_to_all x1 -> x0, waiting for transfers between devices: 9.98 us -> none  [per_device(): total = jnp.sum(lax.all_to_all(pieces, group, 0, 0, tiled=True), 0)]
    unnamed x17 -> x20, local copies, waits for them, and re-layouts: 0.73 us -> 9.64 us
    all_gather x1 -> x0, blocking collectives: 5.4 us -> none  [per_device(): picked = lax.all_gather(picked, 'narrow', axis=1, tiled=True)]
    ppermute x0 -> x5, waiting for transfers between devices: none -> 5.22 us  [the longest x2 2.64 us: fast_path(): other = lax.ppermute(got, 'core', flip_core)]
    all_to_all x3 -> x4, blocking collectives: 40.8 us -> 45.5 us  [the longest x2 24.2 us: fast_path(): got = lax.all_to_all(total, group, 0, 0, tiled=True)]
    ppermute x0 -> x5, starting transfers between devices: none -> 3.28 us  [the longest x1 3.03 us: fast_path(): across = lax.ppermute(picked, 'narrow', flip_core)]
  transfers between devices with their start and end apart: 1 -> 5, of which waited for: 1 -> 4; matrix products, arithmetic and copies ran while one was open for 0% -> 0% of each run, Pallas kernels for 0% -> 2%
where the time goes in v2:
time: 75.9 us; the launch traced here: 75.5 us
  blocking collectives  45.5 us (60%)
  Pallas kernels  11.2 us (15%)
  local copies, waits for them, and re-layouts  9.64 us (13%)
  waiting for transfers between devices  5.22 us (7%)
  starting transfers between devices  3.28 us (4%)
    all_to_all x2, blocking collectives, fast_path(): got = lax.all_to_all(total, group, 0, 0, tiled=True)  24.2 us
    all_to_all x2, blocking collectives, fast_path(): got = lax.all_to_all(sent, group, 0, 0, tiled=True)  21.3 us
    pallas_call x9, Pallas kernels, call(): pl.pallas_call(body, out_shape=[jax.ShapeDtypeStruct(s, d) for s, d in ou...  11.2 us
    unnamed x20, local copies, waits for them, and re-layouts  9.64 us
    ppermute x1, starting transfers between devices, fast_path(): across = lax.ppermute(picked, 'narrow', flip_core)  3.03 us
    ppermute x2, waiting for transfers between devices, fast_path(): other = lax.ppermute(got, 'core', flip_core)  2.64 us
    ppermute x2, waiting for transfers between devices, fast_path(): got = lax.ppermute(give, 'core', flip_core)  2.58 us
  transfers between devices with their start and end apart: 5, of which 4 were waited for; matrix products, arithmetic and copies ran while one was open for 0% of the time, Pallas kernels for 2%

profile of v2, /device:TPU:0, one launch (start us, length us, event | category | flops | bytes accessed | tf_op | source)
XLA Modules:
  0.0 75.5 jit_solution(12347620218444498251)
XLA Ops:
  0.6 0.0 copy-start
  0.6 0.0 copy-start.3
  0.7 1.0 %copy-done.3 = f32[64,512]{1,0:T(8,128)S(1)} copy-done((f32[64,512]{1,0:T(8,128)S(1)}, f32[64,512]{1,0:T(8,128)}, u32[]{:S(2)}) %copy-start.3) | copy-done | bytes 131096
  1.7 0.9 %copy-done.5 = s32[2]{0:T(128)S(1)} copy-done((s32[2]{0:T(128)S(1)}, s32[2]{0:T(128)}, u32[]{:S(2)}) %copy-start.5) | copy-done | bytes 32
  2.6 0.6 pick.1.own
  3.2 3.0 %collective-permute-start = (f32[2,512]{1,0:T(2,128)S(1)}, f32[2,512]{1,0:T(2,128)S(1)}, u32[]{:S(2)}, u32[]{:S(2)}) collective-permute-start(f32[2,512]{1,0:T(2,128)S(1)} %pick.1.own), channel_id=1, source_target_pairs={{0,1},{1,0},{2,3},{3,2},{4,5},{5,4},{6,7},{7,6},{8,9},{9,8},{10,11... | collective-permute-start | bytes 12296 | tf_op jit(solution)/shard_map/ppermute | solution.py:320
  6.2 2.2 %copy-done.2 = f32[1,1024,1024]{2,1,0:T(8,128)S(1)} copy-done((f32[1,1024,1024]{2,1,0:T(8,128)S(1)}, f32[1,1024,1024]{2,1,0:T(8,128)}, u32[]{:S(2)}) %copy-start.2) | copy-done | bytes 4194328
  8.4 0.7 copy-done.4
  9.1 0.7 copy-done.6
  9.8 0.7 copy-done.7
  10.4 0.7 copy-done.8
  11.1 0.7 copy-done.9
  11.7 1.4 %prepare.1 = (f32[32,1024]{1,0:T(8,128)S(1)}, f32[1,32,1024]{2,1,0:T(8,128)S(1)}, bf16[1,1024,1024]{2,1,0:T(8,128)(2,1)S(1)}, bf16[1,1024,1024]{2,1,0:T(8,128)(2,1)S(1)}) custom-call(s32[2]{0:T(128)S(1)} %copy-done.5, f32[64]{0:T(128)S(1)} %copy-done.6, f32[16]{0:T(128)S(1)} %copy-done.7, s32[32]{0:T(128)S(1)} %copy-done.8, f32[32]{0:T(128)S(1)} %copy-done.9, ...), custom_call_target="tpu_custom_call" | custom-call | flops 4194304 | bytes 8388608 | tf_op jit(solution)/shard_map/prepare/pallas_call | solution.py:41
  13.1 0.0 collective-permute-done.other
  13.2 0.0 copy-start.1
  13.2 2.2 %copy-done.1 = bf16[2048,1024]{1,0:T(8,128)(2,1)S(1)} copy-done((bf16[2048,1024]{1,0:T(8,128)(2,1)S(1)}, bf16[2048,1024]{1,0:T(8,128)(2,1)}, u32[]{:S(2)}) %copy-start.1) | copy-done | bytes 4194328
  15.4 4.1 %first.1 = (f32[32,1024]{1,0:T(8,128)S(1)}, f32[64,1024]{1,0:T(8,128)S(1)}, f32[16,2,8,128]{3,2,1,0:T(8,128)S(1)}, f32[16,2,8,128]{3,2,1,0:T(8,128)S(1)}) custom-call(f32[2,512]{1,0:T(2,128)S(1)} %pick.1.own, f32[2,512]{1,0:T(2,128)S(1)} %collective-permute-done.other, f32[32,1024]{1,0:T(8,128)S(1)} %get-tuple-element.13.level, ...), custom_call_target="tpu_custom_call" | custom-call | flops 805306368 | bytes 12582912 | tf_op jit(solution)/shard_map/first/pallas_call | solution.py:41
  19.4 0.1 collective-permute-start.1
  19.5 1.3 %collective-permute-done.1.right = f32[16,2,8,128]{3,2,1,0:T(8,128)S(1)} collective-permute-done((f32[16,2,8,128]{3,2,1,0:T(8,128)S(1)}, f32[16,2,8,128]{3,2,1,0:T(8,128)S(1)}, u32[]{:S(2)}, u32[]{:S(2)}) %collective-permute-start.1) | collective-permute-done | bytes 131104 | tf_op jit(solution)/shard_map/ppermute | solution.py:344
  20.9 13.5 %all_to_all.20.got = f32[16,2,8,128]{3,2,1,0:T(8,128)S(1)} all-to-all(f32[16,2,8,128]{3,2,1,0:T(8,128)S(1)} %add_first.1), channel_id=1, replica_groups=mesh['chip'=8,'core'=2,'narrow'=2] {'chip','narrow'}, dimensions={0} | all-to-all | bytes 262144 | tf_op jit(solution)/shard_map/all_to_all | solution.py:346
  34.4 10.7 %all_to_all.21.own = f32[16,2,8,128]{3,2,1,0:T(8,128)S(1)} all-to-all(f32[16,2,8,128]{3,2,1,0:T(8,128)S(1)} %first_update.1), channel_id=1, replica_groups=mesh['chip'=8,'core'=2,'narrow'=2] {'chip','narrow'}, dimensions={0} | all-to-all | bytes 262144 | tf_op jit(solution)/shard_map/all_to_all | solution.py:350
  45.1 0.0 collective-permute-start.2
  45.1 1.3 %collective-permute-done.2.other = f32[16,2,8,128]{3,2,1,0:T(8,128)S(1)} collective-permute-done((f32[16,2,8,128]{3,2,1,0:T(8,128)S(1)}, f32[16,2,8,128]{3,2,1,0:T(8,128)S(1)}, u32[]{:S(2)}, u32[]{:S(2)}) %collective-permute-start.2) | collective-permute-done | bytes 131104 | tf_op jit(solution)/shard_map/ppermute | solution.py:351
  46.5 4.2 %second.1 = (f32[64,1024]{1,0:T(8,128)S(1)}, f32[16,4,512]{2,1,0:T(4,128)S(1)}, f32[16,4,512]{2,1,0:T(4,128)S(1)}) custom-call(f32[16,2,8,128]{3,2,1,0:T(8,128)S(1)} %all_to_all.21.own, f32[16,2,8,128]{3,2,1,0:T(8,128)S(1)} %collective-permute-done.2.other, f32[32,1024]{1,0:T(8,128)S(1)} %get-tuple-element.13.level, ...), custom_call_target="tpu_custom_call" | custom-call | flops 805306368 | bytes 12582912 | tf_op jit(solution)/shard_map/second/pallas_call | solution.py:41
  50.7 0.2 collective-permute-start.3
  50.8 1.2 %collective-permute-done.3.right = f32[16,4,512]{2,1,0:T(4,128)S(1)} collective-permute-done((f32[16,4,512]{2,1,0:T(4,128)S(1)}, f32[16,4,512]{2,1,0:T(4,128)S(1)}, u32[]{:S(2)}, u32[]{:S(2)}) %collective-permute-start.3) | collective-permute-done | bytes 131104 | tf_op jit(solution)/shard_map/ppermute | solution.py:362
  52.1 10.6 %all_to_all.22.got = f32[16,4,512]{2,1,0:T(4,128)S(1)} all-to-all(f32[16,4,512]{2,1,0:T(4,128)S(1)} %add_second.1), channel_id=1, replica_groups=mesh['chip'=8,'core'=2,'narrow'=2] {'chip','narrow'}, dimensions={0} | all-to-all | bytes 262144 | tf_op jit(solution)/shard_map/all_to_all | solution.py:364
  62.7 0.2 second_update.1
  62.9 10.6 %all_to_all.23.own = f32[16,4,384]{2,1,0:T(4,128)S(1)} all-to-all(f32[16,4,384]{2,1,0:T(4,128)S(1)} %second_update.1), channel_id=1, replica_groups=mesh['chip'=8,'core'=2,'narrow'=2] {'chip','narrow'}, dimensions={0} | all-to-all | bytes 196608 | tf_op jit(solution)/shard_map/all_to_all | solution.py:373
  73.5 0.0 collective-permute-start.4
  73.5 1.3 %collective-permute-done.4.other = f32[16,4,384]{2,1,0:T(4,128)S(1)} collective-permute-done((f32[16,4,384]{2,1,0:T(4,128)S(1)}, f32[16,4,384]{2,1,0:T(4,128)S(1)}, u32[]{:S(2)}, u32[]{:S(2)}) %collective-permute-start.4) | collective-permute-done | bytes 98336 | tf_op jit(solution)/shard_map/ppermute | solution.py:374
  74.8 0.7 finish.1
  (11 shorter events, 0.1 us)
Async XLA Ops:
  0.6 12.5 %copy-start = (bf16[2048,1024]{1,0:T(8,128)(2,1)S(1)}, bf16[2048,1024]{1,0:T(8,128)(2,1)}, u32[]{:S(2)}) copy-start(bf16[2048,1024]{1,0:T(8,128)(2,1)} %slab.3) | copy-start | bytes 12582916
  0.6 1.1 %copy-start.3 = (f32[64,512]{1,0:T(8,128)S(1)}, f32[64,512]{1,0:T(8,128)}, u32[]{:S(2)}) copy-start(f32[64,512]{1,0:T(8,128)} %dipole.1) | copy-start | bytes 393220
  1.7 0.9 %copy-start.5 = (s32[2]{0:T(128)S(1)}, s32[2]{0:T(128)}, u32[]{:S(2)}) copy-start(s32[2]{0:T(128)} %index.3) | copy-start | bytes 28
  3.2 10.0 %collective-permute-start = (f32[2,512]{1,0:T(2,128)S(1)}, f32[2,512]{1,0:T(2,128)S(1)}, u32[]{:S(2)}, u32[]{:S(2)}) collective-permute-start(f32[2,512]{1,0:T(2,128)S(1)} %pick.1.own), channel_id=1, source_target_pairs={{0,1},{1,0},{2,3},{3,2},{4,5},{5,4},{6,7},{7,6},{8,9},{9,8},{10,11... | collective-permute-start | bytes 12296 | tf_op jit(solution)/shard_map/ppermute | solution.py:320
  6.2 2.2 %copy-start.2 = (f32[1,1024,1024]{2,1,0:T(8,128)S(1)}, f32[1,1024,1024]{2,1,0:T(8,128)}, u32[]{:S(2)}) copy-start(f32[1,1024,1024]{2,1,0:T(8,128)} %coupling.1) | copy-start | bytes 12582916
  8.4 0.7 copy-start.4
  9.1 0.7 copy-start.6
  9.8 0.7 copy-start.7
  10.4 0.7 copy-start.8
  11.1 0.7 copy-start.9
  13.2 2.2 %copy-start.1 = (bf16[2048,1024]{1,0:T(8,128)(2,1)S(1)}, bf16[2048,1024]{1,0:T(8,128)(2,1)}, u32[]{:S(2)}) copy-start(bf16[2048,1024]{1,0:T(8,128)(2,1)} %amplitudes.3) | copy-start | bytes 12582916
  19.4 1.4 %collective-permute-start.1 = (f32[16,2,8,128]{3,2,1,0:T(8,128)S(1)}, f32[16,2,8,128]{3,2,1,0:T(8,128)S(1)}, u32[]{:S(2)}, u32[]{:S(2)}) collective-permute-start(f32[16,2,8,128]{3,2,1,0:T(8,128)S(1)} %get-tuple-element.18), channel_id=1, source_target_pairs={{0,2},{2,0},{1,3},{3,1},{4,6},{6,4},{5,7},{7,5},{8,10},{10,8},{9,1... | collective-permute-start | bytes 393224 | tf_op jit(solution)/shard_map/ppermute | solution.py:344
  45.1 1.3 %collective-permute-start.2 = (f32[16,2,8,128]{3,2,1,0:T(8,128)S(1)}, f32[16,2,8,128]{3,2,1,0:T(8,128)S(1)}, u32[]{:S(2)}, u32[]{:S(2)}) collective-permute-start(f32[16,2,8,128]{3,2,1,0:T(8,128)S(1)} %all_to_all.21.own), channel_id=1, source_target_pairs={{0,2},{2,0},{1,3},{3,1},{4,6},{6,4},{5,7},{7,5},{8,10},{10,8},{9,1... | collective-permute-start | bytes 393224 | tf_op jit(solution)/shard_map/ppermute | solution.py:351
  50.7 1.4 %collective-permute-start.3 = (f32[16,4,512]{2,1,0:T(4,128)S(1)}, f32[16,4,512]{2,1,0:T(4,128)S(1)}, u32[]{:S(2)}, u32[]{:S(2)}) collective-permute-start(f32[16,4,512]{2,1,0:T(4,128)S(1)} %get-tuple-element.22), channel_id=1, source_target_pairs={{0,2},{2,0},{1,3},{3,1},{4,6},{6,4},{5,7},{7,5},{8,10},{10,8},{9,1... | collective-permute-start | bytes 393224 | tf_op jit(solution)/shard_map/ppermute | solution.py:362
  73.5 1.3 %collective-permute-start.4 = (f32[16,4,384]{2,1,0:T(4,128)S(1)}, f32[16,4,384]{2,1,0:T(4,128)S(1)}, u32[]{:S(2)}, u32[]{:S(2)}) collective-permute-start(f32[16,4,384]{2,1,0:T(4,128)S(1)} %all_to_all.23.own), channel_id=1, source_target_pairs={{0,2},{2,0},{1,3},{3,1},{4,6},{6,4},{5,7},{7,5},{8,10},{10,8},{9,1... | collective-permute-start | bytes 294920 | tf_op jit(solution)/shard_map/ppermute | solution.py:374

commit v3 on v2

--- a/solution.py
+++ b/solution.py
@@ -16,7 +16,8 @@
 SUB, LANE = 8, 128
 VMEM = pl.BlockSpec(memory_space=pltpu.VMEM)
 SMEM = pl.BlockSpec(memory_space=pltpu.SMEM)
-HBM = pl.BlockSpec(memory_space=pl.ANY)
+HBM = pl.BlockSpec(memory_space=pltpu.HBM)
+PARTS = 4
 
 
 def mxu(left, right, dims):
@@ -38,6 +39,10 @@
 
 
 def call(body, name, operands, in_specs, outs, scratch=(), flops=0, moved=0):
+    operands = [
+        pltpu.with_memory_space_constraint(x, pltpu.HBM) if spec is HBM else x
+        for x, spec in zip(operands, in_specs)
+    ]
     return pl.pallas_call(
         body,
         out_shape=[jax.ShapeDtypeStruct(s, d) for s, d in outs],
@@ -50,23 +55,73 @@
     )(*operands)
 
 
-def pick_body(index, dipole, picked, sem):
-    copies = [
-        pltpu.make_async_copy(dipole.at[pl.ds(index[c], 1)], picked.at[pl.ds(c, 1)], sem.at[c])
-        for c in range(index.shape[0])
-    ]
+def start_all(pairs, sems):
+    copies = [pltpu.make_async_copy(src, dst, sems.at[i]) for i, (src, dst) in enumerate(pairs)]
     for copy in copies:
         copy.start()
+    return copies
+
+
+def pick_body(index_hbm, dipole_hbm, picked, index, dipole, sems):
+    copies = start_all([(index_hbm, index), (dipole_hbm, dipole)], sems)
     for copy in copies:
         copy.wait()
+    for c in range(index.shape[0]):
+        picked[c : c + 1] = dipole[pl.ds(index[c], 1)]
 
 
 def prepare_body(
-    index, energy, frequency, blocks, pair_shift, virt, coupling, level, denom, high, low
+    index_hbm,
+    energy_hbm,
+    frequency_hbm,
+    blocks_hbm,
+    pair_shift_hbm,
+    virt_hbm,
+    coupling_hbm,
+    slab_hbm,
+    level,
+    denom,
+    high,
+    low,
+    slab,
+    index,
+    energy,
+    frequency,
+    blocks,
+    pair_shift,
+    virt,
+    coupling,
+    small_sems,
+    coupling_sems,
+    slab_sems,
 ):
     freqs = frequency.shape[0]
     modes, columns = level.shape
     slots = coupling.shape[0]
+    small = start_all(
+        [
+            (index_hbm, index),
+            (energy_hbm, energy),
+            (frequency_hbm, frequency),
+            (blocks_hbm, blocks),
+            (pair_shift_hbm, pair_shift),
+            (virt_hbm, virt),
+        ],
+        small_sems,
+    )
+    step = coupling.shape[1] // PARTS
+    parts = [(s, slice(i * step, (i + 1) * step)) for s in range(slots) for i in range(PARTS)]
+    coupled = start_all([(coupling_hbm.at[s, r], coupling.at[s, r]) for s, r in parts], coupling_sems)
+    step = slab.shape[0] // PARTS
+    slabs = start_all(
+        [
+            (slab_hbm.at[i * step : (i + 1) * step], slab.at[i * step : (i + 1) * step])
+            for i in range(PARTS)
+        ],
+        slab_sems,
+    )
+    for copy in small:
+        copy.wait()
     device = lax.axis_index(("chip", "core", "narrow"))
     rows = lax.broadcasted_iota(jnp.int32, (SUB, LANE), 0)
     tiles = []
@@ -83,10 +138,13 @@
         for s in range(slots):
             offset = pair_shift[blocks[device * slots + s]]
             denom[s, :, at : at + LANE] = (shift - offset) - here
-    for s in range(slots):
-        upper, lower = halves(coupling[s])
-        high[s] = upper
-        low[s] = lower
+    for (s, r), copy in zip(parts, coupled):
+        copy.wait()
+        upper, lower = halves(coupling[s, r])
+        high[s, r] = upper
+        low[s, r] = lower
+    for copy in slabs:
+        copy.wait()
 
 
 def fold(response, slab, denom, high, low):
@@ -121,8 +179,32 @@
 
 
 def first_body(
-    own, other, level, denom, high, low, slab, amplitudes, rhs, start, give, keep
+    own,
+    other,
+    level,
+    denom,
+    high,
+    low,
+    slab,
+    amplitudes_hbm,
+    rhs,
+    start,
+    give,
+    keep,
+    amplitudes,
+    sems,
 ):
+    step = amplitudes.shape[0] // PARTS
+    copies = start_all(
+        [
+            (
+                amplitudes_hbm.at[i * step : (i + 1) * step],
+                amplitudes.at[i * step : (i + 1) * step],
+            )
+            for i in range(PARTS)
+        ],
+        sems,
+    )
     modes, virt = level.shape
     cores, block = own.shape
     freqs = modes // cores
@@ -138,6 +220,8 @@
     start[:modes] = rhs[...] * lev * inverse
     start[modes:] = rhs[...] * DAMP * inverse
     singles, doubles = fold(start[...], slab, denom, high, low)
+    for copy in copies:
+        copy.wait()
     core = lax.axis_index("core")
     half = virt // 2
     for out, at in ((give, 1 - core), (keep, core)):
@@ -312,33 +396,54 @@
         pick_body,
         "pick",
         (core_index, dipole),
-        [SMEM, HBM],
+        [HBM, HBM],
         [((cores, block), F32)],
-        scratch=[pltpu.SemaphoreType.DMA((cores,))],
+        scratch=[
+            pltpu.SMEM(core_index.shape, jnp.int32),
+            pltpu.VMEM(dipole.shape, F32),
+            pltpu.SemaphoreType.DMA((2,)),
+        ],
         moved=cores * block * 4,
     )
     across = lax.ppermute(picked, "narrow", flip_core)
-    level, denom, high, low = call(
+    scalars = (core_index, core_energy, frequency, pair_of_block, pair_shift)
+    level, denom, high, low, slab = call(
         prepare_body,
         "prepare",
-        (core_index, core_energy, frequency, pair_of_block, pair_shift, virt_energy[None], coupling),
-        [SMEM] * 5 + [VMEM] * 2,
+        scalars + (virt_energy[None], coupling, integral_slab),
+        [HBM] * 8,
         [
             ((modes, virt), F32),
             ((slots, modes, virt), F32),
             ((slots, virt, virt), BF16),
             ((slots, virt, virt), BF16),
+            (integral_slab.shape, BF16),
+        ],
+        scratch=[pltpu.SMEM(a.shape, a.dtype) for a in scalars]
+        + [
+            pltpu.VMEM((1, virt), F32),
+            pltpu.VMEM(coupling.shape, F32),
+            pltpu.SemaphoreType.DMA((6,)),
+            pltpu.SemaphoreType.DMA((PARTS * slots,)),
+            pltpu.SemaphoreType.DMA((PARTS,)),
         ],
         flops=4 * slots * virt * virt,
         moved=8 * slots * virt * virt,
     )
     piece = (members, 2, SUB, LANE)
-    rhs, start, give, keep = call(
+    rhs, start, give, keep, held = call(
         first_body,
         "first",
-        (picked, across, level, denom, high, low, integral_slab, amplitudes),
-        [VMEM] * 8,
-        [((modes, virt), F32), ((2 * modes, virt), F32), (piece, F32), (piece, F32)],
+        (picked, across, level, denom, high, low, slab, amplitudes),
+        [VMEM] * 7 + [HBM],
+        [
+            ((modes, virt), F32),
+            ((2 * modes, virt), F32),
+            (piece, F32),
+            (piece, F32),
+            (amplitudes.shape, BF16),
+        ],
+        scratch=[pltpu.SemaphoreType.DMA((PARTS,))],
         **cost,
     )
     got = lax.ppermute(give, "core", flip_core)
@@ -354,7 +459,7 @@
     response, give, keep = call(
         second_body,
         "second",
-        (got, other, level, denom, high, low, integral_slab, amplitudes),
+        (got, other, level, denom, high, low, slab, held),
         [VMEM] * 8,
         [((2 * modes, virt), F32), (piece, F32), (piece, F32)],
         **cost,

time: 75.9 us -> 68.7 us (0.905)
  local copies, waits for them, and re-layouts: 9.64 us -> 0 us
  Pallas kernels: 11.2 us -> 13.8 us
    unnamed x20 -> x0, local copies, waits for them, and re-layouts: 9.64 us -> none
    pallas_call x9, Pallas kernels: 11.2 us -> 13.8 us  [call(): pl.pallas_call(body, out_shape=[jax.ShapeDtypeStruct(s, d) for s, d in ou...]
  transfers between devices with their start and end apart: 5 -> 5, of which waited for: 4 -> 4; matrix products, arithmetic and copies ran while one was open for 0% -> 0% of each run, Pallas kernels for 2% -> 5%
where the time goes in v3:
time: 68.7 us; the launch traced here: 68.4 us
  blocking collectives  45.5 us (66%)
  Pallas kernels  13.8 us (20%)
  waiting for transfers between devices  5.18 us (8%)
  starting transfers between devices  3.32 us (5%)
  between operations  0.69 us (1%)
    all_to_all x2, blocking collectives, fast_path(): got = lax.all_to_all(total, group, 0, 0, tiled=True)  24.2 us
    all_to_all x2, blocking collectives, fast_path(): got = lax.all_to_all(sent, group, 0, 0, tiled=True)  21.3 us
    pallas_call x9, Pallas kernels, call(): pl.pallas_call(body, out_shape=[jax.ShapeDtypeStruct(s, d) for s, d in ou...  13.8 us
    ppermute x1, starting transfers between devices, fast_path(): across = lax.ppermute(picked, 'narrow', flip_core)  3.03 us
    ppermute x2, waiting for transfers between devices, fast_path(): other = lax.ppermute(got, 'core', flip_core)  2.64 us
    ppermute x2, waiting for transfers between devices, fast_path(): got = lax.ppermute(give, 'core', flip_core)  2.54 us
  transfers between devices with their start and end apart: 5, of which 4 were waited for; matrix products, arithmetic and copies ran while one was open for 0% of the time, Pallas kernels for 5%

profile of v3, /device:TPU:0, one launch (start us, length us, event | category | flops | bytes accessed | tf_op | source)
XLA Modules:
  0.0 68.4 jit_solution(9867024630229749788)
XLA Ops:
  0.6 0.9 %pick.1.own = f32[2,512]{1,0:T(2,128)S(1)} custom-call(s32[2]{0:T(128)} %index_hbm.3, f32[64,512]{1,0:T(8,128)} %dipole_hbm.1), custom_call_target="tpu_custom_call" | custom-call | bytes 4096 | tf_op jit(solution)/shard_map/pick/pallas_call | solution.py:46
  1.6 3.0 %collective-permute-start = (f32[2,512]{1,0:T(2,128)S(1)}, f32[2,512]{1,0:T(2,128)S(1)}, u32[]{:S(2)}, u32[]{:S(2)}) collective-permute-start(f32[2,512]{1,0:T(2,128)S(1)} %pick.1.own), channel_id=1, source_target_pairs={{0,1},{1,0},{2,3},{3,2},{4,5},{5,4},{6,7},{7,6},{8,9},{9,8},{10,11... | collective-permute-start | bytes 12296 | tf_op jit(solution)/shard_map/ppermute | solution.py:408
  4.6 3.5 %prepare.1 = (f32[32,1024]{1,0:T(8,128)S(1)}, f32[1,32,1024]{2,1,0:T(8,128)S(1)}, bf16[1,1024,1024]{2,1,0:T(8,128)(2,1)S(1)}, bf16[1,1024,1024]{2,1,0:T(8,128)(2,1)S(1)}, bf16[2048,1024]{1,0:T(8,128)(2,1)S(1)}) custom-call(s32[2]{0:T(128)} %index_hbm.3, f32[64]{0:T(128)} %energy_hbm.1, f32[16]{0:T(128)} %frequency_hbm.1, s32[32]{0:T(128)} %blocks_hbm.1, ...), custom_call_target="tpu_custom_call" | custom-call | flops 4194304 | bytes 8388608 | tf_op jit(solution)/shard_map/prepare/pallas_call | solution.py:46
  8.1 0.0 collective-permute-done.other
  8.2 4.2 %first.1 = (f32[32,1024]{1,0:T(8,128)S(1)}, f32[64,1024]{1,0:T(8,128)S(1)}, f32[16,2,8,128]{3,2,1,0:T(8,128)S(1)}, f32[16,2,8,128]{3,2,1,0:T(8,128)S(1)}, bf16[2048,1024]{1,0:T(8,128)(2,1)S(1)}) custom-call(f32[2,512]{1,0:T(2,128)S(1)} %pick.1.own, f32[2,512]{1,0:T(2,128)S(1)} %collective-permute-done.other, f32[32,1024]{1,0:T(8,128)S(1)} %get-tuple-element.15.level, ...), custom_call_target="tpu_custom_call" | custom-call | flops 805306368 | bytes 12582912 | tf_op jit(solution)/shard_map/first/pallas_call | solution.py:46
  12.4 0.1 collective-permute-start.1
  12.5 1.3 %collective-permute-done.1.right = f32[16,2,8,128]{3,2,1,0:T(8,128)S(1)} collective-permute-done((f32[16,2,8,128]{3,2,1,0:T(8,128)S(1)}, f32[16,2,8,128]{3,2,1,0:T(8,128)S(1)}, u32[]{:S(2)}, u32[]{:S(2)}) %collective-permute-start.1) | collective-permute-done | bytes 131104 | tf_op jit(solution)/shard_map/ppermute | solution.py:449
  13.8 13.5 %all_to_all.20.got = f32[16,2,8,128]{3,2,1,0:T(8,128)S(1)} all-to-all(f32[16,2,8,128]{3,2,1,0:T(8,128)S(1)} %add_first.1), channel_id=1, replica_groups=mesh['chip'=8,'core'=2,'narrow'=2] {'chip','narrow'}, dimensions={0} | all-to-all | bytes 262144 | tf_op jit(solution)/shard_map/all_to_all | solution.py:451
  27.4 10.7 %all_to_all.21.own = f32[16,2,8,128]{3,2,1,0:T(8,128)S(1)} all-to-all(f32[16,2,8,128]{3,2,1,0:T(8,128)S(1)} %first_update.1), channel_id=1, replica_groups=mesh['chip'=8,'core'=2,'narrow'=2] {'chip','narrow'}, dimensions={0} | all-to-all | bytes 262144 | tf_op jit(solution)/shard_map/all_to_all | solution.py:455
  38.1 0.0 collective-permute-start.2
  38.1 1.3 %collective-permute-done.2.other = f32[16,2,8,128]{3,2,1,0:T(8,128)S(1)} collective-permute-done((f32[16,2,8,128]{3,2,1,0:T(8,128)S(1)}, f32[16,2,8,128]{3,2,1,0:T(8,128)S(1)}, u32[]{:S(2)}, u32[]{:S(2)}) %collective-permute-start.2) | collective-permute-done | bytes 131104 | tf_op jit(solution)/shard_map/ppermute | solution.py:456
  39.5 4.1 %second.1 = (f32[64,1024]{1,0:T(8,128)S(1)}, f32[16,4,512]{2,1,0:T(4,128)S(1)}, f32[16,4,512]{2,1,0:T(4,128)S(1)}) custom-call(f32[16,2,8,128]{3,2,1,0:T(8,128)S(1)} %all_to_all.21.own, f32[16,2,8,128]{3,2,1,0:T(8,128)S(1)} %collective-permute-done.2.other, f32[32,1024]{1,0:T(8,128)S(1)} %get-tuple-element.15.level, ...), custom_call_target="tpu_custom_call" | custom-call | flops 805306368 | bytes 12582912 | tf_op jit(solution)/shard_map/second/pallas_call | solution.py:46
  43.6 0.2 collective-permute-start.3
  43.8 1.2 %collective-permute-done.3.right = f32[16,4,512]{2,1,0:T(4,128)S(1)} collective-permute-done((f32[16,4,512]{2,1,0:T(4,128)S(1)}, f32[16,4,512]{2,1,0:T(4,128)S(1)}, u32[]{:S(2)}, u32[]{:S(2)}) %collective-permute-start.3) | collective-permute-done | bytes 131104 | tf_op jit(solution)/shard_map/ppermute | solution.py:467
  45.0 10.6 %all_to_all.22.got = f32[16,4,512]{2,1,0:T(4,128)S(1)} all-to-all(f32[16,4,512]{2,1,0:T(4,128)S(1)} %add_second.1), channel_id=1, replica_groups=mesh['chip'=8,'core'=2,'narrow'=2] {'chip','narrow'}, dimensions={0} | all-to-all | bytes 262144 | tf_op jit(solution)/shard_map/all_to_all | solution.py:469
  55.6 0.2 second_update.1
  55.8 10.6 %all_to_all.23.own = f32[16,4,384]{2,1,0:T(4,128)S(1)} all-to-all(f32[16,4,384]{2,1,0:T(4,128)S(1)} %second_update.1), channel_id=1, replica_groups=mesh['chip'=8,'core'=2,'narrow'=2] {'chip','narrow'}, dimensions={0} | all-to-all | bytes 196608 | tf_op jit(solution)/shard_map/all_to_all | solution.py:478
  66.4 0.0 collective-permute-start.4
  66.4 1.3 %collective-permute-done.4.other = f32[16,4,384]{2,1,0:T(4,128)S(1)} collective-permute-done((f32[16,4,384]{2,1,0:T(4,128)S(1)}, f32[16,4,384]{2,1,0:T(4,128)S(1)}, u32[]{:S(2)}, u32[]{:S(2)}) %collective-permute-start.4) | collective-permute-done | bytes 98336 | tf_op jit(solution)/shard_map/ppermute | solution.py:479
  67.7 0.7 %finish.1 = (f32[2,32,512]{2,1,0:T(8,128)}, f32[2,32]{1,0:T(2,128)}) custom-call(f32[16,4,384]{2,1,0:T(4,128)S(1)} %all_to_all.23.own, f32[16,4,384]{2,1,0:T(4,128)S(1)} %collective-permute-done.4.other), custom_call_target="tpu_custom_call" | custom-call | tf_op jit(solution)/shard_map/finish/pallas_call | solution.py:46
  (3 shorter events, 0.1 us)
Async XLA Ops:
  1.6 6.6 %collective-permute-start = (f32[2,512]{1,0:T(2,128)S(1)}, f32[2,512]{1,0:T(2,128)S(1)}, u32[]{:S(2)}, u32[]{:S(2)}) collective-permute-start(f32[2,512]{1,0:T(2,128)S(1)} %pick.1.own), channel_id=1, source_target_pairs={{0,1},{1,0},{2,3},{3,2},{4,5},{5,4},{6,7},{7,6},{8,9},{9,8},{10,11... | collective-permute-start | bytes 12296 | tf_op jit(solution)/shard_map/ppermute | solution.py:408
  12.4 1.4 %collective-permute-start.1 = (f32[16,2,8,128]{3,2,1,0:T(8,128)S(1)}, f32[16,2,8,128]{3,2,1,0:T(8,128)S(1)}, u32[]{:S(2)}, u32[]{:S(2)}) collective-permute-start(f32[16,2,8,128]{3,2,1,0:T(8,128)S(1)} %get-tuple-element.21), channel_id=1, source_target_pairs={{0,2},{2,0},{1,3},{3,1},{4,6},{6,4},{5,7},{7,5},{8,10},{10,8},{9,1... | collective-permute-start | bytes 393224 | tf_op jit(solution)/shard_map/ppermute | solution.py:449
  38.1 1.3 %collective-permute-start.2 = (f32[16,2,8,128]{3,2,1,0:T(8,128)S(1)}, f32[16,2,8,128]{3,2,1,0:T(8,128)S(1)}, u32[]{:S(2)}, u32[]{:S(2)}) collective-permute-start(f32[16,2,8,128]{3,2,1,0:T(8,128)S(1)} %all_to_all.21.own), channel_id=1, source_target_pairs={{0,2},{2,0},{1,3},{3,1},{4,6},{6,4},{5,7},{7,5},{8,10},{10,8},{9,1... | collective-permute-start | bytes 393224 | tf_op jit(solution)/shard_map/ppermute | solution.py:456
  43.6 1.4 %collective-permute-start.3 = (f32[16,4,512]{2,1,0:T(4,128)S(1)}, f32[16,4,512]{2,1,0:T(4,128)S(1)}, u32[]{:S(2)}, u32[]{:S(2)}) collective-permute-start(f32[16,4,512]{2,1,0:T(4,128)S(1)} %get-tuple-element.26), channel_id=1, source_target_pairs={{0,2},{2,0},{1,3},{3,1},{4,6},{6,4},{5,7},{7,5},{8,10},{10,8},{9,1... | collective-permute-start | bytes 393224 | tf_op jit(solution)/shard_map/ppermute | solution.py:467
  66.4 1.3 %collective-permute-start.4 = (f32[16,4,384]{2,1,0:T(4,128)S(1)}, f32[16,4,384]{2,1,0:T(4,128)S(1)}, u32[]{:S(2)}, u32[]{:S(2)}) collective-permute-start(f32[16,4,384]{2,1,0:T(4,128)S(1)} %all_to_all.23.own), channel_id=1, source_target_pairs={{0,2},{2,0},{1,3},{3,1},{4,6},{6,4},{5,7},{7,5},{8,10},{10,8},{9,1... | collective-permute-start | bytes 294920 | tf_op jit(solution)/shard_map/ppermute | solution.py:479

commit v4 on v3

--- a/solution.py
+++ b/solution.py
@@ -17,7 +17,8 @@
 VMEM = pl.BlockSpec(memory_space=pltpu.VMEM)
 SMEM = pl.BlockSpec(memory_space=pltpu.SMEM)
 HBM = pl.BlockSpec(memory_space=pltpu.HBM)
-PARTS = 4
+PARTS = 8
+WINDOW = 11
 
 
 def mxu(left, right, dims):
@@ -62,14 +63,6 @@
     return copies
 
 
-def pick_body(index_hbm, dipole_hbm, picked, index, dipole, sems):
-    copies = start_all([(index_hbm, index), (dipole_hbm, dipole)], sems)
-    for copy in copies:
-        copy.wait()
-    for c in range(index.shape[0]):
-        picked[c : c + 1] = dipole[pl.ds(index[c], 1)]
-
-
 def prepare_body(
     index_hbm,
     energy_hbm,
@@ -77,20 +70,25 @@
     blocks_hbm,
     pair_shift_hbm,
     virt_hbm,
+    dipole_hbm,
     coupling_hbm,
     slab_hbm,
+    picked,
+    chosen,
     level,
     denom,
     high,
     low,
-    slab,
+    slab_t,
     index,
     energy,
     frequency,
     blocks,
     pair_shift,
     virt,
+    dipole,
     coupling,
+    slab,
     small_sems,
     coupling_sems,
     slab_sems,
@@ -106,22 +104,36 @@
             (blocks_hbm, blocks),
             (pair_shift_hbm, pair_shift),
             (virt_hbm, virt),
+            (dipole_hbm, dipole),
         ],
         small_sems,
     )
     step = coupling.shape[1] // PARTS
     parts = [(s, slice(i * step, (i + 1) * step)) for s in range(slots) for i in range(PARTS)]
-    coupled = start_all([(coupling_hbm.at[s, r], coupling.at[s, r]) for s, r in parts], coupling_sems)
+    coupled = [
+        pltpu.make_async_copy(coupling_hbm.at[s, r], coupling.at[s, r], coupling_sems.at[i])
+        for i, (s, r) in enumerate(parts)
+    ]
     step = slab.shape[0] // PARTS
-    slabs = start_all(
-        [
-            (slab_hbm.at[i * step : (i + 1) * step], slab.at[i * step : (i + 1) * step])
-            for i in range(PARTS)
-        ],
-        slab_sems,
-    )
+    pieces = [slice(i * step, (i + 1) * step) for i in range(PARTS)]
+    slabs = [
+        pltpu.make_async_copy(slab_hbm.at[r], slab.at[r], slab_sems.at[i])
+        for i, r in enumerate(pieces)
+    ]
+    waiting = coupled + slabs
+
+    def advance(count):
+        for copy in waiting[:count]:
+            copy.start()
+        del waiting[:count]
+
+    advance(WINDOW)
     for copy in small:
         copy.wait()
+    orbital = lax.broadcasted_iota(jnp.int32, chosen.shape[1:], 0)
+    for c in range(index.shape[0]):
+        picked[c : c + 1] = dipole[pl.ds(index[c], 1)]
+        chosen[c] = jnp.where(orbital == index[c], 1.0, 0.0)
     device = lax.axis_index(("chip", "core", "narrow"))
     rows = lax.broadcasted_iota(jnp.int32, (SUB, LANE), 0)
     tiles = []
@@ -140,57 +152,68 @@
             denom[s, :, at : at + LANE] = (shift - offset) - here
     for (s, r), copy in zip(parts, coupled):
         copy.wait()
+        advance(1)
         upper, lower = halves(coupling[s, r])
         high[s, r] = upper
         low[s, r] = lower
-    for copy in slabs:
+    for r, copy in zip(pieces, slabs):
         copy.wait()
-
-
-def fold(response, slab, denom, high, low):
-    modes = response.shape[0] // 2
+        advance(1)
+        slab_t[:, r] = slab[r].T
+
+
+def fold(response, slab_t, high, low, dims):
     upper, lower = halves(response)
     both = jnp.concatenate([upper, lower], 0)
-    singles = stacked(joined(mxu(both, slab[...], LAST)))
-    doubles = []
-    for s in range(high.shape[0]):
-        inner = joined(mxu(both, high[s], LAST)) + mxu(upper, low[s], LAST)
-        re, im = inner[:modes], inner[modes:]
-        den = denom[s]
-        inverse = 1.0 / (den * den + DAMP * DAMP)
-        doubles.append(
-            stacked(
-                jnp.concatenate(
-                    [(re * den + im * DAMP) * inverse, (im * den - re * DAMP) * inverse], 0
-                )
-            )
-        )
+    singles = joined(mxu(both, slab_t, INNER))
+    doubles = [joined(mxu(both, h, dims)) + mxu(upper, l, dims) for h, l in zip(high, low)]
     return singles, doubles
 
 
+def quotient(inner, den):
+    modes = den.shape[0]
+    re, im = inner[:modes], inner[modes:]
+    inverse = 1.0 / (den * den + DAMP * DAMP)
+    return jnp.concatenate(
+        [(re * den + im * DAMP) * inverse, (im * den - re * DAMP) * inverse], 0
+    )
+
+
 def unfold(singles, doubles, amplitudes, high, low, columns):
-    total = mxu(singles, amplitudes[:, columns], INNER)
-    for s, outgoing in enumerate(doubles):
-        total = total + mxu(outgoing, high[s, :, columns], INNER)
+    total = mxu(singles[...], amplitudes[:, columns], INNER)
+    slots, double = doubles.shape[:2]
+    for s in range(slots):
+        total = total + mxu(doubles[s], high[s, :, columns], INNER)
     total = joined(total)
-    for s, outgoing in enumerate(doubles):
-        total = total + mxu(outgoing[: outgoing.shape[0] // 2], low[s, :, columns], INNER)
+    for s in range(slots):
+        total = total + mxu(doubles[s, : double // 2], low[s, :, columns], INNER)
     return total
+
+
+def write_tiles(out, total, modes):
+    tiles = total.shape[1] // LANE
+    for group in range(modes // SUB):
+        for tile in range(tiles):
+            piece, lanes = group * tiles + tile, slice(tile * LANE, (tile + 1) * LANE)
+            out[piece, 0] = total[group * SUB : (group + 1) * SUB, lanes]
+            out[piece, 1] = total[modes + group * SUB : modes + (group + 1) * SUB, lanes]
 
 
 def first_body(
     own,
     other,
+    chosen,
     level,
     denom,
     high,
     low,
-    slab,
+    slab_t,
     amplitudes_hbm,
     rhs,
     start,
+    singles,
+    doubles,
     give,
-    keep,
     amplitudes,
     sems,
 ):
@@ -209,30 +232,40 @@
     cores, block = own.shape
     freqs = modes // cores
     side = lax.axis_index("narrow")
-    for part, at in ((own, side), (other, 1 - side)):
-        columns = pl.ds(pl.multiple_of(at * block, LANE), block)
-        for c in range(cores):
-            rhs[c * freqs : (c + 1) * freqs, columns] = jnp.broadcast_to(
-                part[c : c + 1], (freqs, block)
-            )
+    here = pl.ds(pl.multiple_of(side * block, LANE), block)
+    there = pl.ds(pl.multiple_of((1 - side) * block, LANE), block)
+    for c in range(cores):
+        span = slice(c * freqs, (c + 1) * freqs)
+        mask = jnp.concatenate([chosen[c]] * (block // LANE), 1)
+        theirs = jnp.sum(jnp.where(mask > 0.5, other[...], 0.0), axis=0, keepdims=True)
+        rhs[span, here] = jnp.broadcast_to(own[c : c + 1], (freqs, block))
+        rhs[span, there] = jnp.broadcast_to(theirs, (freqs, block))
     lev = level[...]
     inverse = 1.0 / (lev * lev + DAMP * DAMP)
     start[:modes] = rhs[...] * lev * inverse
     start[modes:] = rhs[...] * DAMP * inverse
-    singles, doubles = fold(start[...], slab, denom, high, low)
+    slots = range(high.shape[0])
+    single, inner = fold(
+        start[...], slab_t[...], [high[s] for s in slots], [low[s] for s in slots], LAST
+    )
+    singles[...] = stacked(single)
+    for s, value in enumerate(inner):
+        doubles[s] = stacked(quotient(value, denom[s]))
     for copy in copies:
         copy.wait()
+    columns = pl.ds(pl.multiple_of((1 - lax.axis_index("core")) * (virt // 2), LANE), virt // 2)
+    write_tiles(give, unfold(singles, doubles, amplitudes, high, low, columns), modes)
+
+
+def first_rest_body(singles, doubles, amplitudes, high, low, keep, high_t, low_t):
+    modes, half = singles.shape[0] // 4, high.shape[2] // 2
     core = lax.axis_index("core")
-    half = virt // 2
-    for out, at in ((give, 1 - core), (keep, core)):
-        columns = pl.ds(pl.multiple_of(at * half, LANE), half)
-        total = unfold(singles, doubles, amplitudes, high, low, columns)
-        for group in range(modes // SUB):
-            for tile in range(half // LANE):
-                piece = group * (half // LANE) + tile
-                lanes = slice(tile * LANE, (tile + 1) * LANE)
-                out[piece, 0] = total[group * SUB : (group + 1) * SUB, lanes]
-                out[piece, 1] = total[modes + group * SUB : modes + (group + 1) * SUB, lanes]
+    columns = pl.ds(pl.multiple_of(core * half, LANE), half)
+    rest = pl.ds(pl.multiple_of((1 - core) * half, LANE), half)
+    write_tiles(keep, unfold(singles, doubles, amplitudes, high, low, columns), modes)
+    for s in range(high.shape[0]):
+        high_t[s] = high[s, :, rest].T
+        low_t[s] = low[s, :, rest].T
 
 
 def add_body(left, right, out):
@@ -264,33 +297,86 @@
         sent[j, 1] = im
 
 
+def read_tiles(part, modes):
+    tiles = part.shape[0] // (modes // SUB)
+    rows = [
+        jnp.concatenate([part[group * tiles + tile, q] for tile in range(tiles)], 1)
+        for q in range(2)
+        for group in range(modes // SUB)
+    ]
+    return jnp.concatenate(rows, 0)
+
+
+def second_own_body(own, slab_t, high, low, response, singles, doubles):
+    modes, half = response.shape[0] // 2, response.shape[1]
+    mine = pl.ds(pl.multiple_of(lax.axis_index("core") * half, LANE), half)
+    slots = range(high.shape[0])
+    response[...] = read_tiles(own, modes)
+    single, inner = fold(
+        response[...],
+        slab_t[mine],
+        [high[s, :, mine] for s in slots],
+        [low[s, :, mine] for s in slots],
+        LAST,
+    )
+    singles[...] = single
+    for s, value in enumerate(inner):
+        doubles[s] = value
+
+
+def write_owned(out, singles, doubles, amplitudes, high, low, at):
+    members, double, half = out.shape
+    owned, quarter = double // 2, half // 2
+    modes = members * owned
+    for side in range(2):
+        columns = pl.ds(pl.multiple_of(side * half + at * quarter, LANE), quarter)
+        total = unfold(singles, doubles, amplitudes, high, low, columns)
+        lanes = slice(side * quarter, (side + 1) * quarter)
+        for j in range(members):
+            out[j, :owned, lanes] = total[j * owned : (j + 1) * owned]
+            out[j, owned:, lanes] = total[modes + j * owned : modes + (j + 1) * owned]
+
+
 def second_body(
-    own, other, level, denom, high, low, slab, amplitudes, response, give, keep
+    mine,
+    other,
+    single_part,
+    double_part,
+    denom,
+    high,
+    low,
+    high_t,
+    low_t,
+    slab_t,
+    amplitudes,
+    response,
+    singles,
+    doubles,
+    give,
 ):
-    modes, virt = level.shape
-    members = own.shape[0]
-    half, quarter = virt // 2, virt // 4
+    half = mine.shape[1]
+    modes = mine.shape[0] // 2
     core = lax.axis_index("core")
-    for part, at in ((own, core), (other, 1 - core)):
-        for group in range(modes // SUB):
-            for tile in range(half // LANE):
-                piece = group * (half // LANE) + tile
-                columns = pl.ds(pl.multiple_of(at * half + tile * LANE, LANE), LANE)
-                response[group * SUB : (group + 1) * SUB, columns] = part[piece, 0]
-                response[modes + group * SUB : modes + (group + 1) * SUB, columns] = part[piece, 1]
-    singles, doubles = fold(response[...], slab, denom, high, low)
-    owned = modes // members
-    for out, at in ((give, 1 - core), (keep, core)):
-        for side in range(2):
-            columns = pl.ds(pl.multiple_of(side * half + at * quarter, LANE), quarter)
-            total = unfold(singles, doubles, amplitudes, high, low, columns)
-            lanes = slice(side * quarter, (side + 1) * quarter)
-            for j in range(members):
-                out[j, :owned, lanes] = total[j * owned : (j + 1) * owned]
-                out[j, owned:, lanes] = total[modes + j * owned : modes + (j + 1) * owned]
-
-
-def second_update_body(got, level, rhs, start, response, sent):
+    columns = pl.ds(pl.multiple_of(core * half, LANE), half)
+    rest = pl.ds(pl.multiple_of((1 - core) * half, LANE), half)
+    theirs = read_tiles(other, modes)
+    response[:, columns] = mine[...]
+    response[:, rest] = theirs
+    slots = range(high_t.shape[0])
+    single, inner = fold(
+        theirs, slab_t[rest], [high_t[s] for s in slots], [low_t[s] for s in slots], INNER
+    )
+    singles[...] = stacked(single_part[...] + single)
+    for s, value in enumerate(inner):
+        doubles[s] = stacked(quotient(double_part[s] + value, denom[s]))
+    write_owned(give, singles, doubles, amplitudes, high, low, 1 - core)
+
+
+def second_rest_body(singles, doubles, amplitudes, high, low, keep):
+    write_owned(keep, singles, doubles, amplitudes, high, low, lax.axis_index("core"))
+
+
+def second_update_body(got, level, rhs, response, sent):
     members, double, width = got.shape
     owned = double // 2
     modes, virt = level.shape
@@ -311,57 +397,66 @@
             rows = jnp.where(within == q, tile[q * owned : (q + 1) * owned], rows)
         return rows
 
-    old_squares = jnp.zeros((owned, 1), F32)
-    new_squares = jnp.zeros((owned, 1), F32)
+    squares = jnp.zeros((owned, 1), F32)
     fresh = []
     for side in range(2):
         columns = pl.ds(pl.multiple_of(side * half + core * quarter, LANE), quarter)
         lanes = slice(side * quarter, (side + 1) * quarter)
         lev, right = own_rows(level, 0, columns), own_rows(rhs, 0, columns)
         re, im = own_rows(response, 0, columns), own_rows(response, modes, columns)
-        step_re = re - own_rows(start, 0, columns)
-        step_im = im - own_rows(start, modes, columns)
-        old_re = lev * step_re + DAMP * step_im
-        old_im = lev * step_im - DAMP * step_re
-        old_squares += jnp.sum(old_re * old_re + old_im * old_im, axis=1, keepdims=True)
         inverse = 1.0 / (lev * lev + DAMP * DAMP)
         res_re = right - (lev * re + DAMP * im + total[:owned, lanes])
         res_im = -(lev * im - DAMP * re + total[owned:, lanes])
-        new_squares += jnp.sum(res_re * res_re + res_im * res_im, axis=1, keepdims=True)
+        squares += jnp.sum(res_re * res_re + res_im * res_im, axis=1, keepdims=True)
         re = re + (res_re * lev - res_im * DAMP) * inverse
         im = im + (res_im * lev + res_re * DAMP) * inverse
-        fresh.append((re, im))
-    squares = jnp.concatenate([old_squares, new_squares], 0)
+        fresh.append(jnp.concatenate([re, im], 0))
+    lane = lax.broadcasted_iota(jnp.int32, (1, LANE), 1)
+    tail = jnp.zeros((1, LANE), F32)
+    for i in range(owned):
+        tail = jnp.where(lane == i, jnp.broadcast_to(squares[i : i + 1], (1, LANE)), tail)
     for j in range(members):
-        re, im = fresh[j % 2]
-        sent[j, :owned, :quarter] = re
-        sent[j, owned:, :quarter] = im
-        sent[j, :, quarter:] = jnp.broadcast_to(squares, (double, LANE))
-
-
-def finish_body(own, other, response, rms):
-    members, double, _ = own.shape
-    owned = double // 2
+        for i in range(double):
+            sent[j, :, i * quarter : (i + 1) * quarter] = fresh[j % 2][i : i + 1]
+        sent[j, :, double * quarter :] = tail
+
+
+def old_squares_body(level, start, response, out):
+    modes = level.shape[0]
+    lev = level[...]
+    re = response[:modes] - start[:modes]
+    im = response[modes:] - start[modes:]
+    res_re = lev * re + DAMP * im
+    res_im = lev * im - DAMP * re
+    out[...] = jnp.sum(res_re * res_re + res_im * res_im, axis=1, keepdims=True)
+
+
+def finish_body(own, other, old, response, rms):
+    members = own.shape[0]
     quarter = response.shape[2] // 2
     sweeps, modes = rms.shape
+    owned = modes // members
+    double = 2 * owned
     core = lax.axis_index("core")
     for part, at in ((own, core), (other, 1 - core)):
         columns = pl.ds(pl.multiple_of(at * quarter, LANE), quarter)
         for j in range(members):
-            for q in range(2):
-                response[q, j * owned : (j + 1) * owned, columns] = part[
-                    j, q * owned : (q + 1) * owned, :quarter
+            for i in range(double):
+                k = j * owned + i % owned
+                response[i // owned, k : k + 1, columns] = part[
+                    j, :, i * quarter : (i + 1) * quarter
                 ]
     row = lax.broadcasted_iota(jnp.int32, (sweeps, LANE), 0)
     lane = lax.broadcasted_iota(jnp.int32, (sweeps, LANE), 1)
     squares = jnp.zeros((sweeps, LANE), F32)
     for j in range(members):
-        both = own[j, :, quarter:] + other[j, :, quarter:]
-        for s in range(sweeps):
-            for i in range(owned):
-                at = s * owned + i
-                value = jnp.broadcast_to(both[at : at + 1], (sweeps, LANE))
-                squares = jnp.where((row == s) & (lane == j * owned + i), value, squares)
+        both = own[j, :, double * quarter :] + other[j, :, double * quarter :]
+        for i in range(owned):
+            k = j * owned + i
+            value = jnp.broadcast_to(both[:, i : i + 1], (sweeps, LANE))
+            squares = jnp.where((row == 1) & (lane == k), value, squares)
+            value = jnp.broadcast_to(old[k : k + 1], (sweeps, LANE))
+            squares = jnp.where((row == 0) & (lane == k), value, squares)
     virt = 4 * quarter
     rms[...] = jnp.sqrt(squares / (2 * virt) + 1e-6)[:, :modes]
 
@@ -390,63 +485,57 @@
     half = virt // 2
     flip_core = [(0, 1), (1, 0)]
     group = ("chip", "narrow")
-    cost = dict(flops=8 * modes * virt * (virt * slots + rows), moved=4 * virt * (virt * slots + rows))
-
-    (picked,) = call(
-        pick_body,
-        "pick",
-        (core_index, dipole),
-        [HBM, HBM],
-        [((cores, block), F32)],
-        scratch=[
-            pltpu.SMEM(core_index.shape, jnp.int32),
-            pltpu.VMEM(dipole.shape, F32),
-            pltpu.SemaphoreType.DMA((2,)),
-        ],
-        moved=cores * block * 4,
-    )
-    across = lax.ppermute(picked, "narrow", flip_core)
+    work = 8 * modes * virt * (virt * slots + rows)
+    size = 2 * virt * (2 * virt * slots + rows)
+
+    across = lax.ppermute(dipole, "narrow", flip_core)
     scalars = (core_index, core_energy, frequency, pair_of_block, pair_shift)
-    level, denom, high, low, slab = call(
+    picked, chosen, level, denom, high, low, slab_t = call(
         prepare_body,
         "prepare",
-        scalars + (virt_energy[None], coupling, integral_slab),
-        [HBM] * 8,
-        [
-            ((modes, virt), F32),
-            ((slots, modes, virt), F32),
-            ((slots, virt, virt), BF16),
-            ((slots, virt, virt), BF16),
-            (integral_slab.shape, BF16),
-        ],
+        scalars + (virt_energy[None], dipole, coupling, integral_slab),
+        [HBM] * 9,
+        [((cores, block), F32), ((cores, dipole.shape[0], LANE), F32)]
+        + [((modes, virt), F32), ((slots, modes, virt), F32)]
+        + [((slots, virt, virt), BF16)] * 2
+        + [((virt, rows), BF16)],
         scratch=[pltpu.SMEM(a.shape, a.dtype) for a in scalars]
         + [
             pltpu.VMEM((1, virt), F32),
+            pltpu.VMEM(dipole.shape, F32),
             pltpu.VMEM(coupling.shape, F32),
-            pltpu.SemaphoreType.DMA((6,)),
+            pltpu.VMEM(integral_slab.shape, BF16),
+            pltpu.SemaphoreType.DMA((7,)),
             pltpu.SemaphoreType.DMA((PARTS * slots,)),
             pltpu.SemaphoreType.DMA((PARTS,)),
         ],
         flops=4 * slots * virt * virt,
-        moved=8 * slots * virt * virt,
+        moved=2 * size,
     )
     piece = (members, 2, SUB, LANE)
-    rhs, start, give, keep, held = call(
+    between = [((4 * modes, rows), BF16), ((slots, 4 * modes, virt), BF16)]
+    rhs, start, singles, doubles, give, held = call(
         first_body,
         "first",
-        (picked, across, level, denom, high, low, slab, amplitudes),
-        [VMEM] * 7 + [HBM],
-        [
-            ((modes, virt), F32),
-            ((2 * modes, virt), F32),
-            (piece, F32),
-            (piece, F32),
-            (amplitudes.shape, BF16),
-        ],
+        (picked, across, chosen, level, denom, high, low, slab_t, amplitudes),
+        [VMEM] * 8 + [HBM],
+        [((modes, virt), F32), ((2 * modes, virt), F32)]
+        + between
+        + [(piece, F32), (amplitudes.shape, BF16)],
         scratch=[pltpu.SemaphoreType.DMA((PARTS,))],
-        **cost,
+        flops=work * 3 // 4,
+        moved=2 * size,
     )
     got = lax.ppermute(give, "core", flip_core)
+    keep, high_t, low_t = call(
+        first_rest_body,
+        "first_rest",
+        (singles, doubles, held, high, low),
+        [VMEM] * 5,
+        [(piece, F32)] + [((slots, half, virt), BF16)] * 2,
+        flops=work // 4,
+        moved=size // 2,
+    )
     (total,) = call(add_body, "add_first", (keep, got), [VMEM] * 2, [(piece, F32)])
     got = lax.all_to_all(total, group, 0, 0, tiled=True)
     (sent,) = call(
@@ -456,33 +545,59 @@
     other = lax.ppermute(got, "core", flip_core)
     owned = modes // members
     piece = (members, 2 * owned, half)
-    response, give, keep = call(
+    mine, single_part, double_part = call(
+        second_own_body,
+        "second_own",
+        (got, slab_t, high, low),
+        [VMEM] * 4,
+        [
+            ((2 * modes, half), F32),
+            ((2 * modes, rows), F32),
+            ((slots, 2 * modes, virt), F32),
+        ],
+        flops=work // 4,
+        moved=size // 2,
+    )
+    response, singles, doubles, give = call(
         second_body,
         "second",
-        (got, other, level, denom, high, low, slab, held),
-        [VMEM] * 8,
-        [((2 * modes, virt), F32), (piece, F32), (piece, F32)],
-        **cost,
+        (mine, other, single_part, double_part, denom, high, low, high_t, low_t, slab_t, held),
+        [VMEM] * 11,
+        [((2 * modes, virt), F32)] + between + [(piece, F32)],
+        flops=work // 2,
+        moved=size,
     )
     got = lax.ppermute(give, "core", flip_core)
+    (keep,) = call(
+        second_rest_body,
+        "second_rest",
+        (singles, doubles, held, high, low),
+        [VMEM] * 5,
+        [(piece, F32)],
+        flops=work // 4,
+        moved=size // 2,
+    )
     (total,) = call(add_body, "add_second", (keep, got), [VMEM] * 2, [(piece, F32)])
     got = lax.all_to_all(total, group, 0, 0, tiled=True)
-    piece = (members, 2 * owned, half // 2 + LANE)
+    piece = (members, 1, owned * virt // 2 + LANE)
     (sent,) = call(
         second_update_body,
         "second_update",
-        (got, level, rhs, start, response),
-        [VMEM] * 5,
+        (got, level, rhs, response),
+        [VMEM] * 4,
         [(piece, F32)],
     )
     got = lax.all_to_all(sent, group, 0, 0, tiled=True)
     other = lax.ppermute(got, "core", flip_core)
+    (old,) = call(
+        old_squares_body, "old_squares", (level, start, response), [VMEM] * 3, [((modes, 1), F32)]
+    )
     return tuple(
         call(
             finish_body,
             "finish",
-            (got, other),
-            [VMEM] * 2,
+            (got, other, old),
+            [VMEM] * 3,
             [((2, modes, block), F32), ((ITERS, modes), F32)],
         )
     )

time: 68.7 us -> 65.8 us (0.958)
  waiting for transfers between devices: 5.18 us -> 2.3 us
    ppermute x2, waiting for transfers between devices: 2.54 us -> 0.9 us  [fast_path(): got = lax.ppermute(give, 'core', flip_core)]
    ppermute x2, waiting for transfers between devices: 2.64 us -> 1.4 us  [fast_path(): other = lax.ppermute(got, 'core', flip_core)]
    pallas_call x9 -> x12, Pallas kernels: 13.8 us -> 13.7 us  [call(): pl.pallas_call(body, out_shape=[jax.ShapeDtypeStruct(s, d) for s, d in ou...]
  transfers between devices with their start and end apart: 5 -> 5, of which waited for: 4 -> 4; matrix products, arithmetic and copies ran while one was open for 0% -> 0% of each run, Pallas kernels for 5% -> 12%
where the time goes in v4:
time: 65.8 us; the launch traced here: 65.5 us
  blocking collectives  45.4 us (69%)
  Pallas kernels  13.7 us (21%)
  starting transfers between devices  3.4 us (5%)
  waiting for transfers between devices  2.3 us (3%)
  between operations  0.71 us (1%)
    all_to_all x2, blocking collectives, fast_path(): got = lax.all_to_all(total, group, 0, 0, tiled=True)  24.2 us
    all_to_all x2, blocking collectives, fast_path(): got = lax.all_to_all(sent, group, 0, 0, tiled=True)  21.2 us
    pallas_call x12, Pallas kernels, call(): pl.pallas_call(body, out_shape=[jax.ShapeDtypeStruct(s, d) for s, d in ou...  13.7 us
    ppermute x1, starting transfers between devices, fast_path(): across = lax.ppermute(dipole, 'narrow', flip_core)  3.03 us
    ppermute x2, waiting for transfers between devices, fast_path(): other = lax.ppermute(got, 'core', flip_core)  1.4 us
  transfers between devices with their start and end apart: 5, of which 4 were waited for; matrix products, arithmetic and copies ran while one was open for 0% of the time, Pallas kernels for 12%

profile of v4, /device:TPU:0, one launch (start us, length us, event | category | flops | bytes accessed | tf_op | source)
XLA Modules:
  0.0 65.5 jit_solution(12424613865827555714)
XLA Ops:
  0.6 3.0 %collective-permute-start = (f32[64,512]{1,0:T(8,128)}, f32[64,512]{1,0:T(8,128)S(1)}, u32[]{:S(2)}, u32[]{:S(2)}) collective-permute-start(f32[64,512]{1,0:T(8,128)} %dipole_hbm.1), channel_id=1, source_target_pairs={{0,1},{1,0},{2,3},{3,2},{4,5},{5,4},{6,7},{7,6},{8,9},{9,8},{10,11... | collective-permute-start | bytes 393224 | tf_op jit(solution)/shard_map/ppermute | solution.py:491
  3.7 4.9 %prepare.1 = (f32[2,512]{1,0:T(2,128)S(1)}, f32[2,64,128]{2,1,0:T(8,128)S(1)}, f32[32,1024]{1,0:T(8,128)S(1)}, f32[1,32,1024]{2,1,0:T(8,128)S(1)}, bf16[1,1024,1...) custom-call(s32[2]{0:T(128)} %index_hbm.1, f32[64]{0:T(128)} %energy_hbm.1, ...), custom_call_target="tpu_custom_call" | custom-call | flops 4194304 | bytes 16777216 | tf_op jit(solution)/shard_map/prepare/pallas_call | solution.py:47
  8.6 0.0 collective-permute-done.other
  8.6 3.6 %first.1 = (f32[32,1024]{1,0:T(8,128)S(1)}, f32[64,1024]{1,0:T(8,128)S(1)}, bf16[128,2048]{1,0:T(8,128)(2,1)S(1)}, bf16[1,128,1024]{2,1,0:T(8,128)(2,1)S(1)}, f3...) custom-call(f32[2,512]{1,0:T(2,128)S(1)} %get-tuple-element.25.own, ...), custom_call_target="tpu_custom_call" | custom-call | flops 603979776 | bytes 16777216 | tf_op jit(solution)/shard_map/first/pallas_call | solution.py:47
  12.2 0.1 collective-permute-start.1
  12.3 0.8 %first_rest.1 = (f32[16,2,8,128]{3,2,1,0:T(8,128)S(1)}, bf16[1,512,1024]{2,1,0:T(8,128)(2,1)S(1)}, bf16[1,512,1024]{2,1,0:T(8,128)(2,1)S(1)}) custom-call(bf16[128,2048]{1,0:T(8,128)(2,1)S(1)} %get-tuple-element.32.singles, bf16[1,128,1024]{2,1,0:T(8,128)(2,1)S(1)} %get-tuple-element.33.doubles, bf16[2048,1024]{1,0:T(8,128)(2,1)S(1)} %get-tuple-element.34.amplitudes, ...), custom_call_target="tpu_custom_call" | custom-call | flops 201326592 | bytes 4194304 | tf_op jit(solution)/shard_map/first_rest/pallas_call | solution.py:47
  13.1 0.5 collective-permute-done.1.right
  13.6 13.5 %all_to_all.20.got = f32[16,2,8,128]{3,2,1,0:T(8,128)S(1)} all-to-all(f32[16,2,8,128]{3,2,1,0:T(8,128)S(1)} %add_first.1), channel_id=1, replica_groups=mesh['chip'=8,'core'=2,'narrow'=2] {'chip','narrow'}, dimensions={0} | all-to-all | bytes 262144 | tf_op jit(solution)/shard_map/all_to_all | solution.py:540
  27.2 10.7 %all_to_all.21.own = f32[16,2,8,128]{3,2,1,0:T(8,128)S(1)} all-to-all(f32[16,2,8,128]{3,2,1,0:T(8,128)S(1)} %first_update.1), channel_id=1, replica_groups=mesh['chip'=8,'core'=2,'narrow'=2] {'chip','narrow'}, dimensions={0} | all-to-all | bytes 262144 | tf_op jit(solution)/shard_map/all_to_all | solution.py:544
  37.9 0.0 collective-permute-start.2
  37.9 1.1 %second_own.1 = (f32[64,512]{1,0:T(8,128)S(1)}, f32[64,2048]{1,0:T(8,128)S(1)}, f32[1,64,1024]{2,1,0:T(8,128)S(1)}) custom-call(f32[16,2,8,128]{3,2,1,0:T(8,128)S(1)} %all_to_all.21.own, bf16[1024,2048]{1,0:T(8,128)(2,1)S(1)} %get-tuple-element.31.slab_t, bf16[1,1024,1024]{2,1,0:T(8,128)(2,1)S(1)} %get-tuple-element.29.high, ...), custom_call_target="tpu_custom_call" | custom-call | flops 201326592 | bytes 4194304 | tf_op jit(solution)/shard_map/second_own/pallas_call | solution.py:47
  39.0 0.3 collective-permute-done.2.other
  39.3 1.5 %second.1 = (f32[64,1024]{1,0:T(8,128)S(1)}, bf16[128,2048]{1,0:T(8,128)(2,1)S(1)}, bf16[1,128,1024]{2,1,0:T(8,128)(2,1)S(1)}, f32[16,4,512]{2,1,0:T(4,128)S(1)}) custom-call(f32[64,512]{1,0:T(8,128)S(1)} %get-tuple-element.39.mine, f32[16,2,8,128]{3,2,1,0:T(8,128)S(1)} %collective-permute-done.2.other, f32[64,2048]{1,0:T(8,128)S(1)} %get-tuple-element.40.single_part, ...), custom_call_target="tpu_custom_call" | custom-call | flops 402653184 | bytes 8388608 | tf_op jit(solution)/shard_map/second/pallas_call | solution.py:47
  40.8 0.3 collective-permute-start.3
  41.1 0.8 %second_rest.1.left = f32[16,4,512]{2,1,0:T(4,128)S(1)} custom-call(bf16[128,2048]{1,0:T(8,128)(2,1)S(1)} %get-tuple-element.44.singles, bf16[1,128,1024]{2,1,0:T(8,128)(2,1)S(1)} %get-tuple-element.45.doubles, bf16[2048,1024]{1,0:T(8,128)(2,1)S(1)} %get-tuple-element.34.amplitudes, bf16[1,1024,1024]{2,1,0:T(8,128)(2,1)S(1)} %get-tuple-element.29.high, ...), custom_call_target="tpu_custom_call" | custom-call | flops 201326592 | bytes 4194304 | tf_op jit(solution)/shard_map/second_rest/pallas_call | solution.py:47
  41.8 0.4 collective-permute-done.3.right
  42.2 10.7 %all_to_all.22.got = f32[16,4,512]{2,1,0:T(4,128)S(1)} all-to-all(f32[16,4,512]{2,1,0:T(4,128)S(1)} %add_second.1), channel_id=1, replica_groups=mesh['chip'=8,'core'=2,'narrow'=2] {'chip','narrow'}, dimensions={0} | all-to-all | bytes 262144 | tf_op jit(solution)/shard_map/all_to_all | solution.py:581
  52.9 0.1 second_update.1
  53.0 10.5 %all_to_all.23.own = f32[16,1,1152]{2,1,0:T(1,128)S(1)} all-to-all(f32[16,1,1152]{2,1,0:T(1,128)S(1)} %second_update.1), channel_id=1, replica_groups=mesh['chip'=8,'core'=2,'narrow'=2] {'chip','narrow'}, dimensions={0} | all-to-all | bytes 147456 | tf_op jit(solution)/shard_map/all_to_all | solution.py:590
  63.5 0.0 collective-permute-start.4
  63.5 0.1 old_squares.1.old
  63.6 1.1 %collective-permute-done.4.other = f32[16,1,1152]{2,1,0:T(1,128)S(1)} collective-permute-done((f32[16,1,1152]{2,1,0:T(1,128)S(1)}, f32[16,1,1152]{2,1,0:T(1,128)S(1)}, u32[]{:S(2)}, u32[]{:S(2)}) %collective-permute-start.4) | collective-permute-done | bytes 73760 | tf_op jit(solution)/shard_map/ppermute | solution.py:591
  64.8 0.8 %finish.1 = (f32[2,32,512]{2,1,0:T(8,128)}, f32[2,32]{1,0:T(2,128)}) custom-call(f32[16,1,1152]{2,1,0:T(1,128)S(1)} %all_to_all.23.own, f32[16,1,1152]{2,1,0:T(1,128)S(1)} %collective-permute-done.4.other, f32[32,1]{1,0:T(8,128)S(1)} %old_squares.1.old), custom_call_target="tpu_custom_call" | custom-call | tf_op jit(solution)/shard_map/finish/pallas_call | solution.py:47
  (3 shorter events, 0.1 us)
Async XLA Ops:
  0.6 8.0 %collective-permute-start = (f32[64,512]{1,0:T(8,128)}, f32[64,512]{1,0:T(8,128)S(1)}, u32[]{:S(2)}, u32[]{:S(2)}) collective-permute-start(f32[64,512]{1,0:T(8,128)} %dipole_hbm.1), channel_id=1, source_target_pairs={{0,1},{1,0},{2,3},{3,2},{4,5},{5,4},{6,7},{7,6},{8,9},{9,8},{10,11... | collective-permute-start | bytes 393224 | tf_op jit(solution)/shard_map/ppermute | solution.py:491
  12.2 1.4 %collective-permute-start.1 = (f32[16,2,8,128]{3,2,1,0:T(8,128)S(1)}, f32[16,2,8,128]{3,2,1,0:T(8,128)S(1)}, u32[]{:S(2)}, u32[]{:S(2)}) collective-permute-start(f32[16,2,8,128]{3,2,1,0:T(8,128)S(1)} %get-tuple-element.36), channel_id=1, source_target_pairs={{0,2},{2,0},{1,3},{3,1},{4,6},{6,4},{5,7},{7,5},{8,10},{10,8},{9,1... | collective-permute-start | bytes 393224 | tf_op jit(solution)/shard_map/ppermute | solution.py:529
  37.9 1.3 %collective-permute-start.2 = (f32[16,2,8,128]{3,2,1,0:T(8,128)S(1)}, f32[16,2,8,128]{3,2,1,0:T(8,128)S(1)}, u32[]{:S(2)}, u32[]{:S(2)}) collective-permute-start(f32[16,2,8,128]{3,2,1,0:T(8,128)S(1)} %all_to_all.21.own), channel_id=1, source_target_pairs={{0,2},{2,0},{1,3},{3,1},{4,6},{6,4},{5,7},{7,5},{8,10},{10,8},{9,1... | collective-permute-start | bytes 393224 | tf_op jit(solution)/shard_map/ppermute | solution.py:545
  40.8 1.4 %collective-permute-start.3 = (f32[16,4,512]{2,1,0:T(4,128)S(1)}, f32[16,4,512]{2,1,0:T(4,128)S(1)}, u32[]{:S(2)}, u32[]{:S(2)}) collective-permute-start(f32[16,4,512]{2,1,0:T(4,128)S(1)} %get-tuple-element.46), channel_id=1, source_target_pairs={{0,2},{2,0},{1,3},{3,1},{4,6},{6,4},{5,7},{7,5},{8,10},{10,8},{9,1... | collective-permute-start | bytes 393224 | tf_op jit(solution)/shard_map/ppermute | solution.py:570
  63.5 1.3 %collective-permute-start.4 = (f32[16,1,1152]{2,1,0:T(1,128)S(1)}, f32[16,1,1152]{2,1,0:T(1,128)S(1)}, u32[]{:S(2)}, u32[]{:S(2)}) collective-permute-start(f32[16,1,1152]{2,1,0:T(1,128)S(1)} %all_to_all.23.own), channel_id=1, source_target_pairs={{0,2},{2,0},{1,3},{3,1},{4,6},{6,4},{5,7},{7,5},{8,10},{10,8},{9,1... | collective-permute-start | bytes 221192 | tf_op jit(solution)/shard_map/ppermute | solution.py:591

commit v5 on v4

--- a/solution.py
+++ b/solution.py
@@ -17,8 +17,8 @@
 VMEM = pl.BlockSpec(memory_space=pltpu.VMEM)
 SMEM = pl.BlockSpec(memory_space=pltpu.SMEM)
 HBM = pl.BlockSpec(memory_space=pltpu.HBM)
-PARTS = 8
-WINDOW = 11
+PARTS = 4
+WINDOW = 6
 
 
 def mxu(left, right, dims):
@@ -372,8 +372,17 @@
     write_owned(give, singles, doubles, amplitudes, high, low, 1 - core)
 
 
-def second_rest_body(singles, doubles, amplitudes, high, low, keep):
+def second_rest_body(
+    singles, doubles, amplitudes, high, low, level, start, response, keep, squares
+):
     write_owned(keep, singles, doubles, amplitudes, high, low, lax.axis_index("core"))
+    modes = level.shape[0]
+    lev = level[...]
+    re = response[:modes] - start[:modes]
+    im = response[modes:] - start[modes:]
+    res_re = lev * re + DAMP * im
+    res_im = lev * im - DAMP * re
+    squares[...] = jnp.sum(res_re * res_re + res_im * res_im, axis=1, keepdims=True)
 
 
 def second_update_body(got, level, rhs, response, sent):
@@ -415,48 +424,39 @@
     tail = jnp.zeros((1, LANE), F32)
     for i in range(owned):
         tail = jnp.where(lane == i, jnp.broadcast_to(squares[i : i + 1], (1, LANE)), tail)
-    for j in range(members):
+    for j in range(sent.shape[0]):
         for i in range(double):
             sent[j, :, i * quarter : (i + 1) * quarter] = fresh[j % 2][i : i + 1]
         sent[j, :, double * quarter :] = tail
 
 
-def old_squares_body(level, start, response, out):
-    modes = level.shape[0]
-    lev = level[...]
-    re = response[:modes] - start[:modes]
-    im = response[modes:] - start[modes:]
-    res_re = lev * re + DAMP * im
-    res_im = lev * im - DAMP * re
-    out[...] = jnp.sum(res_re * res_re + res_im * res_im, axis=1, keepdims=True)
-
-
-def finish_body(own, other, old, response, rms):
-    members = own.shape[0]
+def finish_body(got, old, response, rms):
+    devices = got.shape[0]
     quarter = response.shape[2] // 2
     sweeps, modes = rms.shape
-    owned = modes // members
+    owned = 2 * modes // devices
     double = 2 * owned
-    core = lax.axis_index("core")
-    for part, at in ((own, core), (other, 1 - core)):
-        columns = pl.ds(pl.multiple_of(at * quarter, LANE), quarter)
-        for j in range(members):
-            for i in range(double):
-                k = j * owned + i % owned
-                response[i // owned, k : k + 1, columns] = part[
-                    j, :, i * quarter : (i + 1) * quarter
-                ]
     row = lax.broadcasted_iota(jnp.int32, (sweeps, LANE), 0)
     lane = lax.broadcasted_iota(jnp.int32, (sweeps, LANE), 1)
     squares = jnp.zeros((sweeps, LANE), F32)
-    for j in range(members):
-        both = own[j, :, double * quarter :] + other[j, :, double * quarter :]
-        for i in range(owned):
-            k = j * owned + i
-            value = jnp.broadcast_to(both[:, i : i + 1], (sweeps, LANE))
-            squares = jnp.where((row == 1) & (lane == k), value, squares)
-            value = jnp.broadcast_to(old[k : k + 1], (sweeps, LANE))
-            squares = jnp.where((row == 0) & (lane == k), value, squares)
+    for chip in range(devices // 4):
+        for side in range(2):
+            sources = [(chip * 2 + core) * 2 + side for core in range(2)]
+            first = (chip * 2 + side) * owned
+            for core, j in enumerate(sources):
+                columns = slice(core * quarter, (core + 1) * quarter)
+                for i in range(double):
+                    k = first + i % owned
+                    response[i // owned, k : k + 1, columns] = got[
+                        j, :, i * quarter : (i + 1) * quarter
+                    ]
+            both = sum(got[j, :, double * quarter :] for j in sources)
+            for i in range(owned):
+                k = first + i
+                value = jnp.broadcast_to(both[:, i : i + 1], (sweeps, LANE))
+                squares = jnp.where((row == 1) & (lane == k), value, squares)
+                value = jnp.broadcast_to(old[k : k + 1], (sweeps, LANE))
+                squares = jnp.where((row == 0) & (lane == k), value, squares)
     virt = 4 * quarter
     rms[...] = jnp.sqrt(squares / (2 * virt) + 1e-6)[:, :modes]
 
@@ -568,18 +568,18 @@
         moved=size,
     )
     got = lax.ppermute(give, "core", flip_core)
-    (keep,) = call(
+    keep, old = call(
         second_rest_body,
         "second_rest",
-        (singles, doubles, held, high, low),
-        [VMEM] * 5,
-        [(piece, F32)],
+        (singles, doubles, held, high, low, level, start, response),
+        [VMEM] * 8,
+        [(piece, F32), ((modes, 1), F32)],
         flops=work // 4,
         moved=size // 2,
     )
     (total,) = call(add_body, "add_second", (keep, got), [VMEM] * 2, [(piece, F32)])
     got = lax.all_to_all(total, group, 0, 0, tiled=True)
-    piece = (members, 1, owned * virt // 2 + LANE)
+    piece = (2 * members, 1, owned * virt // 2 + LANE)
     (sent,) = call(
         second_update_body,
         "second_update",
@@ -587,17 +587,13 @@
         [VMEM] * 4,
         [(piece, F32)],
     )
-    got = lax.all_to_all(sent, group, 0, 0, tiled=True)
-    other = lax.ppermute(got, "core", flip_core)
-    (old,) = call(
-        old_squares_body, "old_squares", (level, start, response), [VMEM] * 3, [((modes, 1), F32)]
-    )
+    got = lax.all_to_all(sent, ("chip", "core", "narrow"), 0, 0, tiled=True)
     return tuple(
         call(
             finish_body,
             "finish",
-            (got, other, old),
-            [VMEM] * 3,
+            (got, old),
+            [VMEM] * 2,
             [((2, modes, block), F32), ((ITERS, modes), F32)],
         )
     )

time: 65.8 us -> 64.7 us (0.983)
  waiting for transfers between devices: 2.3 us -> 1.11 us
  blocking collectives: 45.4 us -> 46.1 us
    all_to_all x0 -> x1, blocking collectives: none -> 10.7 us  [fast_path(): got = lax.all_to_all(sent, ('chip', 'core', 'narrow'), 0, 0, tiled=True)]
    all_to_all x2 -> x1, blocking collectives: 21.2 us -> 10.7 us  [fast_path(): got = lax.all_to_all(sent, group, 0, 0, tiled=True)]
    ppermute x2 -> x1, waiting for transfers between devices: 1.4 us -> 0.27 us  [fast_path(): other = lax.ppermute(got, 'core', flip_core)]
    pallas_call x12 -> x11, Pallas kernels: 13.7 us -> 13.1 us  [call(): pl.pallas_call(body, out_shape=[jax.ShapeDtypeStruct(s, d) for s, d in ou...]
  transfers between devices with their start and end apart: 5 -> 4, of which waited for: 4 -> 3; matrix products, arithmetic and copies ran while one was open for 0% -> 0% of each run, Pallas kernels for 12% -> 11%
where the time goes in v5:
time: 64.7 us; the launch traced here: 64.5 us
  blocking collectives  46.1 us (71%)
  Pallas kernels  13.1 us (20%)
  starting transfers between devices  3.4 us (5%)
  waiting for transfers between devices  1.11 us (2%)
  between operations  0.72 us (1%)
    all_to_all x2, blocking collectives, fast_path(): got = lax.all_to_all(total, group, 0, 0, tiled=True)  24.7 us
    pallas_call x11, Pallas kernels, call(): pl.pallas_call(body, out_shape=[jax.ShapeDtypeStruct(s, d) for s, d in ou...  13.1 us
    all_to_all x1, blocking collectives, fast_path(): got = lax.all_to_all(sent, ('chip', 'core', 'narrow'), 0, 0, tiled=True)  10.7 us
    all_to_all x1, blocking collectives, fast_path(): got = lax.all_to_all(sent, group, 0, 0, tiled=True)  10.7 us
    ppermute x1, starting transfers between devices, fast_path(): across = lax.ppermute(dipole, 'narrow', flip_core)  3.03 us
  transfers between devices with their start and end apart: 4, of which 3 were waited for; matrix products, arithmetic and copies ran while one was open for 0% of the time, Pallas kernels for 11%

profile of v5, /device:TPU:0, one launch (start us, length us, event | category | flops | bytes accessed | tf_op | source)
XLA Modules:
  0.0 64.5 jit_solution(15208860548706959245)
XLA Ops:
  0.6 3.0 %collective-permute-start = (f32[64,512]{1,0:T(8,128)}, f32[64,512]{1,0:T(8,128)S(1)}, u32[]{:S(2)}, u32[]{:S(2)}) collective-permute-start(f32[64,512]{1,0:T(8,128)} %dipole_hbm.1), channel_id=1, source_target_pairs={{0,1},{1,0},{2,3},{3,2},{4,5},{5,4},{6,7},{7,6},{8,9},{9,8},{10,11... | collective-permute-start | bytes 393224 | tf_op jit(solution)/shard_map/ppermute | solution.py:491
  3.7 4.4 %prepare.1 = (f32[2,512]{1,0:T(2,128)S(1)}, f32[2,64,128]{2,1,0:T(8,128)S(1)}, f32[32,1024]{1,0:T(8,128)S(1)}, f32[1,32,1024]{2,1,0:T(8,128)S(1)}, bf16[1,1024,1...) custom-call(s32[2]{0:T(128)} %index_hbm.1, f32[64]{0:T(128)} %energy_hbm.1, ...), custom_call_target="tpu_custom_call" | custom-call | flops 4194304 | bytes 16777216 | tf_op jit(solution)/shard_map/prepare/pallas_call | solution.py:47
  8.1 0.0 collective-permute-done.other
  8.1 3.6 %first.1 = (f32[32,1024]{1,0:T(8,128)S(1)}, f32[64,1024]{1,0:T(8,128)S(1)}, bf16[128,2048]{1,0:T(8,128)(2,1)S(1)}, bf16[1,128,1024]{2,1,0:T(8,128)(2,1)S(1)}, f3...) custom-call(f32[2,512]{1,0:T(2,128)S(1)} %get-tuple-element.27.own, ...), custom_call_target="tpu_custom_call" | custom-call | flops 603979776 | bytes 16777216 | tf_op jit(solution)/shard_map/first/pallas_call | solution.py:47
  11.7 0.1 collective-permute-start.1
  11.8 0.8 %first_rest.1 = (f32[16,2,8,128]{3,2,1,0:T(8,128)S(1)}, bf16[1,512,1024]{2,1,0:T(8,128)(2,1)S(1)}, bf16[1,512,1024]{2,1,0:T(8,128)(2,1)S(1)}) custom-call(bf16[128,2048]{1,0:T(8,128)(2,1)S(1)} %get-tuple-element.34.singles, bf16[1,128,1024]{2,1,0:T(8,128)(2,1)S(1)} %get-tuple-element.35.doubles, bf16[2048,1024]{1,0:T(8,128)(2,1)S(1)} %get-tuple-element.36.amplitudes, ...), custom_call_target="tpu_custom_call" | custom-call | flops 201326592 | bytes 4194304 | tf_op jit(solution)/shard_map/first_rest/pallas_call | solution.py:47
  12.6 0.5 collective-permute-done.1.right
  13.1 14.0 %all_to_all.20.got = f32[16,2,8,128]{3,2,1,0:T(8,128)S(1)} all-to-all(f32[16,2,8,128]{3,2,1,0:T(8,128)S(1)} %add_first.1), channel_id=1, replica_groups=mesh['chip'=8,'core'=2,'narrow'=2] {'chip','narrow'}, dimensions={0} | all-to-all | bytes 262144 | tf_op jit(solution)/shard_map/all_to_all | solution.py:540
  27.1 10.7 %all_to_all.21.own = f32[16,2,8,128]{3,2,1,0:T(8,128)S(1)} all-to-all(f32[16,2,8,128]{3,2,1,0:T(8,128)S(1)} %first_update.1), channel_id=1, replica_groups=mesh['chip'=8,'core'=2,'narrow'=2] {'chip','narrow'}, dimensions={0} | all-to-all | bytes 262144 | tf_op jit(solution)/shard_map/all_to_all | solution.py:544
  37.9 0.0 collective-permute-start.2
  37.9 1.1 %second_own.1 = (f32[64,512]{1,0:T(8,128)S(1)}, f32[64,2048]{1,0:T(8,128)S(1)}, f32[1,64,1024]{2,1,0:T(8,128)S(1)}) custom-call(f32[16,2,8,128]{3,2,1,0:T(8,128)S(1)} %all_to_all.21.own, bf16[1024,2048]{1,0:T(8,128)(2,1)S(1)} %get-tuple-element.33.slab_t, bf16[1,1024,1024]{2,1,0:T(8,128)(2,1)S(1)} %get-tuple-element.31.high, ...), custom_call_target="tpu_custom_call" | custom-call | flops 201326592 | bytes 4194304 | tf_op jit(solution)/shard_map/second_own/pallas_call | solution.py:47
  38.9 0.3 collective-permute-done.2.other
  39.2 1.5 %second.1 = (f32[64,1024]{1,0:T(8,128)S(1)}, bf16[128,2048]{1,0:T(8,128)(2,1)S(1)}, bf16[1,128,1024]{2,1,0:T(8,128)(2,1)S(1)}, f32[16,4,512]{2,1,0:T(4,128)S(1)}) custom-call(f32[64,512]{1,0:T(8,128)S(1)} %get-tuple-element.41.mine, f32[16,2,8,128]{3,2,1,0:T(8,128)S(1)} %collective-permute-done.2.other, f32[64,2048]{1,0:T(8,128)S(1)} %get-tuple-element.42.single_part, ...), custom_call_target="tpu_custom_call" | custom-call | flops 402653184 | bytes 8388608 | tf_op jit(solution)/shard_map/second/pallas_call | solution.py:47
  40.7 0.3 collective-permute-start.3
  41.0 0.8 %second_rest.1 = (f32[16,4,512]{2,1,0:T(4,128)S(1)}, f32[32,1]{1,0:T(8,128)S(1)}) custom-call(bf16[128,2048]{1,0:T(8,128)(2,1)S(1)} %get-tuple-element.46.singles, bf16[1,128,1024]{2,1,0:T(8,128)(2,1)S(1)} %get-tuple-element.47.doubles, bf16[2048,1024]{1,0:T(8,128)(2,1)S(1)} %get-tuple-element.36.amplitudes, ...), custom_call_target="tpu_custom_call" | custom-call | flops 201326592 | bytes 4194304 | tf_op jit(solution)/shard_map/second_rest/pallas_call | solution.py:47
  41.8 0.3 collective-permute-done.3.right
  42.1 10.7 %all_to_all.22.got = f32[16,4,512]{2,1,0:T(4,128)S(1)} all-to-all(f32[16,4,512]{2,1,0:T(4,128)S(1)} %add_second.1), channel_id=1, replica_groups=mesh['chip'=8,'core'=2,'narrow'=2] {'chip','narrow'}, dimensions={0} | all-to-all | bytes 262144 | tf_op jit(solution)/shard_map/all_to_all | solution.py:581
  52.8 0.1 second_update.1
  53.0 10.7 %all_to_all.23.got = f32[32,1,1152]{2,1,0:T(1,128)S(1)} all-to-all(f32[32,1,1152]{2,1,0:T(1,128)S(1)} %second_update.1), channel_id=1, replica_groups=mesh['chip'=8,'core'=2,'narrow'=2] {'chip','core','narrow'}, dimensions={0} | all-to-all | bytes 294912 | tf_op jit(solution)/shard_map/all_to_all | solution.py:590
  63.7 0.8 %finish.1 = (f32[2,32,512]{2,1,0:T(8,128)}, f32[2,32]{1,0:T(2,128)}) custom-call(f32[32,1,1152]{2,1,0:T(1,128)S(1)} %all_to_all.23.got, f32[32,1]{1,0:T(8,128)S(1)} %get-tuple-element.51.old), custom_call_target="tpu_custom_call" | custom-call | tf_op jit(solution)/shard_map/finish/pallas_call | solution.py:47
  (3 shorter events, 0.1 us)
Async XLA Ops:
  0.6 7.5 %collective-permute-start = (f32[64,512]{1,0:T(8,128)}, f32[64,512]{1,0:T(8,128)S(1)}, u32[]{:S(2)}, u32[]{:S(2)}) collective-permute-start(f32[64,512]{1,0:T(8,128)} %dipole_hbm.1), channel_id=1, source_target_pairs={{0,1},{1,0},{2,3},{3,2},{4,5},{5,4},{6,7},{7,6},{8,9},{9,8},{10,11... | collective-permute-start | bytes 393224 | tf_op jit(solution)/shard_map/ppermute | solution.py:491
  11.7 1.4 %collective-permute-start.1 = (f32[16,2,8,128]{3,2,1,0:T(8,128)S(1)}, f32[16,2,8,128]{3,2,1,0:T(8,128)S(1)}, u32[]{:S(2)}, u32[]{:S(2)}) collective-permute-start(f32[16,2,8,128]{3,2,1,0:T(8,128)S(1)} %get-tuple-element.38), channel_id=1, source_target_pairs={{0,2},{2,0},{1,3},{3,1},{4,6},{6,4},{5,7},{7,5},{8,10},{10,8},{9,1... | collective-permute-start | bytes 393224 | tf_op jit(solution)/shard_map/ppermute | solution.py:529
  37.9 1.3 %collective-permute-start.2 = (f32[16,2,8,128]{3,2,1,0:T(8,128)S(1)}, f32[16,2,8,128]{3,2,1,0:T(8,128)S(1)}, u32[]{:S(2)}, u32[]{:S(2)}) collective-permute-start(f32[16,2,8,128]{3,2,1,0:T(8,128)S(1)} %all_to_all.21.own), channel_id=1, source_target_pairs={{0,2},{2,0},{1,3},{3,1},{4,6},{6,4},{5,7},{7,5},{8,10},{10,8},{9,1... | collective-permute-start | bytes 393224 | tf_op jit(solution)/shard_map/ppermute | solution.py:545
  40.7 1.4 %collective-permute-start.3 = (f32[16,4,512]{2,1,0:T(4,128)S(1)}, f32[16,4,512]{2,1,0:T(4,128)S(1)}, u32[]{:S(2)}, u32[]{:S(2)}) collective-permute-start(f32[16,4,512]{2,1,0:T(4,128)S(1)} %get-tuple-element.50), channel_id=1, source_target_pairs={{0,2},{2,0},{1,3},{3,1},{4,6},{6,4},{5,7},{7,5},{8,10},{10,8},{9,1... | collective-permute-start | bytes 393224 | tf_op jit(solution)/shard_map/ppermute | solution.py:570

commit v6 on v5

--- a/solution.py
+++ b/solution.py
@@ -208,26 +208,13 @@
     high,
     low,
     slab_t,
-    amplitudes_hbm,
+    amplitudes,
     rhs,
     start,
     singles,
     doubles,
     give,
-    amplitudes,
-    sems,
 ):
-    step = amplitudes.shape[0] // PARTS
-    copies = start_all(
-        [
-            (
-                amplitudes_hbm.at[i * step : (i + 1) * step],
-                amplitudes.at[i * step : (i + 1) * step],
-            )
-            for i in range(PARTS)
-        ],
-        sems,
-    )
     modes, virt = level.shape
     cores, block = own.shape
     freqs = modes // cores
@@ -251,8 +238,6 @@
     singles[...] = stacked(single)
     for s, value in enumerate(inner):
         doubles[s] = stacked(quotient(value, denom[s]))
-    for copy in copies:
-        copy.wait()
     columns = pl.ds(pl.multiple_of((1 - lax.axis_index("core")) * (virt // 2), LANE), virt // 2)
     write_tiles(give, unfold(singles, doubles, amplitudes, high, low, columns), modes)
 
@@ -514,15 +499,14 @@
     )
     piece = (members, 2, SUB, LANE)
     between = [((4 * modes, rows), BF16), ((slots, 4 * modes, virt), BF16)]
-    rhs, start, singles, doubles, give, held = call(
+    rhs, start, singles, doubles, give = call(
         first_body,
         "first",
         (picked, across, chosen, level, denom, high, low, slab_t, amplitudes),
-        [VMEM] * 8 + [HBM],
+        [VMEM] * 9,
         [((modes, virt), F32), ((2 * modes, virt), F32)]
         + between
-        + [(piece, F32), (amplitudes.shape, BF16)],
-        scratch=[pltpu.SemaphoreType.DMA((PARTS,))],
+        + [(piece, F32)],
         flops=work * 3 // 4,
         moved=2 * size,
     )
@@ -530,7 +514,7 @@
     keep, high_t, low_t = call(
         first_rest_body,
         "first_rest",
-        (singles, doubles, held, high, low),
+        (singles, doubles, amplitudes, high, low),
         [VMEM] * 5,
         [(piece, F32)] + [((slots, half, virt), BF16)] * 2,
         flops=work // 4,
@@ -561,7 +545,7 @@
     response, singles, doubles, give = call(
         second_body,
         "second",
-        (mine, other, single_part, double_part, denom, high, low, high_t, low_t, slab_t, held),
+        (mine, other, single_part, double_part, denom, high, low, high_t, low_t, slab_t, amplitudes),
         [VMEM] * 11,
         [((2 * modes, virt), F32)] + between + [(piece, F32)],
         flops=work // 2,
@@ -571,7 +555,7 @@
     keep, old = call(
         second_rest_body,
         "second_rest",
-        (singles, doubles, held, high, low, level, start, response),
+        (singles, doubles, amplitudes, high, low, level, start, response),
         [VMEM] * 8,
         [(piece, F32), ((modes, 1), F32)],
         flops=work // 4,

time: 64.7 us -> 63.9 us (0.988)
    pallas_call x11, Pallas kernels: 13.1 us -> 12.5 us  [call(): pl.pallas_call(body, out_shape=[jax.ShapeDtypeStruct(s, d) for s, d in ou...]
where the time goes in v6:
time: 63.9 us; the launch traced here: 63.7 us
  blocking collectives  45.9 us (72%)
  Pallas kernels  12.5 us (20%)
  starting transfers between devices  3.41 us (5%)
  waiting for transfers between devices  1.09 us (2%)
  between operations  0.72 us (1%)
    all_to_all x2, blocking collectives, fast_path(): got = lax.all_to_all(total, group, 0, 0, tiled=True)  24.4 us
    pallas_call x11, Pallas kernels, call(): pl.pallas_call(body, out_shape=[jax.ShapeDtypeStruct(s, d) for s, d in ou...  12.5 us
    all_to_all x1, blocking collectives, fast_path(): got = lax.all_to_all(sent, ('chip', 'core', 'narrow'), 0, 0, tiled=True)  10.7 us
    all_to_all x1, blocking collectives, fast_path(): got = lax.all_to_all(sent, group, 0, 0, tiled=True)  10.7 us
    ppermute x1, starting transfers between devices, fast_path(): across = lax.ppermute(dipole, 'narrow', flip_core)  3.03 us
  transfers between devices with their start and end apart: 4, of which 3 were waited for; matrix products, arithmetic and copies ran while one was open for 0% of the time, Pallas kernels for 11%

profile of v6, /device:TPU:0, one launch (start us, length us, event | category | flops | bytes accessed | tf_op | source)
XLA Modules:
  0.0 63.7 jit_solution(13122904927260749896)
XLA Ops:
  0.6 3.0 %collective-permute-start = (f32[64,512]{1,0:T(8,128)}, f32[64,512]{1,0:T(8,128)S(1)}, u32[]{:S(2)}, u32[]{:S(2)}) collective-permute-start(f32[64,512]{1,0:T(8,128)} %dipole_hbm.1), channel_id=1, source_target_pairs={{0,1},{1,0},{2,3},{3,2},{4,5},{5,4},{6,7},{7,6},{8,9},{9,8},{10,11... | collective-permute-start | bytes 393224 | tf_op jit(solution)/shard_map/ppermute | solution.py:476
  3.7 0.0 copy-start
  3.7 4.6 %prepare.1 = (f32[2,512]{1,0:T(2,128)S(1)}, f32[2,64,128]{2,1,0:T(8,128)S(1)}, f32[32,1024]{1,0:T(8,128)S(1)}, f32[1,32,1024]{2,1,0:T(8,128)S(1)}, bf16[1,1024,1...) custom-call(s32[2]{0:T(128)} %index_hbm.1, f32[64]{0:T(128)} %energy_hbm.1, ...), custom_call_target="tpu_custom_call" | custom-call | flops 4194304 | bytes 16777216 | tf_op jit(solution)/shard_map/prepare/pallas_call | solution.py:47
  8.3 0.0 collective-permute-done.other
  8.3 0.1 copy-done
  8.4 2.7 %first.1 = (f32[32,1024]{1,0:T(8,128)S(1)}, f32[64,1024]{1,0:T(8,128)S(1)}, bf16[128,2048]{1,0:T(8,128)(2,1)S(1)}, bf16[1,128,1024]{2,1,0:T(8,128)(2,1)S(1)}, f32[16,2,8,128]{3,2,1,0:T(8,128)S(1)}) custom-call(f32[2,512]{1,0:T(2,128)S(1)} %get-tuple-element.26.own, f32[64,512]{1,0:T(8,128)S(1)} %collective-permute-done.other, ...), custom_call_target="tpu_custom_call" | custom-call | flops 603979776 | bytes 16777216 | tf_op jit(solution)/shard_map/first/pallas_call | solution.py:47
  11.2 0.1 collective-permute-start.1
  11.2 0.8 %first_rest.1 = (f32[16,2,8,128]{3,2,1,0:T(8,128)S(1)}, bf16[1,512,1024]{2,1,0:T(8,128)(2,1)S(1)}, bf16[1,512,1024]{2,1,0:T(8,128)(2,1)S(1)}) custom-call(bf16[128,2048]{1,0:T(8,128)(2,1)S(1)} %get-tuple-element.33.singles, bf16[1,128,1024]{2,1,0:T(8,128)(2,1)S(1)} %get-tuple-element.34.doubles, bf16[2048,1024]{1,0:T(8,128)(2,1)S(1)} %copy-done, ...), custom_call_target="tpu_custom_call" | custom-call | flops 201326592 | bytes 4194304 | tf_op jit(solution)/shard_map/first_rest/pallas_call | solution.py:47
  12.0 0.5 collective-permute-done.1.right
  12.6 13.7 %all_to_all.20.got = f32[16,2,8,128]{3,2,1,0:T(8,128)S(1)} all-to-all(f32[16,2,8,128]{3,2,1,0:T(8,128)S(1)} %add_first.1), channel_id=1, replica_groups=mesh['chip'=8,'core'=2,'narrow'=2] {'chip','narrow'}, dimensions={0} | all-to-all | bytes 262144 | tf_op jit(solution)/shard_map/all_to_all | solution.py:524
  26.3 10.7 %all_to_all.21.own = f32[16,2,8,128]{3,2,1,0:T(8,128)S(1)} all-to-all(f32[16,2,8,128]{3,2,1,0:T(8,128)S(1)} %first_update.1), channel_id=1, replica_groups=mesh['chip'=8,'core'=2,'narrow'=2] {'chip','narrow'}, dimensions={0} | all-to-all | bytes 262144 | tf_op jit(solution)/shard_map/all_to_all | solution.py:528
  37.0 0.0 collective-permute-start.2
  37.0 1.1 %second_own.1 = (f32[64,512]{1,0:T(8,128)S(1)}, f32[64,2048]{1,0:T(8,128)S(1)}, f32[1,64,1024]{2,1,0:T(8,128)S(1)}) custom-call(f32[16,2,8,128]{3,2,1,0:T(8,128)S(1)} %all_to_all.21.own, bf16[1024,2048]{1,0:T(8,128)(2,1)S(1)} %get-tuple-element.32.slab_t, bf16[1,1024,1024]{2,1,0:T(8,128)(2,1)S(1)} %get-tuple-element.30.high, ...), custom_call_target="tpu_custom_call" | custom-call | flops 201326592 | bytes 4194304 | tf_op jit(solution)/shard_map/second_own/pallas_call | solution.py:47
  38.1 0.3 collective-permute-done.2.other
  38.4 1.5 %second.1 = (f32[64,1024]{1,0:T(8,128)S(1)}, bf16[128,2048]{1,0:T(8,128)(2,1)S(1)}, bf16[1,128,1024]{2,1,0:T(8,128)(2,1)S(1)}, f32[16,4,512]{2,1,0:T(4,128)S(1)}) custom-call(f32[64,512]{1,0:T(8,128)S(1)} %get-tuple-element.39.mine, f32[16,2,8,128]{3,2,1,0:T(8,128)S(1)} %collective-permute-done.2.other, f32[64,2048]{1,0:T(8,128)S(1)} %get-tuple-element.40.single_part, ...), custom_call_target="tpu_custom_call" | custom-call | flops 402653184 | bytes 8388608 | tf_op jit(solution)/shard_map/second/pallas_call | solution.py:47
  39.9 0.3 collective-permute-start.3
  40.2 0.8 %second_rest.1 = (f32[16,4,512]{2,1,0:T(4,128)S(1)}, f32[32,1]{1,0:T(8,128)S(1)}) custom-call(bf16[128,2048]{1,0:T(8,128)(2,1)S(1)} %get-tuple-element.44.singles, bf16[1,128,1024]{2,1,0:T(8,128)(2,1)S(1)} %get-tuple-element.45.doubles, bf16[2048,1024]{1,0:T(8,128)(2,1)S(1)} %copy-done, bf16[1,1024,1024]{2,1,0:T(8,128)(2,1)S(1)} %get-tuple-element.30.high, ...), custom_call_target="tpu_custom_call" | custom-call | flops 201326592 | bytes 4194304 | tf_op jit(solution)/shard_map/second_rest/pallas_call | solution.py:47
  41.0 0.3 collective-permute-done.3.right
  41.3 10.7 %all_to_all.22.got = f32[16,4,512]{2,1,0:T(4,128)S(1)} all-to-all(f32[16,4,512]{2,1,0:T(4,128)S(1)} %add_second.1), channel_id=1, replica_groups=mesh['chip'=8,'core'=2,'narrow'=2] {'chip','narrow'}, dimensions={0} | all-to-all | bytes 262144 | tf_op jit(solution)/shard_map/all_to_all | solution.py:565
  52.0 0.1 second_update.1
  52.2 10.7 %all_to_all.23.got = f32[32,1,1152]{2,1,0:T(1,128)S(1)} all-to-all(f32[32,1,1152]{2,1,0:T(1,128)S(1)} %second_update.1), channel_id=1, replica_groups=mesh['chip'=8,'core'=2,'narrow'=2] {'chip','core','narrow'}, dimensions={0} | all-to-all | bytes 294912 | tf_op jit(solution)/shard_map/all_to_all | solution.py:574
  62.9 0.8 %finish.1 = (f32[2,32,512]{2,1,0:T(8,128)}, f32[2,32]{1,0:T(2,128)}) custom-call(f32[32,1,1152]{2,1,0:T(1,128)S(1)} %all_to_all.23.got, f32[32,1]{1,0:T(8,128)S(1)} %get-tuple-element.49.old), custom_call_target="tpu_custom_call" | custom-call | tf_op jit(solution)/shard_map/finish/pallas_call | solution.py:47
  (3 shorter events, 0.1 us)
Async XLA Ops:
  0.6 7.6 %collective-permute-start = (f32[64,512]{1,0:T(8,128)}, f32[64,512]{1,0:T(8,128)S(1)}, u32[]{:S(2)}, u32[]{:S(2)}) collective-permute-start(f32[64,512]{1,0:T(8,128)} %dipole_hbm.1), channel_id=1, source_target_pairs={{0,1},{1,0},{2,3},{3,2},{4,5},{5,4},{6,7},{7,6},{8,9},{9,8},{10,11... | collective-permute-start | bytes 393224 | tf_op jit(solution)/shard_map/ppermute | solution.py:476
  3.7 4.7 %copy-start = (bf16[2048,1024]{1,0:T(8,128)(2,1)S(1)}, bf16[2048,1024]{1,0:T(8,128)(2,1)}, u32[]{:S(2)}) copy-start(bf16[2048,1024]{1,0:T(8,128)(2,1)} %amplitudes.7) | copy-start | bytes 12582916
  11.2 1.4 %collective-permute-start.1 = (f32[16,2,8,128]{3,2,1,0:T(8,128)S(1)}, f32[16,2,8,128]{3,2,1,0:T(8,128)S(1)}, u32[]{:S(2)}, u32[]{:S(2)}) collective-permute-start(f32[16,2,8,128]{3,2,1,0:T(8,128)S(1)} %get-tuple-element.36), channel_id=1, source_target_pairs={{0,2},{2,0},{1,3},{3,1},{4,6},{6,4},{5,7},{7,5},{8,10},{10,8},{9,1... | collective-permute-start | bytes 393224 | tf_op jit(solution)/shard_map/ppermute | solution.py:513
  37.0 1.3 %collective-permute-start.2 = (f32[16,2,8,128]{3,2,1,0:T(8,128)S(1)}, f32[16,2,8,128]{3,2,1,0:T(8,128)S(1)}, u32[]{:S(2)}, u32[]{:S(2)}) collective-permute-start(f32[16,2,8,128]{3,2,1,0:T(8,128)S(1)} %all_to_all.21.own), channel_id=1, source_target_pairs={{0,2},{2,0},{1,3},{3,1},{4,6},{6,4},{5,7},{7,5},{8,10},{10,8},{9,1... | collective-permute-start | bytes 393224 | tf_op jit(solution)/shard_map/ppermute | solution.py:529
  39.9 1.4 %collective-permute-start.3 = (f32[16,4,512]{2,1,0:T(4,128)S(1)}, f32[16,4,512]{2,1,0:T(4,128)S(1)}, u32[]{:S(2)}, u32[]{:S(2)}) collective-permute-start(f32[16,4,512]{2,1,0:T(4,128)S(1)} %get-tuple-element.48), channel_id=1, source_target_pairs={{0,2},{2,0},{1,3},{3,1},{4,6},{6,4},{5,7},{7,5},{8,10},{10,8},{9,1... | collective-permute-start | bytes 393224 | tf_op jit(solution)/shard_map/ppermute | solution.py:554

commit v7 on v6

--- a/solution.py
+++ b/solution.py
@@ -72,14 +72,12 @@
     virt_hbm,
     dipole_hbm,
     coupling_hbm,
-    slab_hbm,
     picked,
     chosen,
     level,
     denom,
     high,
     low,
-    slab_t,
     index,
     energy,
     frequency,
@@ -88,10 +86,8 @@
     virt,
     dipole,
     coupling,
-    slab,
     small_sems,
     coupling_sems,
-    slab_sems,
 ):
     freqs = frequency.shape[0]
     modes, columns = level.shape
@@ -114,13 +110,7 @@
         pltpu.make_async_copy(coupling_hbm.at[s, r], coupling.at[s, r], coupling_sems.at[i])
         for i, (s, r) in enumerate(parts)
     ]
-    step = slab.shape[0] // PARTS
-    pieces = [slice(i * step, (i + 1) * step) for i in range(PARTS)]
-    slabs = [
-        pltpu.make_async_copy(slab_hbm.at[r], slab.at[r], slab_sems.at[i])
-        for i, r in enumerate(pieces)
-    ]
-    waiting = coupled + slabs
+    waiting = list(coupled)
 
     def advance(count):
         for copy in waiting[:count]:
@@ -156,11 +146,6 @@
         upper, lower = halves(coupling[s, r])
         high[s, r] = upper
         low[s, r] = lower
-    for r, copy in zip(pieces, slabs):
-        copy.wait()
-        advance(1)
-        slab_t[:, r] = slab[r].T
-
 
 def fold(response, slab_t, high, low, dims):
     upper, lower = halves(response)
@@ -199,8 +184,33 @@
             out[piece, 1] = total[modes + group * SUB : modes + (group + 1) * SUB, lanes]
 
 
+def starting(rhs, level):
+    inverse = 1.0 / (level * level + DAMP * DAMP)
+    return jnp.concatenate([rhs * level * inverse, rhs * DAMP * inverse], 0)
+
+
+def first_own_body(own, level, high, low, slab, rhs, start, singles, doubles, slab_t):
+    modes, block = rhs.shape
+    freqs = modes // own.shape[0]
+    here = pl.ds(pl.multiple_of(lax.axis_index("narrow") * block, LANE), block)
+    for c in range(own.shape[0]):
+        rhs[c * freqs : (c + 1) * freqs] = jnp.broadcast_to(own[c : c + 1], (freqs, block))
+    start[...] = starting(rhs[...], level[:, here])
+    slots = range(high.shape[0])
+    slab_t[...] = slab[...].T
+    single, inner = fold(
+        start[...],
+        slab_t[here],
+        [high[s, :, here] for s in slots],
+        [low[s, :, here] for s in slots],
+        LAST,
+    )
+    singles[...] = single
+    for s, value in enumerate(inner):
+        doubles[s] = value
+
+
 def first_body(
-    own,
     other,
     chosen,
     level,
@@ -208,6 +218,10 @@
     high,
     low,
     slab_t,
+    rhs_part,
+    start_part,
+    single_part,
+    double_part,
     amplitudes,
     rhs,
     start,
@@ -216,28 +230,30 @@
     give,
 ):
     modes, virt = level.shape
-    cores, block = own.shape
+    cores, block = chosen.shape[0], other.shape[1]
     freqs = modes // cores
     side = lax.axis_index("narrow")
     here = pl.ds(pl.multiple_of(side * block, LANE), block)
     there = pl.ds(pl.multiple_of((1 - side) * block, LANE), block)
+    rhs[:, here] = rhs_part[...]
+    start[:, here] = start_part[...]
     for c in range(cores):
-        span = slice(c * freqs, (c + 1) * freqs)
         mask = jnp.concatenate([chosen[c]] * (block // LANE), 1)
         theirs = jnp.sum(jnp.where(mask > 0.5, other[...], 0.0), axis=0, keepdims=True)
-        rhs[span, here] = jnp.broadcast_to(own[c : c + 1], (freqs, block))
-        rhs[span, there] = jnp.broadcast_to(theirs, (freqs, block))
-    lev = level[...]
-    inverse = 1.0 / (lev * lev + DAMP * DAMP)
-    start[:modes] = rhs[...] * lev * inverse
-    start[modes:] = rhs[...] * DAMP * inverse
+        rhs[c * freqs : (c + 1) * freqs, there] = jnp.broadcast_to(theirs, (freqs, block))
+    rest = starting(rhs[:, there], level[:, there])
+    start[:, there] = rest
     slots = range(high.shape[0])
     single, inner = fold(
-        start[...], slab_t[...], [high[s] for s in slots], [low[s] for s in slots], LAST
-    )
-    singles[...] = stacked(single)
+        rest,
+        slab_t[there],
+        [high[s, :, there] for s in slots],
+        [low[s, :, there] for s in slots],
+        LAST,
+    )
+    singles[...] = stacked(single_part[...] + single)
     for s, value in enumerate(inner):
-        doubles[s] = stacked(quotient(value, denom[s]))
+        doubles[s] = stacked(quotient(double_part[s] + value, denom[s]))
     columns = pl.ds(pl.multiple_of((1 - lax.axis_index("core")) * (virt // 2), LANE), virt // 2)
     write_tiles(give, unfold(singles, doubles, amplitudes, high, low, columns), modes)
 
@@ -475,35 +491,43 @@
 
     across = lax.ppermute(dipole, "narrow", flip_core)
     scalars = (core_index, core_energy, frequency, pair_of_block, pair_shift)
-    picked, chosen, level, denom, high, low, slab_t = call(
+    picked, chosen, level, denom, high, low = call(
         prepare_body,
         "prepare",
-        scalars + (virt_energy[None], dipole, coupling, integral_slab),
-        [HBM] * 9,
+        scalars + (virt_energy[None], dipole, coupling),
+        [HBM] * 8,
         [((cores, block), F32), ((cores, dipole.shape[0], LANE), F32)]
         + [((modes, virt), F32), ((slots, modes, virt), F32)]
-        + [((slots, virt, virt), BF16)] * 2
-        + [((virt, rows), BF16)],
+        + [((slots, virt, virt), BF16)] * 2,
         scratch=[pltpu.SMEM(a.shape, a.dtype) for a in scalars]
         + [
             pltpu.VMEM((1, virt), F32),
             pltpu.VMEM(dipole.shape, F32),
             pltpu.VMEM(coupling.shape, F32),
-            pltpu.VMEM(integral_slab.shape, BF16),
             pltpu.SemaphoreType.DMA((7,)),
             pltpu.SemaphoreType.DMA((PARTS * slots,)),
-            pltpu.SemaphoreType.DMA((PARTS,)),
         ],
         flops=4 * slots * virt * virt,
         moved=2 * size,
     )
     piece = (members, 2, SUB, LANE)
     between = [((4 * modes, rows), BF16), ((slots, 4 * modes, virt), BF16)]
+    *parts, slab_t = call(
+        first_own_body,
+        "first_own",
+        (picked, level, high, low, integral_slab),
+        [VMEM] * 5,
+        [((modes, block), F32), ((2 * modes, block), F32)]
+        + [((2 * modes, rows), F32), ((slots, 2 * modes, virt), F32)]
+        + [((virt, rows), BF16)],
+        flops=work // 4,
+        moved=size // 2,
+    )
     rhs, start, singles, doubles, give = call(
         first_body,
         "first",
-        (picked, across, chosen, level, denom, high, low, slab_t, amplitudes),
-        [VMEM] * 9,
+        (across, chosen, level, denom, high, low, slab_t, *parts, amplitudes),
+        [VMEM] * 12,
         [((modes, virt), F32), ((2 * modes, virt), F32)]
         + between
         + [(piece, F32)],

time: 63.9 us -> 63.4 us (level)
    pallas_call x11 -> x12, Pallas kernels: 12.5 us -> 11.9 us  [call(): pl.pallas_call(body, out_shape=[jax.ShapeDtypeStruct(s, d) for s, d in ou...]
  transfers between devices with their start and end apart: 4 -> 4, of which waited for: 3 -> 3; matrix products, arithmetic and copies ran while one was open for 0% -> 0% of each run, Pallas kernels for 11% -> 12%
where the time goes in v7:
time: 63.4 us; the launch traced here: 63.1 us
  blocking collectives  45.9 us (72%)
  Pallas kernels  11.9 us (19%)
  starting transfers between devices  3.4 us (5%)
  waiting for transfers between devices  1.11 us (2%)
  between operations  0.76 us (1%)
    all_to_all x2, blocking collectives, fast_path(): got = lax.all_to_all(total, group, 0, 0, tiled=True)  24.5 us
    pallas_call x12, Pallas kernels, call(): pl.pallas_call(body, out_shape=[jax.ShapeDtypeStruct(s, d) for s, d in ou...  11.9 us
    all_to_all x1, blocking collectives, fast_path(): got = lax.all_to_all(sent, ('chip', 'core', 'narrow'), 0, 0, tiled=True)  10.8 us
    all_to_all x1, blocking collectives, fast_path(): got = lax.all_to_all(sent, group, 0, 0, tiled=True)  10.7 us
    ppermute x1, starting transfers between devices, fast_path(): across = lax.ppermute(dipole, 'narrow', flip_core)  3.03 us
  transfers between devices with their start and end apart: 4, of which 3 were waited for; matrix products, arithmetic and copies ran while one was open for 0% of the time, Pallas kernels for 12%

profile of v7, /device:TPU:0, one launch (start us, length us, event | category | flops | bytes accessed | tf_op | source)
XLA Modules:
  0.0 63.1 jit_solution(2515223489295665292)
XLA Ops:
  0.6 0.0 copy-start.1
  0.6 3.0 %collective-permute-start = (f32[64,512]{1,0:T(8,128)}, f32[64,512]{1,0:T(8,128)S(1)}, u32[]{:S(2)}, u32[]{:S(2)}) collective-permute-start(f32[64,512]{1,0:T(8,128)} %dipole_hbm.1), channel_id=1, source_target_pairs={{0,1},{1,0},{2,3},{3,2},{4,5},{5,4},{6,7},{7,6},{8,9},{9,8},{10,11... | collective-permute-start | bytes 393224 | tf_op jit(solution)/shard_map/ppermute | solution.py:492
  3.7 2.6 %prepare.1 = (f32[2,512]{1,0:T(2,128)S(1)}, f32[2,64,128]{2,1,0:T(8,128)S(1)}, f32[32,1024]{1,0:T(8,128)S(1)}, f32[1,32,1024]{2,1,0:T(8,128)S(1)}, bf16[1,1024,1...) custom-call(s32[2]{0:T(128)} %index_hbm.1, f32[64]{0:T(128)} %energy_hbm.1, f32[16]{0:T(128)} %frequency_hbm.1, ...), custom_call_target="tpu_custom_call" | custom-call | flops 4194304 | bytes 16777216 | tf_op jit(solution)/shard_map/prepare/pallas_call | solution.py:47
  6.3 0.0 copy-done.1
  6.3 0.0 copy-start
  6.3 2.4 %first_own.1 = (f32[32,512]{1,0:T(8,128)S(1)}, f32[64,512]{1,0:T(8,128)S(1)}, f32[64,2048]{1,0:T(8,128)S(1)}, f32[1,64,1024]{2,1,0:T(8,128)S(1)}, bf16[1024,2048]{1,0:T(8,128)(2,1)S(1)}) custom-call(f32[2,512]{1,0:T(2,128)S(1)} %get-tuple-element.35.own, f32[32,1024]{1,0:T(8,128)S(1)} %get-tuple-element.31.level, ...), custom_call_target="tpu_custom_call" | custom-call | flops 201326592 | bytes 4194304 | tf_op jit(solution)/shard_map/first_own/pallas_call | solution.py:47
  8.7 0.0 collective-permute-done.other
  8.7 0.0 copy-done
  8.7 1.8 %first.1 = (f32[32,1024]{1,0:T(8,128)S(1)}, f32[64,1024]{1,0:T(8,128)S(1)}, bf16[128,2048]{1,0:T(8,128)(2,1)S(1)}, bf16[1,128,1024]{2,1,0:T(8,128)(2,1)S(1)}, f32[16,2,8,128]{3,2,1,0:T(8,128)S(1)}) custom-call(f32[64,512]{1,0:T(8,128)S(1)} %collective-permute-done.other, f32[2,64,128]{2,1,0:T(8,128)S(1)} %get-tuple-element.30.chosen, ...), custom_call_target="tpu_custom_call" | custom-call | flops 603979776 | bytes 16777216 | tf_op jit(solution)/shard_map/first/pallas_call | solution.py:47
  10.5 0.1 collective-permute-start.1
  10.6 0.8 %first_rest.1 = (f32[16,2,8,128]{3,2,1,0:T(8,128)S(1)}, bf16[1,512,1024]{2,1,0:T(8,128)(2,1)S(1)}, bf16[1,512,1024]{2,1,0:T(8,128)(2,1)S(1)}) custom-call(bf16[128,2048]{1,0:T(8,128)(2,1)S(1)} %get-tuple-element.41.singles, bf16[1,128,1024]{2,1,0:T(8,128)(2,1)S(1)} %get-tuple-element.42.doubles, bf16[2048,1024]{1,0:T(8,128)(2,1)S(1)} %copy-done, ...), custom_call_target="tpu_custom_call" | custom-call | flops 201326592 | bytes 4194304 | tf_op jit(solution)/shard_map/first_rest/pallas_call | solution.py:47
  11.4 0.5 collective-permute-done.1.right
  12.0 13.8 %all_to_all.20.got = f32[16,2,8,128]{3,2,1,0:T(8,128)S(1)} all-to-all(f32[16,2,8,128]{3,2,1,0:T(8,128)S(1)} %add_first.1), channel_id=1, replica_groups=mesh['chip'=8,'core'=2,'narrow'=2] {'chip','narrow'}, dimensions={0} | all-to-all | bytes 262144 | tf_op jit(solution)/shard_map/all_to_all | solution.py:548
  25.8 10.7 %all_to_all.21.own = f32[16,2,8,128]{3,2,1,0:T(8,128)S(1)} all-to-all(f32[16,2,8,128]{3,2,1,0:T(8,128)S(1)} %first_update.1), channel_id=1, replica_groups=mesh['chip'=8,'core'=2,'narrow'=2] {'chip','narrow'}, dimensions={0} | all-to-all | bytes 262144 | tf_op jit(solution)/shard_map/all_to_all | solution.py:552
  36.5 0.0 collective-permute-start.2
  36.5 1.1 %second_own.1 = (f32[64,512]{1,0:T(8,128)S(1)}, f32[64,2048]{1,0:T(8,128)S(1)}, f32[1,64,1024]{2,1,0:T(8,128)S(1)}) custom-call(f32[16,2,8,128]{3,2,1,0:T(8,128)S(1)} %all_to_all.21.own, bf16[1024,2048]{1,0:T(8,128)(2,1)S(1)} %get-tuple-element.36.slab_t, bf16[1,1024,1024]{2,1,0:T(8,128)(2,1)S(1)} %get-tuple-element.33.high, ...), custom_call_target="tpu_custom_call" | custom-call | flops 201326592 | bytes 4194304 | tf_op jit(solution)/shard_map/second_own/pallas_call | solution.py:47
  37.6 0.3 collective-permute-done.2.other
  37.9 1.5 %second.1 = (f32[64,1024]{1,0:T(8,128)S(1)}, bf16[128,2048]{1,0:T(8,128)(2,1)S(1)}, bf16[1,128,1024]{2,1,0:T(8,128)(2,1)S(1)}, f32[16,4,512]{2,1,0:T(4,128)S(1)}) custom-call(f32[64,512]{1,0:T(8,128)S(1)} %get-tuple-element.47.mine, f32[16,2,8,128]{3,2,1,0:T(8,128)S(1)} %collective-permute-done.2.other, f32[64,2048]{1,0:T(8,128)S(1)} %get-tuple-element.48.single_part, ...), custom_call_target="tpu_custom_call" | custom-call | flops 402653184 | bytes 8388608 | tf_op jit(solution)/shard_map/second/pallas_call | solution.py:47
  39.3 0.3 collective-permute-start.3
  39.6 0.8 %second_rest.1 = (f32[16,4,512]{2,1,0:T(4,128)S(1)}, f32[32,1]{1,0:T(8,128)S(1)}) custom-call(bf16[128,2048]{1,0:T(8,128)(2,1)S(1)} %get-tuple-element.52.singles, bf16[1,128,1024]{2,1,0:T(8,128)(2,1)S(1)} %get-tuple-element.53.doubles, bf16[2048,1024]{1,0:T(8,128)(2,1)S(1)} %copy-done, bf16[1,1024,1024]{2,1,0:T(8,128)(2,1)S(1)} %get-tuple-element.33.high, ...), custom_call_target="tpu_custom_call" | custom-call | flops 201326592 | bytes 4194304 | tf_op jit(solution)/shard_map/second_rest/pallas_call | solution.py:47
  40.5 0.3 collective-permute-done.3.right
  40.8 10.7 %all_to_all.22.got = f32[16,4,512]{2,1,0:T(4,128)S(1)} all-to-all(f32[16,4,512]{2,1,0:T(4,128)S(1)} %add_second.1), channel_id=1, replica_groups=mesh['chip'=8,'core'=2,'narrow'=2] {'chip','narrow'}, dimensions={0} | all-to-all | bytes 262144 | tf_op jit(solution)/shard_map/all_to_all | solution.py:589
  51.5 0.1 second_update.1
  51.6 10.8 %all_to_all.23.got = f32[32,1,1152]{2,1,0:T(1,128)S(1)} all-to-all(f32[32,1,1152]{2,1,0:T(1,128)S(1)} %second_update.1), channel_id=1, replica_groups=mesh['chip'=8,'core'=2,'narrow'=2] {'chip','core','narrow'}, dimensions={0} | all-to-all | bytes 294912 | tf_op jit(solution)/shard_map/all_to_all | solution.py:598
  62.4 0.8 %finish.1 = (f32[2,32,512]{2,1,0:T(8,128)}, f32[2,32]{1,0:T(2,128)}) custom-call(f32[32,1,1152]{2,1,0:T(1,128)S(1)} %all_to_all.23.got, f32[32,1]{1,0:T(8,128)S(1)} %get-tuple-element.57.old), custom_call_target="tpu_custom_call" | custom-call | tf_op jit(solution)/shard_map/finish/pallas_call | solution.py:47
  (3 shorter events, 0.1 us)
Async XLA Ops:
  0.6 5.6 %copy-start.1 = (bf16[2048,1024]{1,0:T(8,128)(2,1)S(1)}, bf16[2048,1024]{1,0:T(8,128)(2,1)}, u32[]{:S(2)}) copy-start(bf16[2048,1024]{1,0:T(8,128)(2,1)} %slab.1) | copy-start | bytes 12582916
  0.6 8.1 %collective-permute-start = (f32[64,512]{1,0:T(8,128)}, f32[64,512]{1,0:T(8,128)S(1)}, u32[]{:S(2)}, u32[]{:S(2)}) collective-permute-start(f32[64,512]{1,0:T(8,128)} %dipole_hbm.1), channel_id=1, source_target_pairs={{0,1},{1,0},{2,3},{3,2},{4,5},{5,4},{6,7},{7,6},{8,9},{9,8},{10,11... | collective-permute-start | bytes 393224 | tf_op jit(solution)/shard_map/ppermute | solution.py:492
  6.3 2.4 %copy-start = (bf16[2048,1024]{1,0:T(8,128)(2,1)S(1)}, bf16[2048,1024]{1,0:T(8,128)(2,1)}, u32[]{:S(2)}) copy-start(bf16[2048,1024]{1,0:T(8,128)(2,1)} %amplitudes.7) | copy-start | bytes 12582916
  10.5 1.4 %collective-permute-start.1 = (f32[16,2,8,128]{3,2,1,0:T(8,128)S(1)}, f32[16,2,8,128]{3,2,1,0:T(8,128)S(1)}, u32[]{:S(2)}, u32[]{:S(2)}) collective-permute-start(f32[16,2,8,128]{3,2,1,0:T(8,128)S(1)} %get-tuple-element.44), channel_id=1, source_target_pairs={{0,2},{2,0},{1,3},{3,1},{4,6},{6,4},{5,7},{7,5},{8,10},{10,8},{9,1... | collective-permute-start | bytes 393224 | tf_op jit(solution)/shard_map/ppermute | solution.py:537
  36.5 1.3 %collective-permute-start.2 = (f32[16,2,8,128]{3,2,1,0:T(8,128)S(1)}, f32[16,2,8,128]{3,2,1,0:T(8,128)S(1)}, u32[]{:S(2)}, u32[]{:S(2)}) collective-permute-start(f32[16,2,8,128]{3,2,1,0:T(8,128)S(1)} %all_to_all.21.own), channel_id=1, source_target_pairs={{0,2},{2,0},{1,3},{3,1},{4,6},{6,4},{5,7},{7,5},{8,10},{10,8},{9,1... | collective-permute-start | bytes 393224 | tf_op jit(solution)/shard_map/ppermute | solution.py:553
  39.3 1.4 %collective-permute-start.3 = (f32[16,4,512]{2,1,0:T(4,128)S(1)}, f32[16,4,512]{2,1,0:T(4,128)S(1)}, u32[]{:S(2)}, u32[]{:S(2)}) collective-permute-start(f32[16,4,512]{2,1,0:T(4,128)S(1)} %get-tuple-element.56), channel_id=1, source_target_pairs={{0,2},{2,0},{1,3},{3,1},{4,6},{6,4},{5,7},{7,5},{8,10},{10,8},{9,1... | collective-permute-start | bytes 393224 | tf_op jit(solution)/shard_map/ppermute | solution.py:578

commit v8 on v7

--- a/solution.py
+++ b/solution.py
@@ -39,7 +39,7 @@
     return value[:rows] + value[rows:]
 
 
-def call(body, name, operands, in_specs, outs, scratch=(), flops=0, moved=0):
+def call(body, name, operands, in_specs, outs, scratch=(), flops=0, moved=0, aliases={}):
     operands = [
         pltpu.with_memory_space_constraint(x, pltpu.HBM) if spec is HBM else x
         for x, spec in zip(operands, in_specs)
@@ -51,6 +51,7 @@
         out_specs=[VMEM] * len(outs),
         scratch_shapes=scratch,
         name=name,
+        input_output_aliases=aliases,
         compiler_params=pltpu.CompilerParams(vmem_limit_bytes=20 << 20),
         cost_estimate=pl.CostEstimate(flops=flops, bytes_accessed=moved, transcendentals=0),
     )(*operands)
@@ -197,7 +198,7 @@
         rhs[c * freqs : (c + 1) * freqs] = jnp.broadcast_to(own[c : c + 1], (freqs, block))
     start[...] = starting(rhs[...], level[:, here])
     slots = range(high.shape[0])
-    slab_t[...] = slab[...].T
+    slab_t[here] = slab[:, here].T
     single, inner = fold(
         start[...],
         slab_t[here],
@@ -217,7 +218,8 @@
     denom,
     high,
     low,
-    slab_t,
+    _,
+    slab,
     rhs_part,
     start_part,
     single_part,
@@ -228,6 +230,7 @@
     singles,
     doubles,
     give,
+    slab_t,
 ):
     modes, virt = level.shape
     cores, block = chosen.shape[0], other.shape[1]
@@ -243,6 +246,7 @@
         rhs[c * freqs : (c + 1) * freqs, there] = jnp.broadcast_to(theirs, (freqs, block))
     rest = starting(rhs[:, there], level[:, there])
     start[:, there] = rest
+    slab_t[there] = slab[:, there].T
     slots = range(high.shape[0])
     single, inner = fold(
         rest,
@@ -523,14 +527,15 @@
         flops=work // 4,
         moved=size // 2,
     )
-    rhs, start, singles, doubles, give = call(
+    rhs, start, singles, doubles, give, slab_t = call(
         first_body,
         "first",
-        (across, chosen, level, denom, high, low, slab_t, *parts, amplitudes),
-        [VMEM] * 12,
+        (across, chosen, level, denom, high, low, slab_t, integral_slab, *parts, amplitudes),
+        [VMEM] * 13,
         [((modes, virt), F32), ((2 * modes, virt), F32)]
         + between
-        + [(piece, F32)],
+        + [(piece, F32), ((virt, rows), BF16)],
+        aliases={6: 5},
         flops=work * 3 // 4,
         moved=2 * size,
     )

time: 63.4 us -> 63.4 us (level)
  Pallas kernels: 11.9 us -> 11.1 us
  local copies, waits for them, and re-layouts: 0.01 us -> 0.79 us
    pallas_call x12, Pallas kernels: 11.9 us -> 11.1 us  [call(): pl.pallas_call(body, out_shape=[jax.ShapeDtypeStruct(s, d) for s, d in ou...]
    unnamed x4, local copies, waits for them, and re-layouts: 0.01 us -> 0.79 us
  transfers between devices with their start and end apart: 4 -> 4, of which waited for: 3 -> 3; matrix products, arithmetic and copies ran while one was open for 0% -> 0% of each run, Pallas kernels for 12% -> 11%
where the time goes in v8:
time: 63.4 us; the launch traced here: 63.1 us
  blocking collectives  46 us (73%)
  Pallas kernels  11.1 us (18%)
  starting transfers between devices  3.41 us (5%)
  waiting for transfers between devices  1.1 us (2%)
  local copies, waits for them, and re-layouts  0.79 us (1%)
  between operations  0.74 us (1%)
    all_to_all x2, blocking collectives, fast_path(): got = lax.all_to_all(total, group, 0, 0, tiled=True)  24.5 us
    pallas_call x12, Pallas kernels, call(): pl.pallas_call(body, out_shape=[jax.ShapeDtypeStruct(s, d) for s, d in ou...  11.1 us
    all_to_all x1, blocking collectives, fast_path(): got = lax.all_to_all(sent, ('chip', 'core', 'narrow'), 0, 0, tiled=True)  10.7 us
    all_to_all x1, blocking collectives, fast_path(): got = lax.all_to_all(sent, group, 0, 0, tiled=True)  10.7 us
    ppermute x1, starting transfers between devices, fast_path(): across = lax.ppermute(dipole, 'narrow', flip_core)  3.03 us
  transfers between devices with their start and end apart: 4, of which 3 were waited for; matrix products, arithmetic and copies ran while one was open for 0% of the time, Pallas kernels for 11%

profile of v8, /device:TPU:0, one launch (start us, length us, event | category | flops | bytes accessed | tf_op | source)
XLA Modules:
  0.0 63.1 jit_solution(13331711925792959370)
XLA Ops:
  0.6 0.0 copy-start.1
  0.6 3.0 %collective-permute-start = (f32[64,512]{1,0:T(8,128)}, f32[64,512]{1,0:T(8,128)S(1)}, u32[]{:S(2)}, u32[]{:S(2)}) collective-permute-start(f32[64,512]{1,0:T(8,128)} %dipole_hbm.1), channel_id=1, source_target_pairs={{0,1},{1,0},{2,3},{3,2},{4,5},{5,4},{6,7},{7,6},{8,9},{9,8},{10,11... | collective-permute-start | bytes 393224 | tf_op jit(solution)/shard_map/ppermute | solution.py:496
  3.7 2.6 %prepare.1 = (f32[2,512]{1,0:T(2,128)S(1)}, f32[2,64,128]{2,1,0:T(8,128)S(1)}, f32[32,1024]{1,0:T(8,128)S(1)}, f32[1,32,1024]{2,1,0:T(8,128)S(1)}, bf16[1,1024,1...) custom-call(s32[2]{0:T(128)} %index_hbm.1, f32[64]{0:T(128)} %energy_hbm.1, f32[16]{0:T(128)} %frequency_hbm.1, ...), custom_call_target="tpu_custom_call" | custom-call | flops 4194304 | bytes 16777216 | tf_op jit(solution)/shard_map/prepare/pallas_call | solution.py:47
  6.3 0.0 copy-done.1
  6.3 0.0 copy-start
  6.3 1.4 %first_own.1 = (f32[32,512]{1,0:T(8,128)S(1)}, f32[64,512]{1,0:T(8,128)S(1)}, f32[64,2048]{1,0:T(8,128)S(1)}, f32[1,64,1024]{2,1,0:T(8,128)S(1)}, bf16[1024,2048]{1,0:T(8,128)(2,1)S(1)}) custom-call(f32[2,512]{1,0:T(2,128)S(1)} %get-tuple-element.36.own, f32[32,1024]{1,0:T(8,128)S(1)} %get-tuple-element.32.level, ...), custom_call_target="tpu_custom_call" | custom-call | flops 201326592 | bytes 4194304 | tf_op jit(solution)/shard_map/first_own/pallas_call | solution.py:47
  7.7 0.0 collective-permute-done.other
  7.7 0.8 %copy-done = bf16[2048,1024]{1,0:T(8,128)(2,1)S(1)} copy-done((bf16[2048,1024]{1,0:T(8,128)(2,1)S(1)}, bf16[2048,1024]{1,0:T(8,128)(2,1)}, u32[]{:S(2)}) %copy-start) | copy-done | bytes 4194328
  8.5 2.0 %first.1 = (f32[32,1024]{1,0:T(8,128)S(1)}, f32[64,1024]{1,0:T(8,128)S(1)}, bf16[128,2048]{1,0:T(8,128)(2,1)S(1)}, bf16[1,128,1024]{2,1,0:T(8,128)(2,1)S(1)}, f3...) custom-call(f32[64,512]{1,0:T(8,128)S(1)} %collective-permute-done.other, ...), custom_call_target="tpu_custom_call", output_to_operand_aliasing={{5}: (6, {})} | custom-call | flops 603979776 | bytes 16777216 | tf_op jit(solution)/shard_map/first/pallas_call | solution.py:47
  10.5 0.1 collective-permute-start.1
  10.6 0.8 %first_rest.1 = (f32[16,2,8,128]{3,2,1,0:T(8,128)S(1)}, bf16[1,512,1024]{2,1,0:T(8,128)(2,1)S(1)}, bf16[1,512,1024]{2,1,0:T(8,128)(2,1)S(1)}) custom-call(bf16[128,2048]{1,0:T(8,128)(2,1)S(1)} %get-tuple-element.42.singles, bf16[1,128,1024]{2,1,0:T(8,128)(2,1)S(1)} %get-tuple-element.43.doubles, bf16[2048,1024]{1,0:T(8,128)(2,1)S(1)} %copy-done, ...), custom_call_target="tpu_custom_call" | custom-call | flops 201326592 | bytes 4194304 | tf_op jit(solution)/shard_map/first_rest/pallas_call | solution.py:47
  11.3 0.5 collective-permute-done.1.right
  11.9 13.8 %all_to_all.20.got = f32[16,2,8,128]{3,2,1,0:T(8,128)S(1)} all-to-all(f32[16,2,8,128]{3,2,1,0:T(8,128)S(1)} %add_first.1), channel_id=1, replica_groups=mesh['chip'=8,'core'=2,'narrow'=2] {'chip','narrow'}, dimensions={0} | all-to-all | bytes 262144 | tf_op jit(solution)/shard_map/all_to_all | solution.py:553
  25.7 10.7 %all_to_all.21.own = f32[16,2,8,128]{3,2,1,0:T(8,128)S(1)} all-to-all(f32[16,2,8,128]{3,2,1,0:T(8,128)S(1)} %first_update.1), channel_id=1, replica_groups=mesh['chip'=8,'core'=2,'narrow'=2] {'chip','narrow'}, dimensions={0} | all-to-all | bytes 262144 | tf_op jit(solution)/shard_map/all_to_all | solution.py:557
  36.4 0.0 collective-permute-start.2
  36.5 1.1 %second_own.1 = (f32[64,512]{1,0:T(8,128)S(1)}, f32[64,2048]{1,0:T(8,128)S(1)}, f32[1,64,1024]{2,1,0:T(8,128)S(1)}) custom-call(f32[16,2,8,128]{3,2,1,0:T(8,128)S(1)} %all_to_all.21.own, bf16[1024,2048]{1,0:T(8,128)(2,1)S(1)} %get-tuple-element.48.slab_t, bf16[1,1024,1024]{2,1,0:T(8,128)(2,1)S(1)} %get-tuple-element.34.high, ...), custom_call_target="tpu_custom_call" | custom-call | flops 201326592 | bytes 4194304 | tf_op jit(solution)/shard_map/second_own/pallas_call | solution.py:47
  37.5 0.3 collective-permute-done.2.other
  37.8 1.5 %second.1 = (f32[64,1024]{1,0:T(8,128)S(1)}, bf16[128,2048]{1,0:T(8,128)(2,1)S(1)}, bf16[1,128,1024]{2,1,0:T(8,128)(2,1)S(1)}, f32[16,4,512]{2,1,0:T(4,128)S(1)}) custom-call(f32[64,512]{1,0:T(8,128)S(1)} %get-tuple-element.49.mine, f32[16,2,8,128]{3,2,1,0:T(8,128)S(1)} %collective-permute-done.2.other, f32[64,2048]{1,0:T(8,128)S(1)} %get-tuple-element.50.single_part, ...), custom_call_target="tpu_custom_call" | custom-call | flops 402653184 | bytes 8388608 | tf_op jit(solution)/shard_map/second/pallas_call | solution.py:47
  39.3 0.3 collective-permute-start.3
  39.6 0.8 %second_rest.1 = (f32[16,4,512]{2,1,0:T(4,128)S(1)}, f32[32,1]{1,0:T(8,128)S(1)}) custom-call(bf16[128,2048]{1,0:T(8,128)(2,1)S(1)} %get-tuple-element.54.singles, bf16[1,128,1024]{2,1,0:T(8,128)(2,1)S(1)} %get-tuple-element.55.doubles, bf16[2048,1024]{1,0:T(8,128)(2,1)S(1)} %copy-done, bf16[1,1024,1024]{2,1,0:T(8,128)(2,1)S(1)} %get-tuple-element.34.high, ...), custom_call_target="tpu_custom_call" | custom-call | flops 201326592 | bytes 4194304 | tf_op jit(solution)/shard_map/second_rest/pallas_call | solution.py:47
  40.4 0.3 collective-permute-done.3.right
  40.7 10.7 %all_to_all.22.got = f32[16,4,512]{2,1,0:T(4,128)S(1)} all-to-all(f32[16,4,512]{2,1,0:T(4,128)S(1)} %add_second.1), channel_id=1, replica_groups=mesh['chip'=8,'core'=2,'narrow'=2] {'chip','narrow'}, dimensions={0} | all-to-all | bytes 262144 | tf_op jit(solution)/shard_map/all_to_all | solution.py:594
  51.4 0.1 second_update.1
  51.6 10.7 %all_to_all.23.got = f32[32,1,1152]{2,1,0:T(1,128)S(1)} all-to-all(f32[32,1,1152]{2,1,0:T(1,128)S(1)} %second_update.1), channel_id=1, replica_groups=mesh['chip'=8,'core'=2,'narrow'=2] {'chip','core','narrow'}, dimensions={0} | all-to-all | bytes 294912 | tf_op jit(solution)/shard_map/all_to_all | solution.py:603
  62.3 0.8 %finish.1 = (f32[2,32,512]{2,1,0:T(8,128)}, f32[2,32]{1,0:T(2,128)}) custom-call(f32[32,1,1152]{2,1,0:T(1,128)S(1)} %all_to_all.23.got, f32[32,1]{1,0:T(8,128)S(1)} %get-tuple-element.59.old), custom_call_target="tpu_custom_call" | custom-call | tf_op jit(solution)/shard_map/finish/pallas_call | solution.py:47
  (3 shorter events, 0.1 us)
Async XLA Ops:
  0.6 5.6 %copy-start.1 = (bf16[2048,1024]{1,0:T(8,128)(2,1)S(1)}, bf16[2048,1024]{1,0:T(8,128)(2,1)}, u32[]{:S(2)}) copy-start(bf16[2048,1024]{1,0:T(8,128)(2,1)} %slab.3) | copy-start | bytes 12582916
  0.6 7.0 %collective-permute-start = (f32[64,512]{1,0:T(8,128)}, f32[64,512]{1,0:T(8,128)S(1)}, u32[]{:S(2)}, u32[]{:S(2)}) collective-permute-start(f32[64,512]{1,0:T(8,128)} %dipole_hbm.1), channel_id=1, source_target_pairs={{0,1},{1,0},{2,3},{3,2},{4,5},{5,4},{6,7},{7,6},{8,9},{9,8},{10,11... | collective-permute-start | bytes 393224 | tf_op jit(solution)/shard_map/ppermute | solution.py:496
  6.3 2.2 %copy-start = (bf16[2048,1024]{1,0:T(8,128)(2,1)S(1)}, bf16[2048,1024]{1,0:T(8,128)(2,1)}, u32[]{:S(2)}) copy-start(bf16[2048,1024]{1,0:T(8,128)(2,1)} %amplitudes.7) | copy-start | bytes 12582916
  10.5 1.4 %collective-permute-start.1 = (f32[16,2,8,128]{3,2,1,0:T(8,128)S(1)}, f32[16,2,8,128]{3,2,1,0:T(8,128)S(1)}, u32[]{:S(2)}, u32[]{:S(2)}) collective-permute-start(f32[16,2,8,128]{3,2,1,0:T(8,128)S(1)} %get-tuple-element.45), channel_id=1, source_target_pairs={{0,2},{2,0},{1,3},{3,1},{4,6},{6,4},{5,7},{7,5},{8,10},{10,8},{9,1... | collective-permute-start | bytes 393224 | tf_op jit(solution)/shard_map/ppermute | solution.py:542
  36.4 1.3 %collective-permute-start.2 = (f32[16,2,8,128]{3,2,1,0:T(8,128)S(1)}, f32[16,2,8,128]{3,2,1,0:T(8,128)S(1)}, u32[]{:S(2)}, u32[]{:S(2)}) collective-permute-start(f32[16,2,8,128]{3,2,1,0:T(8,128)S(1)} %all_to_all.21.own), channel_id=1, source_target_pairs={{0,2},{2,0},{1,3},{3,1},{4,6},{6,4},{5,7},{7,5},{8,10},{10,8},{9,1... | collective-permute-start | bytes 393224 | tf_op jit(solution)/shard_map/ppermute | solution.py:558
  39.3 1.4 %collective-permute-start.3 = (f32[16,4,512]{2,1,0:T(4,128)S(1)}, f32[16,4,512]{2,1,0:T(4,128)S(1)}, u32[]{:S(2)}, u32[]{:S(2)}) collective-permute-start(f32[16,4,512]{2,1,0:T(4,128)S(1)} %get-tuple-element.58), channel_id=1, source_target_pairs={{0,2},{2,0},{1,3},{3,1},{4,6},{6,4},{5,7},{7,5},{8,10},{10,8},{9,1... | collective-permute-start | bytes 393224 | tf_op jit(solution)/shard_map/ppermute | solution.py:583
